TPU v7x, 32 devices: a whole 2x2x4 slice. The times are simulated.
32 devices in a mesh: dp: 4 (over y, core), tensor: 8 (over z, x).
Axes of the slice: x: 2, y: 2, z: 4, core: 2. Of those that a mesh axis runs over, the one named last changes fastest.
Arguments:
- tokens: bfloat16 [8192, 2048], P(('dp', 'tensor')), may hold values from -6 to 6
- gain_one: float32 [2048], replicated, may hold values from 0.5 to 1.5
- w_query: bfloat16 [2048, 256], P(None, 'tensor'), may hold values from -0.125 to 0.125
- w_key: bfloat16 [2048, 256], P(None, 'tensor'), may hold values from -0.125 to 0.125
- w_value: bfloat16 [2048, 2048], P(None, 'tensor'), may hold values from -0.125 to 0.125
- w_out: bfloat16 [2048, 2048], P('tensor'), may hold values from -0.5 to 0.5
- gain_two: float32 [2048], replicated, may hold values from 0.5 to 1.5
- w_gate: bfloat16 [2048, 5632], P(None, 'tensor'), may hold values from -0.125 to 0.125
- w_up: bfloat16 [2048, 5632], P(None, 'tensor'), may hold values from -0.125 to 0.125
- w_down: bfloat16 [5632, 2048], P('tensor'), may hold values from -0.078125 to 0.078125
- doc_ids: int32 [4, 2048], P('dp'), may hold values from 0 to 7, never falling along the last dimension, each value on 1 to 1024 neighbouring positions
- cotangent: bfloat16 [8192, 2048], P(('dp', 'tensor')), may hold values from -6 to 6
Outputs:
- block_out: bfloat16 [8192, 2048], P(('dp', 'tensor'))
- grad_tokens: float32 [8192, 2048], P(('dp', 'tensor'))
- grad_gain_one: float32 [2048], replicated
- grad_query: float32 [2048, 256], P(None, 'tensor')
- grad_key: float32 [2048, 256], P(None, 'tensor')
- grad_value: float32 [2048, 2048], P(None, 'tensor')
- grad_out_proj: float32 [2048, 2048], P('tensor')
- grad_gain_two: float32 [2048], replicated
- grad_gate: float32 [2048, 5632], P(None, 'tensor')
- grad_up: float32 [2048, 5632], P(None, 'tensor')
- grad_down: float32 [5632, 2048], P('tensor')
Inputs may be any that keep to these rules, and one draw needn't show every extreme that they name: Each row of doc_ids never falls along the row; each of the 8 documents of a group has 1 to 1024 tokens, and one has exactly 1024.
All inputs are finite; a program needn't handle non-finite values.
Results may differ from a plain program's by a relative error of at most 0.02.
Values may be sent and summed in bfloat16 or wider, within the bound.
No kernel may reach another device: no remote copies, remote signals or barrier semaphores. Data moves between devices by JAX's collectives and lax.ppermute only.
A program may use at most 256 MiB of HBM per device.

v0:
```python
import jax
import jax.numpy as jnp
from jax import lax
from jax.sharding import PartitionSpec as P

FEAT = 16
HEAD_V = 128


EPS = 1e-05


def norm_rows(values, gain_vec):
    row_scale = lax.rsqrt(jnp.mean(values * values, axis=-1, keepdims=True) + EPS)
    normed = values * row_scale
    return (normed, row_scale, (normed * gain_vec).astype(jnp.bfloat16))


def norm_back(grad_normed, normed, row_scale, gain_vec):
    weighted = grad_normed * gain_vec
    inner_mean = jnp.mean(weighted * normed, axis=-1, keepdims=True)
    return (row_scale * (weighted - normed * inner_mean), jnp.sum(grad_normed * normed, axis=0))


def contract_rows(left_mat, right_mat):
    return lax.dot_general(
        left_mat, right_mat, (((0,), (0,)), ((), ())), preferred_element_type=jnp.float32
    )


def times_transposed(left_mat, right_mat):
    return lax.dot_general(
        left_mat, right_mat, (((1,), (1,)), ((), ())), preferred_element_type=jnp.float32
    )


def block_kernel(query_rows, key_row_block, doc_row, row_start, block_rows):
    row_end_index = row_start + block_rows
    query_portion = query_rows[row_start:row_end_index]
    score_matrix = (
        jnp.einsum(
            "gsn,jsn->sgj",
            query_portion,
            key_row_block[:row_end_index],
            preferred_element_type=jnp.float32,
        )
        * 0.25
    )
    query_index = row_start + jnp.arange(block_rows)
    key_index = jnp.arange(row_end_index)
    allowed = (doc_row[row_start:row_end_index, None] == doc_row[None, :row_end_index]) & (
        query_index[:, None] >= key_index[None, :]
    )
    kernel = jnp.where(allowed[None], 1.0 + score_matrix + 0.5 * score_matrix * score_matrix, 0.0)
    return (score_matrix, allowed, kernel)


def attention_forward(query_rows, key_row_block, value_rows, doc_row, block_rows):
    group_rows = query_rows.shape[0]
    outputs = []
    denoms = []
    for row_start in range(0, group_rows, block_rows):
        row_end_index = row_start + block_rows
        score_matrix, allowed, kernel = block_kernel(
            query_rows, key_row_block, doc_row, row_start, block_rows
        )
        denominator = jnp.sum(kernel, axis=-1)
        numerator = jnp.einsum(
            "hqk,khd->qhd",
            kernel.astype(jnp.bfloat16),
            value_rows[:row_end_index],
            preferred_element_type=jnp.float32,
        )
        outputs.append((numerator / denominator.T[:, :, None]).astype(jnp.bfloat16))
        denoms.append(denominator)
    return (jnp.concatenate(outputs, axis=0), jnp.concatenate(denoms, axis=1))


def attention_backward(
    query_rows, key_row_block, value_rows, doc_row, denoms, grad_mixed, block_rows
):
    group_rows = query_rows.shape[0]
    grad_queries = []
    grad_keys = jnp.zeros(key_row_block.shape, jnp.float32)
    grad_values = jnp.zeros(value_rows.shape, jnp.float32)
    for row_start in range(0, group_rows, block_rows):
        row_end_index = row_start + block_rows
        score_matrix, allowed, kernel = block_kernel(
            query_rows, key_row_block, doc_row, row_start, block_rows
        )
        kernel_low = kernel.astype(jnp.bfloat16)
        denominator = denoms[:, row_start:row_end_index]
        numerator = jnp.einsum(
            "hqk,khd->qhd",
            kernel_low,
            value_rows[:row_end_index],
            preferred_element_type=jnp.float32,
        )
        grad_output = grad_mixed[row_start:row_end_index].astype(jnp.float32)
        grad_numer = (grad_output / denominator.T[:, :, None]).astype(jnp.bfloat16)
        grad_denom = -jnp.sum(grad_output * numerator, axis=-1).T / (denominator * denominator)
        grad_kernel = (
            jnp.einsum(
                "qhd,khd->hqk",
                grad_numer,
                value_rows[:row_end_index],
                preferred_element_type=jnp.float32,
            )
            + grad_denom[:, :, None]
        )
        score_gradients = jnp.where(allowed[None], grad_kernel * (1.0 + score_matrix), 0.0).astype(
            jnp.bfloat16
        )
        grad_queries.append(
            jnp.einsum(
                "zxu,uzc->xzc",
                score_gradients,
                key_row_block[:row_end_index],
                preferred_element_type=jnp.float32,
            )
            * 0.25
        )
        grad_keys = grad_keys.at[:row_end_index].add(
            jnp.einsum(
                "ari,ran->ian",
                score_gradients,
                query_rows[row_start:row_end_index],
                preferred_element_type=jnp.float32,
            )
            * 0.25
        )
        grad_values = grad_values.at[:row_end_index].add(
            jnp.einsum("hqk,qhd->khd", kernel_low, grad_numer, preferred_element_type=jnp.float32)
        )
    grad_query_rows = jnp.concatenate(grad_queries, axis=0).astype(jnp.bfloat16)
    return (grad_query_rows, grad_keys.astype(jnp.bfloat16), grad_values.astype(jnp.bfloat16))


def body(
    tokens,
    gain_one,
    w_query,
    w_key,
    w_value,
    w_out,
    gain_two,
    w_gate,
    w_up,
    w_down,
    doc_ids,
    cotangent,
):
    heads_here = w_query.shape[1] // FEAT
    doc_row = doc_ids[0]
    inputs = tokens.astype(jnp.float32)
    normed_one, scale_one, low_one = norm_rows(inputs, gain_one)
    gathered_one = lax.all_gather(low_one, "tensor", axis=0, tiled=True)
    group_rows = gathered_one.shape[0]
    block_rows = min(512, group_rows)
    query_flat = jnp.dot(gathered_one, w_query, preferred_element_type=jnp.float32).astype(
        jnp.bfloat16
    )
    key_flat = jnp.dot(gathered_one, w_key, preferred_element_type=jnp.float32).astype(jnp.bfloat16)
    value_flat = jnp.dot(gathered_one, w_value, preferred_element_type=jnp.float32).astype(
        jnp.bfloat16
    )
    query_rows = query_flat.reshape(group_rows, heads_here, FEAT)
    key_row_block = key_flat.reshape(group_rows, heads_here, FEAT)
    value_rows = value_flat.reshape(group_rows, heads_here, HEAD_V)
    mixed_blocks, denoms = attention_forward(
        query_rows, key_row_block, value_rows, doc_row, block_rows
    )
    mixed_heads = mixed_blocks.reshape(group_rows, heads_here * HEAD_V)
    part_rows = mixed_heads
    attn_out = lax.psum_scatter(
        jnp.dot(part_rows, w_out, preferred_element_type=jnp.float32),
        "tensor",
        scatter_dimension=0,
        tiled=True,
    )
    residual = inputs + attn_out
    normed_two, scale_two, low_two = norm_rows(residual, gain_two)
    gathered_two = lax.all_gather(low_two, "tensor", axis=0, tiled=True)
    gate_pre = jnp.dot(gathered_two, w_gate, preferred_element_type=jnp.float32)
    upward = jnp.dot(gathered_two, w_up, preferred_element_type=jnp.float32)
    sigmoid_gate = jax.nn.sigmoid(gate_pre)
    hidden = (gate_pre * sigmoid_gate * upward).astype(jnp.bfloat16)
    part_rows = hidden
    ffn_out = lax.psum_scatter(
        jnp.dot(part_rows, w_down, preferred_element_type=jnp.float32).astype(jnp.bfloat16),
        "tensor",
        scatter_dimension=0,
        tiled=True,
    ).astype(jnp.float32)
    block_out = (residual + ffn_out).astype(jnp.bfloat16)
    grad_rows = lax.all_gather(cotangent, "tensor", axis=0, tiled=True)
    grad_down_w = contract_rows(hidden, grad_rows)
    grad_hidden = times_transposed(grad_rows, w_down)
    slope_gate = sigmoid_gate * (1.0 + gate_pre * (1.0 - sigmoid_gate))
    grad_gate_act = (grad_hidden * upward * slope_gate).astype(jnp.bfloat16)
    grad_upward = (grad_hidden * (gate_pre * sigmoid_gate)).astype(jnp.bfloat16)
    grad_gate_w = contract_rows(gathered_two, grad_gate_act)
    grad_up_w = contract_rows(gathered_two, grad_upward)
    grad_normed_two = lax.psum_scatter(
        (times_transposed(grad_gate_act, w_gate) + times_transposed(grad_upward, w_up)).astype(
            jnp.bfloat16
        ),
        "tensor",
        scatter_dimension=0,
        tiled=True,
    ).astype(jnp.float32)
    grad_resid_norm, gain_two_part = norm_back(grad_normed_two, normed_two, scale_two, gain_two)
    grad_resid = cotangent.astype(jnp.float32) + grad_resid_norm
    grad_attn = grad_resid.astype(jnp.bfloat16)
    grad_attn_rows = lax.all_gather(grad_attn, "tensor", axis=0, tiled=True)
    grad_mixed = times_transposed(grad_attn_rows, w_out).astype(jnp.bfloat16)
    grad_out_w = contract_rows(mixed_heads, grad_attn_rows)
    grad_query_rows, grad_key_rows, grad_value_rows = attention_backward(
        query_rows,
        key_row_block,
        value_rows,
        doc_row,
        denoms,
        grad_mixed.reshape(group_rows, heads_here, HEAD_V),
        block_rows,
    )
    grad_query_flat = grad_query_rows.reshape(group_rows, heads_here * FEAT)
    grad_key_flat = grad_key_rows.reshape(group_rows, heads_here * FEAT)
    grad_value_flat = grad_value_rows.reshape(group_rows, heads_here * HEAD_V)
    grad_query_w = contract_rows(gathered_one, grad_query_flat)
    grad_key_w = contract_rows(gathered_one, grad_key_flat)
    grad_value_w = contract_rows(gathered_one, grad_value_flat)
    grad_normed_one = lax.psum_scatter(
        (
            times_transposed(grad_query_flat, w_query)
            + times_transposed(grad_key_flat, w_key)
            + times_transposed(grad_value_flat, w_value)
        ).astype(jnp.bfloat16),
        "tensor",
        scatter_dimension=0,
        tiled=True,
    ).astype(jnp.float32)
    grad_input_norm, gain_one_part = norm_back(grad_normed_one, normed_one, scale_one, gain_one)
    grad_tokens = grad_resid + grad_input_norm
    gain_grads = lax.psum((gain_one_part, gain_two_part), ("dp", "tensor"))
    weight_grads = (
        lax.psum(grad_query_w.astype(jnp.bfloat16), "dp").astype(jnp.float32),
        lax.psum(grad_key_w.astype(jnp.bfloat16), "dp").astype(jnp.float32),
        lax.psum(grad_value_w.astype(jnp.bfloat16), "dp").astype(jnp.float32),
        lax.psum(grad_out_w.astype(jnp.bfloat16), "dp").astype(jnp.float32),
        lax.psum(grad_gate_w.astype(jnp.bfloat16), "dp").astype(jnp.float32),
        lax.psum(grad_up_w.astype(jnp.bfloat16), "dp").astype(jnp.float32),
        lax.psum(grad_down_w.astype(jnp.bfloat16), "dp").astype(jnp.float32),
    )
    return (
        block_out,
        grad_tokens,
        gain_grads[0],
        weight_grads[0],
        weight_grads[1],
        weight_grads[2],
        weight_grads[3],
        gain_grads[1],
        weight_grads[4],
        weight_grads[5],
        weight_grads[6],
    )


def solution(mesh):
    in_specs = (
        P(("dp", "tensor"), None),
        P(),
        P(None, "tensor"),
        P(None, "tensor"),
        P(None, "tensor"),
        P("tensor", None),
        P(),
        P(None, "tensor"),
        P(None, "tensor"),
        P("tensor", None),
        P("dp", None),
        P(("dp", "tensor"), None),
    )
    out_specs = (
        P(("dp", "tensor"), None),
        P(("dp", "tensor"), None),
        P(),
        P(None, "tensor"),
        P(None, "tensor"),
        P(None, "tensor"),
        P("tensor", None),
        P(),
        P(None, "tensor"),
        P(None, "tensor"),
        P("tensor", None),
    )
    return jax.shard_map(body, mesh=mesh, in_specs=in_specs, out_specs=out_specs, check_vma=False)
```

profile of v0, /device:TPU:1, one launch (start us, length us, event | category | flops | bytes accessed | tf_op | source)
XLA Modules:
  0.0 1586.0 jit_solution(5318080155431390041)
XLA Ops:
  17.0 121.2 %all-gather.5.cloned.1.call-done = bf16[2048,2048]{1,0:T(8,128)(2,1)} async-done(((bf16[256,2048]{1,0:T(8,128)(2,1)}), bf16[2048,2048]{1,0:T(8,128)(2,1)}) %all-gather.5.cloned.1.call-update) | async-done | bytes 8388624 | tf_op jit(solution)/shard_map/all_gather | solution.py:157
  169.0 8.2 fusion.81
  177.7 281.1 %reduce-scatter.5.cloned.1.call-done = f32[256,2048]{1,0:T(8,128)} async-done(((f32[2048,2048]{1,0:T(8,128)}), f32[256,2048]{1,0:T(8,128)}) %reduce-scatter.5.cloned.1.call-update) | async-done | bytes 2097168 | tf_op jit(solution)/shard_map/reduce_scatter | solution.py:175
  464.2 123.1 %all-gather.7.cloned.1.call-done = bf16[2048,2048]{1,0:T(8,128)(2,1)} async-done(((bf16[256,2048]{1,0:T(8,128)(2,1)}), bf16[2048,2048]{1,0:T(8,128)(2,1)}) %all-gather.7.cloned.1.call-update) | async-done | bytes 8388624 | tf_op jit(solution)/shard_map/all_gather | solution.py:183
  587.3 11.2 fusion.83
  598.5 8.0 fusion.82
  606.4 106.2 %all-gather.9.cloned.1.call-done = bf16[2048,2048]{1,0:T(8,128)(2,1)} async-done(((bf16[256,2048]{1,0:T(8,128)(2,1)}), bf16[2048,2048]{1,0:T(8,128)(2,1)}) %all-gather.9.cloned.1.call-update) | async-done | bytes 8388624 | tf_op jit(solution)/shard_map/all_gather | solution.py:196
  712.6 14.6 multiply_convert_fusion
  727.3 10.5 fusion.84
  737.8 12.6 add_convert_fusion.1
  750.4 147.8 %reduce-scatter.9.cloned.1.call-done = bf16[256,2048]{1,0:T(8,128)(2,1)} async-done(((bf16[2048,2048]{1,0:T(8,128)(2,1)}), bf16[256,2048]{1,0:T(8,128)(2,1)}) %reduce-scatter.9.cloned.1.call-update) | async-done | bytes 1048592 | tf_op jit(solution)/shard_map/reduce_scatter | solution.py:204
  905.5 10.9 convolution_convert_fusion.1
  916.4 10.9 convolution_convert_fusion.2
  927.4 7.8 convolution_convert_fusion.3
  935.2 93.8 %all-gather.11.cloned.1.call-done = bf16[2048,2048]{1,0:T(8,128)(2,1)} async-done(((bf16[256,2048]{1,0:T(8,128)(2,1)}), bf16[2048,2048]{1,0:T(8,128)(2,1)}) %all-gather.11.cloned.1.call-update) | async-done | bytes 8388624 | tf_op jit(solution)/shard_map/all_gather | solution.py:215
  1029.1 6.1 convolution_convert_fusion.6
  1071.8 8.9 fusion.58
  1080.7 8.1 fusion.85
  1088.8 15.9 add_convert_fusion
  1104.8 11.1 convolution_convert_fusion
  1115.9 151.0 %all-reduce.6.cloned.1.call-done = (bf16[2048,32]{0,1:T(8,128)(2,1)}, bf16[2048,32]{0,1:T(8,128)(2,1)}, bf16[2048,256]{1,0:T(8,128)(2,1)}, bf16[256,2048]{1,0:T(...) async-done(((bf16[2048,32]{0,1:T(8,128)(2,1)}, bf16[2048,32]{0,1:T(8,128)(2,1)}, bf16[2048,256]{1,0:T(8,128)(2,1)}, ...) | async-done | bytes 11010064 | tf_op jit(solution)/shard_map/psum | solution.py:247
  1284.6 135.4 %reduce-scatter.11.cloned.1.call-done = bf16[256,2048]{1,0:T(8,128)(2,1)} async-done(((bf16[2048,2048]{1,0:T(8,128)(2,1)}), bf16[256,2048]{1,0:T(8,128)(2,1)}) %reduce-scatter.11.cloned.1.call-update) | async-done | bytes 1048592 | tf_op jit(solution)/shard_map/reduce_scatter | solution.py:233
  1422.4 43.3 %all-reduce.2 = (f32[2048]{0:T(1024)}, f32[2048]{0:T(1024)}) all-reduce(f32[2048]{0:T(1024)S(1)} %get-tuple-element.125, f32[2048]{0:T(1024)S(1)} %copy-done.56), channel_id=1, replica_groups=mesh['dp'=4,'tensor'=8] {'dp','tensor'}, use_global_device_ids=true, to_apply=%region_17.18 | all-reduce | flops 4096 | bytes 32768 | tf_op jit(solution)/shard_map/psum | solution.py:245
  1465.7 107.4 %reduce-scatter.7.cloned.1.call-done = bf16[256,2048]{1,0:T(8,128)(2,1)} async-done(((bf16[2048,2048]{1,0:T(8,128)(2,1)}), bf16[256,2048]{1,0:T(8,128)(2,1)}) %reduce-scatter.7.cloned.1.call-update) | async-done | bytes 1048592 | tf_op jit(solution)/shard_map/reduce_scatter | solution.py:189
  (288 shorter events, 115.5 us)
Async XLA Ops:
  7.2 705.5 %copy-start = (bf16[704,2048]{1,0:T(8,128)(2,1)S(1)}, bf16[704,2048]{1,0:T(8,128)(2,1)}, u32[]{:S(2)}) copy-start(bf16[704,2048]{1,0:T(8,128)(2,1)} %param.41) | copy-start | bytes 8650756
  7.2 131.0 %copy-start.25 = (bf16[2048,32]{0,1:T(8,128)(2,1)S(1)}, bf16[2048,32]{0,1:T(8,128)(2,1)}, u32[]{:S(2)}) copy-start(bf16[2048,32]{0,1:T(8,128)(2,1)} %param.35) | copy-start | bytes 393220
  7.2 131.0 %all-gather.5.cloned.1.call-start = ((), (), s32[]{:S(2)}) async-start(), calls=%async_computation.4 | async-start | bytes 9437184 | tf_op jit(solution)/shard_map/all_gather | solution.py:157
  11.5 447.3 %reduce-scatter.5.cloned.1.call-start = ((), (), s32[]{:S(2)}) async-start(), calls=%async_computation.5 | async-start | bytes 18874368 | tf_op jit(solution)/shard_map/reduce_scatter | solution.py:175
  13.1 141.0 %copy-start.27 = (pred[512,1024]{1,0:T(8,128)(4,1)}, pred[512,1024]{1,0:T(8,128)(4,1)S(1)}, u32[]{:S(2)}) copy-start(pred[512,1024]{1,0:T(8,128)(4,1)S(1)} %fusion.36) | copy-start | bytes 1572868
  144.4 17.2 %copy-start.11 = (bf16[2048,32]{0,1:T(8,128)(2,1)}, bf16[2048,32]{0,1:T(8,128)(2,1)S(1)}, u32[]{:S(2)}) copy-start(bf16[2048,32]{0,1:T(8,128)(2,1)S(1)} %convolution_convert_fusion.10) | copy-start | bytes 393220
  146.9 17.8 %copy-start.9 = (bf16[2048,256]{0,1:T(8,128)(2,1)}, bf16[2048,256]{0,1:T(8,128)(2,1)S(1)}, u32[]{:S(2)}) copy-start(bf16[2048,256]{0,1:T(8,128)(2,1)S(1)} %convolution_convert_fusion.7) | copy-start | bytes 3145732
  177.2 285.1 %copy-start.44 = (f32[2048]{0:T(1024)S(1)}, f32[2048]{0:T(1024)}, u32[]{:S(2)}) copy-start(f32[2048]{0:T(1024)} %param.38) | copy-start | bytes 24580
  177.2 410.0 %all-gather.7.cloned.1.call-start = ((), (), s32[]{:S(2)}) async-start(), calls=%async_computation.6 | async-start | bytes 9437184 | tf_op jit(solution)/shard_map/all_gather | solution.py:183
  461.0 440.6 %copy-start.57 = (f32[256]{0:T(256)}, f32[256]{0:T(256)S(1)}, u32[]{:S(2)}) copy-start(f32[256]{0:T(256)S(1)} %add_rsqrt_fusion) | copy-start | bytes 3076
  463.6 249.1 %all-gather.9.cloned.1.call-start = ((), (), s32[]{:S(2)}) async-start(), calls=%async_computation.8 | async-start | bytes 9437184 | tf_op jit(solution)/shard_map/all_gather | solution.py:196
  464.2 434.0 %reduce-scatter.9.cloned.1.call-start = ((), (), s32[]{:S(2)}) async-start(), calls=%async_computation.9 | async-start | bytes 9437184 | tf_op jit(solution)/shard_map/reduce_scatter | solution.py:204
  750.4 278.7 %all-gather.11.cloned.1.call-start = ((), (), s32[]{:S(2)}) async-start(), calls=%async_computation.10 | async-start | bytes 9437184 | tf_op jit(solution)/shard_map/all_gather | solution.py:215
  905.4 361.4 %all-reduce.6.cloned.1.call-start = ((), (), s32[]{:S(2)}) async-start(), calls=%async_computation.12 | async-start | bytes 22020096 | tf_op jit(solution)/shard_map/psum | solution.py:247
  905.5 21.9 %slice-start.5 = ((s8[8388608]{0:T(1024)(128)(4,1)}), s8[4194304]{0:T(1024)(128)(4,1)S(1)}, s32[]{:S(2)}) async-start(s8[8388608]{0:T(1024)(128)(4,1)} %bitcast.245), calls=%async_computation.18 | async-start | bytes 8388608
  935.2 100.1 %copy-start.70 = (f32[2,512]{1,0:T(2,128)S(1)}, f32[2,512]{1,0:T(2,128)}, u32[]{:S(2)}) copy-start(f32[2,512]{1,0:T(2,128)} %copy-done.69) | copy-start | bytes 12292
  1070.9 349.0 %reduce-scatter.11.cloned.1.call-start = ((), (), s32[]{:S(2)}) async-start(), calls=%async_computation.11 | async-start | bytes 9437184 | tf_op jit(solution)/shard_map/reduce_scatter | solution.py:233
  1104.7 468.4 %reduce-scatter.7.cloned.1.call-start = ((), (), s32[]{:S(2)}) async-start(), calls=%async_computation.7 | async-start | bytes 9437184 | tf_op jit(solution)/shard_map/reduce_scatter | solution.py:189
  1281.2 138.7 %copy-start.55 = (f32[2048]{0:T(1024)S(1)}, f32[2048]{0:T(1024)}, u32[]{:S(2)}) copy-start(f32[2048]{0:T(1024)} %param.33) | copy-start | bytes 24580
  1281.2 138.7 %copy-start.60 = (f32[256]{0:T(256)S(1)}, f32[256]{0:T(256)}, u32[]{:S(2)}) copy-start(f32[256]{0:T(256)} %copy-done.59) | copy-start | bytes 3076
  1281.2 141.1 %copy-start.56 = (f32[2048]{0:T(1024)S(1)}, f32[2048]{0:T(1024)}, u32[]{:S(2)}) copy-start(f32[2048]{0:T(1024)} %get-tuple-element.123) | copy-start | bytes 24580
  1281.2 291.9 %copy-start.45 = (f32[2048]{0:T(1024)S(1)}, f32[2048]{0:T(1024)}, u32[]{:S(2)}) copy-start(f32[2048]{0:T(1024)} %param.38) | copy-start | bytes 24580
  1281.2 291.9 %copy-start.58 = (f32[256]{0:T(256)S(1)}, f32[256]{0:T(256)}, u32[]{:S(2)}) copy-start(f32[256]{0:T(256)} %copy-done.57) | copy-start | bytes 3076
  1281.2 291.9 %copy-start.62 = (f32[256]{0:T(256)S(1)}, f32[256]{0:T(256)}, u32[]{:S(2)}) copy-start(f32[256]{0:T(256)} %copy-done.61) | copy-start | bytes 3076
  (81 other events, 384.4 us)
Sparse Core Ops, SparseCore 0:
  11.6 126.5 all-gather.4
  177.4 281.4 reduce-scatter.4
  463.7 123.5 all-gather.6
  589.5 123.1 all-gather.8
  750.5 147.6 reduce-scatter.8
  905.6 123.4 all-gather.10
  1071.0 195.7 all-reduce.5
  1270.5 149.4 reduce-scatter.10
  1424.0 149.0 reduce-scatter.6
where the time goes:
time: 1600 us; the launch traced here: 1590 us
  waiting for transfers between devices  1270 us (79%)
  matrix products  206 us (13%)
  other arithmetic  46.1 us (3%)
  blocking collectives  43.3 us (3%)
    reduce_scatter x1, waiting for transfers between devices, body(): lax.psum_scatter(jnp.dot(part_rows, w_out, preferred_element_type=jnp.flo...  281 us
    psum x1, waiting for transfers between devices, body(): lax.psum(grad_query_w.astype(jnp.bfloat16), 'dp').astype(jnp.float32)  151 us
    reduce_scatter x1, waiting for transfers between devices, body(): lax.psum_scatter((times_transposed(grad_gate_act, w_gate) + times_transpo...  148 us
    reduce_scatter x1, waiting for transfers between devices, body(): lax.psum_scatter((times_transposed(grad_query_flat, w_query) + times_tran...  135 us
    all_gather x1, waiting for transfers between devices, body(): gathered_two = lax.all_gather(low_two, 'tensor', axis=0, tiled=True)  123 us
    all_gather x1, waiting for transfers between devices, body(): gathered_one = lax.all_gather(low_one, 'tensor', axis=0, tiled=True)  121 us
    reduce_scatter x1, waiting for transfers between devices, body(): lax.psum_scatter(jnp.dot(part_rows, w_down, preferred_element_type=jnp.fl...  107 us
    all_gather x1, waiting for transfers between devices, body(): grad_rows = lax.all_gather(cotangent, 'tensor', axis=0, tiled=True)  106 us
  transfers between devices with their start and end apart: 9, of which 9 were waited for; matrix products, arithmetic and copies ran while one was open for 7% of the time, Pallas kernels for 0%

commit v1 on v0

v1 whole, which is shorter than its diff:
```python
import jax
import jax.numpy as jnp
from jax import lax
from jax.sharding import Mesh
from jax.sharding import PartitionSpec as P

FEAT = 16
HEAD_V = 128
EPS = 1e-05

ALL_AXES = ("y", "k", "h", "l", "x")
SQUARE = ("k", "l", "x")


def norm_rows(values, gain_vec):
    row_scale = lax.rsqrt(jnp.mean(values * values, axis=-1, keepdims=True) + EPS)
    normed = values * row_scale
    return (normed, row_scale, (normed * gain_vec).astype(jnp.bfloat16))


def norm_back(grad_normed, normed, row_scale, gain_vec):
    weighted = grad_normed * gain_vec
    inner_mean = jnp.mean(weighted * normed, axis=-1, keepdims=True)
    return row_scale * (weighted - normed * inner_mean)


def dot_nn(left_mat, right_mat):
    return jnp.dot(left_mat, right_mat, preferred_element_type=jnp.float32)


def dot_tn(left_mat, right_mat):
    return lax.dot_general(
        left_mat, right_mat, (((0,), (0,)), ((), ())), preferred_element_type=jnp.float32
    )


def dot_nt(left_mat, right_mat):
    return lax.dot_general(
        left_mat, right_mat, (((1,), (1,)), ((), ())), preferred_element_type=jnp.float32
    )


def block_kernel(query_rows, key_row_block, doc_row, row_start, block_rows):
    row_end_index = row_start + block_rows
    query_portion = query_rows[row_start:row_end_index]
    score_matrix = (
        jnp.einsum(
            "gsn,jsn->sgj",
            query_portion,
            key_row_block[:row_end_index],
            preferred_element_type=jnp.float32,
        )
        * 0.25
    )
    query_index = row_start + jnp.arange(block_rows)
    key_index = jnp.arange(row_end_index)
    allowed = (doc_row[row_start:row_end_index, None] == doc_row[None, :row_end_index]) & (
        query_index[:, None] >= key_index[None, :]
    )
    kernel = jnp.where(allowed[None], 1.0 + score_matrix + 0.5 * score_matrix * score_matrix, 0.0)
    return (score_matrix, allowed, kernel)


def attention_forward(query_rows, key_row_block, value_rows, doc_row, block_rows):
    group_rows = query_rows.shape[0]
    outputs = []
    denoms = []
    for row_start in range(0, group_rows, block_rows):
        row_end_index = row_start + block_rows
        score_matrix, allowed, kernel = block_kernel(
            query_rows, key_row_block, doc_row, row_start, block_rows
        )
        denominator = jnp.sum(kernel, axis=-1)
        numerator = jnp.einsum(
            "hqk,khd->qhd",
            kernel.astype(jnp.bfloat16),
            value_rows[:row_end_index],
            preferred_element_type=jnp.float32,
        )
        outputs.append((numerator / denominator.T[:, :, None]).astype(jnp.bfloat16))
        denoms.append(denominator)
    return (jnp.concatenate(outputs, axis=0), jnp.concatenate(denoms, axis=1))


def attention_backward(
    query_rows, key_row_block, value_rows, doc_row, denoms, grad_mixed, block_rows
):
    group_rows = query_rows.shape[0]
    grad_queries = []
    grad_keys = jnp.zeros(key_row_block.shape, jnp.float32)
    grad_values = jnp.zeros(value_rows.shape, jnp.float32)
    for row_start in range(0, group_rows, block_rows):
        row_end_index = row_start + block_rows
        score_matrix, allowed, kernel = block_kernel(
            query_rows, key_row_block, doc_row, row_start, block_rows
        )
        kernel_low = kernel.astype(jnp.bfloat16)
        denominator = denoms[:, row_start:row_end_index]
        numerator = jnp.einsum(
            "hqk,khd->qhd",
            kernel_low,
            value_rows[:row_end_index],
            preferred_element_type=jnp.float32,
        )
        grad_output = grad_mixed[row_start:row_end_index].astype(jnp.float32)
        grad_numer = (grad_output / denominator.T[:, :, None]).astype(jnp.bfloat16)
        grad_denom = -jnp.sum(grad_output * numerator, axis=-1).T / (denominator * denominator)
        grad_kernel = (
            jnp.einsum(
                "qhd,khd->hqk",
                grad_numer,
                value_rows[:row_end_index],
                preferred_element_type=jnp.float32,
            )
            + grad_denom[:, :, None]
        )
        score_gradients = jnp.where(allowed[None], grad_kernel * (1.0 + score_matrix), 0.0).astype(
            jnp.bfloat16
        )
        grad_queries.append(
            jnp.einsum(
                "zxu,uzc->xzc",
                score_gradients,
                key_row_block[:row_end_index],
                preferred_element_type=jnp.float32,
            )
            * 0.25
        )
        grad_keys = grad_keys.at[:row_end_index].add(
            jnp.einsum(
                "ari,ran->ian",
                score_gradients,
                query_rows[row_start:row_end_index],
                preferred_element_type=jnp.float32,
            )
            * 0.25
        )
        grad_values = grad_values.at[:row_end_index].add(
            jnp.einsum("hqk,qhd->khd", kernel_low, grad_numer, preferred_element_type=jnp.float32)
        )
    grad_query_rows = jnp.concatenate(grad_queries, axis=0).astype(jnp.bfloat16)
    return (grad_query_rows, grad_keys.astype(jnp.bfloat16), grad_values.astype(jnp.bfloat16))


def make_body(y_size):
    y_pairs = [(i, i ^ 1) for i in range(y_size)]

    def trade(values):
        return lax.ppermute(values, ("k", "h"), [(0, 0), (1, 2), (2, 1), (3, 3)])

    def over_y(values):
        return lax.ppermute(values, "y", y_pairs)

    def fetch_shard(own, axis):
        half = own.shape[axis] // 2
        mine = lax.dynamic_slice_in_dim(own, (lax.axis_index("y") % 2) * half, half, axis)
        got = trade(mine)
        other = over_y(got)
        return jnp.concatenate([got, other], axis=axis)

    def reduce_grad(part, axis):
        half = part.shape[axis] // 2
        mine = lax.slice_in_dim(part, 0, half, axis=axis)
        other = lax.slice_in_dim(part, half, 2 * half, axis=axis)
        total = mine + over_y(other)
        step = 2
        while step < y_size:
            total = total + lax.ppermute(total, "y", [(i, i ^ step) for i in range(y_size)])
            step *= 2
        arrived = lax.ppermute(total, ("k", "h"), [(1, 0), (2, 3)])
        total = total + arrived
        twin = lax.ppermute(total, ("k", "h"), [(0, 2), (3, 1)])
        mine = jnp.where(lax.axis_index("k") == lax.axis_index("h"), total, twin)
        other = over_y(mine)
        first = lax.axis_index("y") % 2 == 0
        return jnp.where(
            first,
            jnp.concatenate([mine, other], axis=axis),
            jnp.concatenate([other, mine], axis=axis),
        ).astype(jnp.float32)

    def gather(rows):
        return lax.all_gather(rows, SQUARE, axis=0, tiled=True)

    def scatter(parts):
        return lax.psum_scatter(parts, SQUARE, scatter_dimension=0, tiled=True)

    def body(
        tokens,
        gain_one,
        w_query,
        w_key,
        w_value,
        w_out,
        gain_two,
        w_gate,
        w_up,
        w_down,
        doc_ids,
        cotangent,
    ):
        doc_row = trade(doc_ids)[0]
        own_tokens = trade(tokens)
        inputs = own_tokens.astype(jnp.float32)
        own_grad = trade(cotangent)
        wq = fetch_shard(w_query.T, 0)
        wk = fetch_shard(w_key.T, 0)
        wv = fetch_shard(w_value, 1)
        wo = fetch_shard(w_out, 0)
        wg = fetch_shard(w_gate.T, 0)
        wu = fetch_shard(w_up.T, 0)
        wd = fetch_shard(w_down, 0)
        heads_here = wq.shape[0] // FEAT
        wqk = jnp.concatenate([wq, wk], axis=0)

        normed_one, scale_one, low_one = norm_rows(inputs, gain_one)
        gathered_one = gather(low_one)
        group_rows = gathered_one.shape[0]
        block_rows = min(512, group_rows)
        qk_flat = dot_nt(gathered_one, wqk).astype(jnp.bfloat16)
        value_flat = dot_nn(gathered_one, wv).astype(jnp.bfloat16)
        width = heads_here * FEAT
        query_rows = qk_flat[:, :width].reshape(group_rows, heads_here, FEAT)
        key_row_block = qk_flat[:, width:].reshape(group_rows, heads_here, FEAT)
        value_rows = value_flat.reshape(group_rows, heads_here, HEAD_V)
        mixed_blocks, denoms = attention_forward(
            query_rows, key_row_block, value_rows, doc_row, block_rows
        )
        mixed_heads = mixed_blocks.reshape(group_rows, heads_here * HEAD_V)
        attn_out = scatter(dot_nn(mixed_heads, wo).astype(jnp.bfloat16)).astype(jnp.float32)
        residual = inputs + attn_out
        normed_two, scale_two, low_two = norm_rows(residual, gain_two)
        grad_rows = gather(own_grad)
        gathered_two = gather(low_two)
        gate_pre = dot_nt(gathered_two, wg)
        upward = dot_nt(gathered_two, wu)
        sigmoid_gate = jax.nn.sigmoid(gate_pre)
        hidden = (gate_pre * sigmoid_gate * upward).astype(jnp.bfloat16)
        grad_hidden = dot_nt(grad_rows, wd)
        slope_gate = sigmoid_gate * (1.0 + gate_pre * (1.0 - sigmoid_gate))
        grad_gate_act = (grad_hidden * upward * slope_gate).astype(jnp.bfloat16)
        grad_upward = (grad_hidden * (gate_pre * sigmoid_gate)).astype(jnp.bfloat16)
        grad_normed_two = scatter(
            (dot_nn(grad_gate_act, wg) + dot_nn(grad_upward, wu)).astype(jnp.bfloat16)
        ).astype(jnp.float32)
        grad_gate_w = dot_tn(grad_gate_act, gathered_two).astype(jnp.bfloat16)
        grad_up_w = dot_tn(grad_upward, gathered_two).astype(jnp.bfloat16)
        grad_down_w = dot_tn(hidden, grad_rows).astype(jnp.bfloat16)
        ffn_out = scatter(dot_nn(hidden, wd).astype(jnp.bfloat16)).astype(jnp.float32)
        block_out = trade((residual + ffn_out).astype(jnp.bfloat16))

        gain_two_part = jnp.sum(grad_normed_two * normed_two, axis=0)
        grad_resid = own_grad.astype(jnp.float32) + norm_back(
            grad_normed_two, normed_two, scale_two, gain_two
        )
        grad_attn_rows = gather(grad_resid.astype(jnp.bfloat16))
        grad_mixed = dot_nt(grad_attn_rows, wo).astype(jnp.bfloat16)
        grad_out_w = dot_tn(mixed_heads, grad_attn_rows).astype(jnp.bfloat16)
        grad_query_rows, grad_key_rows, grad_value_rows = attention_backward(
            query_rows,
            key_row_block,
            value_rows,
            doc_row,
            denoms,
            grad_mixed.reshape(group_rows, heads_here, HEAD_V),
            block_rows,
        )
        grad_qk_flat = jnp.concatenate(
            [grad_query_rows.reshape(group_rows, -1), grad_key_rows.reshape(group_rows, -1)],
            axis=1,
        )
        grad_value_flat = grad_value_rows.reshape(group_rows, heads_here * HEAD_V)
        grad_normed_one = scatter(
            (dot_nn(grad_qk_flat, wqk) + dot_nt(grad_value_flat, wv)).astype(jnp.bfloat16)
        ).astype(jnp.float32)
        grad_qk_w = dot_tn(grad_qk_flat, gathered_one)
        grad_value_w = dot_tn(gathered_one, grad_value_flat)
        gain_one_part = (
            jnp.sum(grad_qk_w * wqk, axis=0) + jnp.sum(grad_value_w * wv, axis=1)
        ) / gain_one
        grad_tokens = grad_resid + norm_back(grad_normed_one, normed_one, scale_one, gain_one)
        grad_tokens = trade(grad_tokens.astype(jnp.bfloat16)).astype(jnp.float32)
        gain_parts = lax.all_gather(jnp.stack([gain_one_part, gain_two_part]), ALL_AXES)
        gain_grads = jnp.sum(gain_parts, axis=0)
        grad_qk_w = grad_qk_w.astype(jnp.bfloat16)
        grad_query_w = reduce_grad(grad_qk_w[:width], 0)
        grad_key_w = reduce_grad(grad_qk_w[width:], 0)
        return (
            block_out,
            grad_tokens,
            gain_grads[0],
            grad_query_w.T,
            grad_key_w.T,
            reduce_grad(grad_value_w.astype(jnp.bfloat16), 1),
            reduce_grad(grad_out_w, 0),
            gain_grads[1],
            reduce_grad(grad_gate_w, 0).T,
            reduce_grad(grad_up_w, 0).T,
            reduce_grad(grad_down_w, 0),
        )

    return body


def solution(mesh):
    dp_size, tensor_size = mesh.devices.shape
    fine = Mesh(mesh.devices.reshape(dp_size // 2, 2, 2, 2, tensor_size // 4), ALL_AXES)
    rows = P(ALL_AXES, None)
    shard = ("h", "l", "x")
    in_specs = (
        rows,
        P(),
        P(None, shard),
        P(None, shard),
        P(None, shard),
        P(shard, None),
        P(),
        P(None, shard),
        P(None, shard),
        P(shard, None),
        P(("y", "k"), None),
        rows,
    )
    out_specs = (
        rows,
        rows,
        P(),
        P(None, shard),
        P(None, shard),
        P(None, shard),
        P(shard, None),
        P(),
        P(None, shard),
        P(None, shard),
        P(shard, None),
    )
    return jax.shard_map(
        make_body(dp_size // 2), mesh=fine, in_specs=in_specs, out_specs=out_specs, check_vma=False
    )
```

time: 1600 us -> 1270 us (0.79)
  waiting for transfers between devices: 1270 us -> 757 us
  starting transfers between devices: 0.99 us -> 101 us
  blocking collectives: 43.3 us -> 110 us
  matrix products: 206 us -> 185 us
  local copies, waits for them, and re-layouts: 6.93 us -> 26.7 us
    ppermute x0 -> x47, waiting for transfers between devices: none -> 405 us  [the longest x12 185 us: trade(): return lax.ppermute(values, ('k', 'h'), [(0, 0), (1, 2), (2, 1), (3, 3)])]
    all_gather x4, waiting for transfers between devices: 444 us -> 52.4 us  [gather(): return lax.all_gather(rows, SQUARE, axis=0, tiled=True)]
    reduce_scatter x4, waiting for transfers between devices: 672 us -> 300 us  [scatter(): return lax.psum_scatter(parts, SQUARE, scatter_dimension=0, tiled=True)]
    psum x1 -> x0, waiting for transfers between devices: 151 us -> none  [body(): lax.psum(grad_query_w.astype(jnp.bfloat16), 'dp').astype(jnp.float32)]
    all_gather x0 -> x1, blocking collectives: none -> 110 us  [body(): lax.all_gather(jnp.stack([gain_one_part, gain_two_part]), ALL_AXES)]
    ppermute x0 -> x47, starting transfers between devices: none -> 100 us  [the longest x12 46.2 us: trade(): return lax.ppermute(values, ('k', 'h'), [(0, 0), (1, 2), (2, 1), (3, 3)])]
    psum x1 -> x0, blocking collectives: 43.3 us -> none  [body(): gain_grads = lax.psum((gain_one_part, gain_two_part), ('dp', 'tensor'))]
    dot_general x21 -> x18, matrix products: 167 us -> 145 us  [the longest x6 58 us: dot_nn(): return jnp.dot(left_mat, right_mat, preferred_element_type=jnp.float32)]
  transfers between devices with their start and end apart: 9 -> 55, of which waited for: 9 -> 28; matrix products, arithmetic and copies ran while one was open for 7% -> 10% of each run, Pallas kernels for 0% -> 0%
where the time goes in v1:
time: 1270 us; the launch traced here: 1260 us
  waiting for transfers between devices  757 us (60%)
  matrix products  185 us (15%)
  blocking collectives  110 us (9%)
  starting transfers between devices  101 us (8%)
  other arithmetic  62 us (5%)
  local copies, waits for them, and re-layouts  26.7 us (2%)
  between operations  16.5 us (1%)
    reduce_scatter x4, waiting for transfers between devices, scatter(): return lax.psum_scatter(parts, SQUARE, scatter_dimension=0, tiled=True)  300 us
    ppermute x12, waiting for transfers between devices, trade(): return lax.ppermute(values, ('k', 'h'), [(0, 0), (1, 2), (2, 1), (3, 3)])  185 us
    ppermute x21, waiting for transfers between devices, over_y(): return lax.ppermute(values, 'y', y_pairs)  156 us
    all_gather x1, blocking collectives, body(): lax.all_gather(jnp.stack([gain_one_part, gain_two_part]), ALL_AXES)  110 us
    dot_general x6, matrix products, dot_nn(): return jnp.dot(left_mat, right_mat, preferred_element_type=jnp.float32)  58 us
    dot_general x6, matrix products, dot_nt(): lax.dot_general(left_mat, right_mat, (((1,), (1,)), ((), ())), preferred_...  54.9 us
    all_gather x4, waiting for transfers between devices, gather(): return lax.all_gather(rows, SQUARE, axis=0, tiled=True)  52.4 us
    ppermute x12, starting transfers between devices, trade(): return lax.ppermute(values, ('k', 'h'), [(0, 0), (1, 2), (2, 1), (3, 3)])  46.2 us
  transfers between devices with their start and end apart: 55, of which 28 were waited for; matrix products, arithmetic and copies ran while one was open for 10% of the time, Pallas kernels for 0%

profile of v1, /device:TPU:1, one launch (start us, length us, event | category | flops | bytes accessed | tf_op | source)
XLA Modules:
  0.0 1258.3 jit_solution(15396055613430344092)
XLA Ops:
  13.1 23.9 %collective-permute-done = bf16[256,2048]{1,0:T(8,128)(2,1)S(1)} collective-permute-done((bf16[256,2048]{1,0:T(8,128)(2,1)}, bf16[256,2048]{1,0:T(8,128)(2,1)S(1)}, u32[]{:S(2)}, u32[]{:S(2)}) %collective-permute-start) | collective-permute-done | bytes 1048608 | tf_op jit(solution)/shard_map/ppermute | solution.py:149
  69.7 20.6 %collective-permute-done.1 = bf16[2048,128]{0,1:T(8,128)(2,1)S(1)} collective-permute-done((bf16[2048,128]{0,1:T(8,128)(2,1)}, bf16[2048,128]{0,1:T(8,128)(2,1)S(1)}, u32[]{:S(2)}, u32[]{:S(2)}) %collective-permute-start.1) | collective-permute-done | bytes 524320 | tf_op jit(solution)/shard_map/ppermute | solution.py:149
  149.0 30.0 %collective-permute-done.17 = bf16[256,2048]{1,0:T(8,128)(2,1)} collective-permute-done((bf16[256,2048]{1,0:T(8,128)(2,1)}, bf16[256,2048]{1,0:T(8,128)(2,1)}, u32[]{:S(2)}, u32[]{:S(2)}) %collective-permute-start.17) | collective-permute-done | bytes 1048608 | tf_op jit(solution)/shard_map/ppermute | solution.py:149
  179.1 133.4 %reduce-scatter.5.cloned.1.call-done = bf16[256,2048]{1,0:T(8,128)(2,1)} async-done(((bf16[2048,2048]{1,0:T(8,128)(2,1)}), bf16[256,2048]{1,0:T(8,128)(2,1)}) %reduce-scatter.5.cloned.1.call-update) | async-done | bytes 1048592 | tf_op jit(solution)/shard_map/reduce_scatter | solution.py:186
  329.8 31.2 %collective-permute-done.10 = bf16[352,2048]{1,0:T(8,128)(2,1)S(1)} collective-permute-done((bf16[352,2048]{1,0:T(8,128)(2,1)S(1)}, bf16[352,2048]{1,0:T(8,128)(2,1)S(1)}, u32[]{:S(2)}, u32[]{:S(2)}) %collective-permute-start.10) | collective-permute-done | bytes 1441824 | tf_op jit(solution)/shard_map/ppermute | solution.py:149
  362.2 25.1 %collective-permute-done.12 = bf16[352,2048]{1,0:T(8,128)(2,1)S(1)} collective-permute-done((bf16[352,2048]{1,0:T(8,128)(2,1)S(1)}, bf16[352,2048]{1,0:T(8,128)(2,1)S(1)}, u32[]{:S(2)}, u32[]{:S(2)}) %collective-permute-start.12) | collective-permute-done | bytes 1441824 | tf_op jit(solution)/shard_map/ppermute | solution.py:149
  388.7 27.9 %collective-permute-done.14 = bf16[352,2048]{1,0:T(8,128)(2,1)S(1)} collective-permute-done((bf16[352,2048]{1,0:T(8,128)(2,1)S(1)}, bf16[352,2048]{1,0:T(8,128)(2,1)S(1)}, u32[]{:S(2)}, u32[]{:S(2)}) %collective-permute-start.14) | collective-permute-done | bytes 1441824 | tf_op jit(solution)/shard_map/ppermute | solution.py:149
  419.7 15.2 %collective-permute-done.15 = bf16[352,2048]{1,0:T(8,128)(2,1)S(1)} collective-permute-done((bf16[352,2048]{1,0:T(8,128)(2,1)S(1)}, bf16[352,2048]{1,0:T(8,128)(2,1)S(1)}, u32[]{:S(2)}, u32[]{:S(2)}) %collective-permute-start.15) | collective-permute-done | bytes 1441824 | tf_op jit(solution)/shard_map/ppermute | solution.py:152
  462.3 12.3 fusion.1
  474.7 12.5 fusion.90
  487.1 12.5 add_convert_fusion.1
  499.7 166.1 %reduce-scatter.9.cloned.1.call-done = bf16[256,2048]{1,0:T(8,128)(2,1)} async-done(((bf16[2048,2048]{1,0:T(8,128)(2,1)}), bf16[256,2048]{1,0:T(8,128)(2,1)}) %reduce-scatter.9.cloned.1.call-update) | async-done | bytes 1048592 | tf_op jit(solution)/shard_map/reduce_scatter | solution.py:186
  672.3 47.2 %all-gather.13.cloned.1.call-done = bf16[2048,2048]{1,0:T(8,128)(2,1)} async-done(((bf16[256,2048]{1,0:T(8,128)(2,1)}), bf16[2048,2048]{1,0:T(8,128)(2,1)}) %all-gather.13.cloned.1.call-update) | async-done | bytes 8388624 | tf_op jit(solution)/shard_map/all_gather | solution.py:183
  759.4 11.5 add_convert_fusion
  811.5 54.7 %collective-permute-done.39 = bf16[352,2048]{1,0:T(8,128)(2,1)S(1)} collective-permute-done((bf16[352,2048]{1,0:T(8,128)(2,1)S(1)}, bf16[352,2048]{1,0:T(8,128)(2,1)S(1)}, u32[]{:S(2)}, u32[]{:S(2)}) %collective-permute-start.39) | collective-permute-done | bytes 1441824 | tf_op jit(solution)/shard_map/ppermute | solution.py:152
  872.1 25.1 %collective-permute-done.43 = bf16[352,2048]{1,0:T(8,128)(2,1)S(1)} collective-permute-done((bf16[352,2048]{1,0:T(8,128)(2,1)S(1)}, bf16[352,2048]{1,0:T(8,128)(2,1)S(1)}, u32[]{:S(2)}, u32[]{:S(2)}) %collective-permute-start.43) | collective-permute-done | bytes 1441824 | tf_op jit(solution)/shard_map/ppermute | solution.py:152
  910.7 19.2 %collective-permute-done.36 = bf16[352,2048]{1,0:T(8,128)(2,1)S(1)} collective-permute-done((bf16[352,2048]{1,0:T(8,128)(2,1)S(1)}, bf16[352,2048]{1,0:T(8,128)(2,1)S(1)}, u32[]{:S(2)}, u32[]{:S(2)}) %collective-permute-start.36) | collective-permute-done | bytes 1441824 | tf_op jit(solution)/shard_map/ppermute | solution.py:170
  931.8 13.6 %collective-permute-done.44 = bf16[352,2048]{1,0:T(8,128)(2,1)S(1)} collective-permute-done((bf16[352,2048]{1,0:T(8,128)(2,1)S(1)}, bf16[352,2048]{1,0:T(8,128)(2,1)S(1)}, u32[]{:S(2)}, u32[]{:S(2)}) %collective-permute-start.44) | collective-permute-done | bytes 1441824 | tf_op jit(solution)/shard_map/ppermute | solution.py:170
  954.0 19.1 %collective-permute-done.45 = bf16[352,2048]{1,0:T(8,128)(2,1)} collective-permute-done((bf16[352,2048]{1,0:T(8,128)(2,1)}, bf16[352,2048]{1,0:T(8,128)(2,1)}, u32[]{:S(2)}, u32[]{:S(2)}) %collective-permute-start.45) | collective-permute-done | bytes 1441824 | tf_op jit(solution)/shard_map/ppermute | solution.py:172
  981.1 12.7 %collective-permute-done.38 = bf16[352,2048]{1,0:T(8,128)(2,1)} collective-permute-done((bf16[352,2048]{1,0:T(8,128)(2,1)S(1)}, bf16[352,2048]{1,0:T(8,128)(2,1)}, u32[]{:S(2)}, u32[]{:S(2)}) %collective-permute-start.38) | collective-permute-done | bytes 1441824 | tf_op jit(solution)/shard_map/ppermute | solution.py:152
  998.4 26.2 %collective-permute-done.46 = bf16[352,2048]{1,0:T(8,128)(2,1)} collective-permute-done((bf16[352,2048]{1,0:T(8,128)(2,1)S(1)}, bf16[352,2048]{1,0:T(8,128)(2,1)}, u32[]{:S(2)}, u32[]{:S(2)}) %collective-permute-start.46) | collective-permute-done | bytes 1441824 | tf_op jit(solution)/shard_map/ppermute | solution.py:152
  1048.5 109.7 %all-gather.1 = f32[32,2,2048]{2,1,0:T(2,128)S(1)} all-gather(f32[1,2,2048]{2,1,0:T(2,128)S(1)} %maximum_bitcast_fusion), channel_id=2, replica_groups=mesh['y'=2,'k'=2,'h'=2,'l'=2,'x'=2] {'y','k','h','l','x'}, dimensions={0}, use_global_device_ids=true | all-gather | bytes 540672 | tf_op jit(solution)/shard_map/all_gather | solution.py:283
  1167.0 13.1 %collective-permute-start.32 = (bf16[128,2048]{1,0:T(8,128)(2,1)S(1)}, bf16[128,2048]{1,0:T(8,128)(2,1)S(1)}, u32[]{:S(2)}, u32[]{:S(2)}) collective-permute-start(bf16[128,2048]{1,0:T(8,128)(2,1)S(1)} %slice_add_fusion.3), channel_id=1, source_target_pairs={{4,0},{8,12},{5,1},{9,13},{6,2},{10,14},{7,3},{11,15},{20,16},{24,... | collective-permute-start | bytes 1572872 | tf_op jit(solution)/shard_map/ppermute | solution.py:170
  1219.2 18.2 %collective-permute-done.18 = bf16[256,2048]{1,0:T(8,128)(2,1)} collective-permute-done((bf16[256,2048]{1,0:T(8,128)(2,1)}, bf16[256,2048]{1,0:T(8,128)(2,1)}, u32[]{:S(2)}, u32[]{:S(2)}) %collective-permute-start.18) | collective-permute-done | bytes 1048608 | tf_op jit(solution)/shard_map/ppermute | solution.py:149
  (439 shorter events, 360.6 us)
Async XLA Ops:
  7.2 97.6 %all-gather.7.cloned.1.call-start = ((), (), s32[]{:S(2)}) async-start(), calls=%async_computation.4 | async-start | bytes 9437184 | tf_op jit(solution)/shard_map/all_gather | solution.py:183
  40.6 272.0 %reduce-scatter.5.cloned.1.call-start = ((), (), s32[]{:S(2)}) async-start(), calls=%async_computation.5 | async-start | bytes 9437184 | tf_op jit(solution)/shard_map/reduce_scatter | solution.py:186
  142.7 293.5 %all-gather.11.cloned.1.call-start = ((), (), s32[]{:S(2)}) async-start(), calls=%async_computation.8 | async-start | bytes 9437184 | tf_op jit(solution)/shard_map/all_gather | solution.py:183
  179.1 273.5 %all-gather.9.cloned.1.call-start = ((), (), s32[]{:S(2)}) async-start(), calls=%async_computation.6 | async-start | bytes 9437184 | tf_op jit(solution)/shard_map/all_gather | solution.py:183
  317.5 348.4 %reduce-scatter.9.cloned.1.call-start = ((), (), s32[]{:S(2)}) async-start(), calls=%async_computation.9 | async-start | bytes 9437184 | tf_op jit(solution)/shard_map/reduce_scatter | solution.py:186
  317.7 43.2 %collective-permute-start.10 = (bf16[352,2048]{1,0:T(8,128)(2,1)S(1)}, bf16[352,2048]{1,0:T(8,128)(2,1)S(1)}, u32[]{:S(2)}, u32[]{:S(2)}) collective-permute-start(bf16[352,2048]{1,0:T(8,128)(2,1)S(1)} %dynamic-slice_bitcast_fusion.1), channel_id=1, source_target_pairs={{0,0},{4,8},{8,4},{12,12},{1,1},{5,9},{9,5},{13,13},{2,2},{6,10},{... | collective-permute-start | bytes 4325384 | tf_op jit(solution)/shard_map/ppermute | solution.py:149
  322.7 64.6 %collective-permute-start.12 = (bf16[352,2048]{1,0:T(8,128)(2,1)S(1)}, bf16[352,2048]{1,0:T(8,128)(2,1)S(1)}, u32[]{:S(2)}, u32[]{:S(2)}) collective-permute-start(bf16[352,2048]{1,0:T(8,128)(2,1)S(1)} %dynamic-slice_bitcast_fusion), channel_id=1, source_target_pairs={{0,0},{4,8},{8,4},{12,12},{1,1},{5,9},{9,5},{13,13},{2,2},{6,10},{... | collective-permute-start | bytes 4325384 | tf_op jit(solution)/shard_map/ppermute | solution.py:149
  324.9 91.7 %collective-permute-start.14 = (bf16[352,2048]{1,0:T(8,128)(2,1)S(1)}, bf16[352,2048]{1,0:T(8,128)(2,1)S(1)}, u32[]{:S(2)}, u32[]{:S(2)}) collective-permute-start(bf16[352,2048]{1,0:T(8,128)(2,1)S(1)} %constant_dynamic-slice_fusion), channel_id=1, source_target_pairs={{0,0},{4,8},{8,4},{12,12},{1,1},{5,9},{9,5},{13,13},{2,2},{6,10},{... | collective-permute-start | bytes 4325384 | tf_op jit(solution)/shard_map/ppermute | solution.py:149
  360.9 58.5 %collective-permute-start.11 = (bf16[352,2048]{1,0:T(8,128)(2,1)S(1)}, bf16[352,2048]{1,0:T(8,128)(2,1)S(1)}, u32[]{:S(2)}, u32[]{:S(2)}) collective-permute-start(bf16[352,2048]{1,0:T(8,128)(2,1)S(1)} %collective-permute-done.10), channel_id=1, source_target_pairs={{0,16},{16,0},{1,17},{17,1},{2,18},{18,2},{3,19},{19,3},{4,20},{20... | collective-permute-start | bytes 4325384 | tf_op jit(solution)/shard_map/ppermute | solution.py:152
  499.7 219.8 %all-gather.13.cloned.1.call-start = ((), (), s32[]{:S(2)}) async-start(), calls=%async_computation.10 | async-start | bytes 9437184 | tf_op jit(solution)/shard_map/all_gather | solution.py:183
  672.0 519.4 %reduce-scatter.11.cloned.1.call-start = ((), (), s32[]{:S(2)}) async-start(), calls=%async_computation.11 | async-start | bytes 9437184 | tf_op jit(solution)/shard_map/reduce_scatter | solution.py:186
  770.9 422.4 %reduce-scatter.7.cloned.1.call-start = ((), (), s32[]{:S(2)}) async-start(), calls=%async_computation.7 | async-start | bytes 9437184 | tf_op jit(solution)/shard_map/reduce_scatter | solution.py:186
  802.3 68.2 %collective-permute-start.35 = (bf16[352,2048]{1,0:T(8,128)(2,1)S(1)}, bf16[352,2048]{1,0:T(8,128)(2,1)S(1)}, u32[]{:S(2)}, u32[]{:S(2)}) collective-permute-start(bf16[352,2048]{1,0:T(8,128)(2,1)S(1)} %slice.460), channel_id=1, source_target_pairs={{0,16},{16,0},{1,17},{17,1},{2,18},{18,2},{3,19},{19,3},{4,20},{20... | collective-permute-start | bytes 4325384 | tf_op jit(solution)/shard_map/ppermute | solution.py:152
  803.6 62.7 %collective-permute-start.39 = (bf16[352,2048]{1,0:T(8,128)(2,1)S(1)}, bf16[352,2048]{1,0:T(8,128)(2,1)S(1)}, u32[]{:S(2)}, u32[]{:S(2)}) collective-permute-start(bf16[352,2048]{1,0:T(8,128)(2,1)S(1)} %slice.462), channel_id=1, source_target_pairs={{0,16},{16,0},{1,17},{17,1},{2,18},{18,2},{3,19},{19,3},{4,20},{20... | collective-permute-start | bytes 4325384 | tf_op jit(solution)/shard_map/ppermute | solution.py:152
  810.3 86.9 %collective-permute-start.43 = (bf16[352,2048]{1,0:T(8,128)(2,1)S(1)}, bf16[352,2048]{1,0:T(8,128)(2,1)S(1)}, u32[]{:S(2)}, u32[]{:S(2)}) collective-permute-start(bf16[352,2048]{1,0:T(8,128)(2,1)S(1)} %slice.464), channel_id=1, source_target_pairs={{0,16},{16,0},{1,17},{17,1},{2,18},{18,2},{3,19},{19,3},{4,20},{20... | collective-permute-start | bytes 4325384 | tf_op jit(solution)/shard_map/ppermute | solution.py:152
  866.4 42.5 %collective-permute-start.40 = (bf16[352,2048]{1,0:T(8,128)(2,1)S(1)}, bf16[352,2048]{1,0:T(8,128)(2,1)S(1)}, u32[]{:S(2)}, u32[]{:S(2)}) collective-permute-start(bf16[352,2048]{1,0:T(8,128)(2,1)S(1)} %slice_add_fusion.1), channel_id=1, source_target_pairs={{4,0},{8,12},{5,1},{9,13},{6,2},{10,14},{7,3},{11,15},{20,16},{24,... | collective-permute-start | bytes 4325384 | tf_op jit(solution)/shard_map/ppermute | solution.py:170
  870.7 59.3 %collective-permute-start.36 = (bf16[352,2048]{1,0:T(8,128)(2,1)S(1)}, bf16[352,2048]{1,0:T(8,128)(2,1)S(1)}, u32[]{:S(2)}, u32[]{:S(2)}) collective-permute-start(bf16[352,2048]{1,0:T(8,128)(2,1)S(1)} %slice_add_fusion.2), channel_id=1, source_target_pairs={{4,0},{8,12},{5,1},{9,13},{6,2},{10,14},{7,3},{11,15},{20,16},{24,... | collective-permute-start | bytes 4325384 | tf_op jit(solution)/shard_map/ppermute | solution.py:170
  897.4 48.1 %collective-permute-start.44 = (bf16[352,2048]{1,0:T(8,128)(2,1)S(1)}, bf16[352,2048]{1,0:T(8,128)(2,1)S(1)}, u32[]{:S(2)}, u32[]{:S(2)}) collective-permute-start(bf16[352,2048]{1,0:T(8,128)(2,1)S(1)} %slice_add_fusion), channel_id=1, source_target_pairs={{4,0},{8,12},{5,1},{9,13},{6,2},{10,14},{7,3},{11,15},{20,16},{24,... | collective-permute-start | bytes 4325384 | tf_op jit(solution)/shard_map/ppermute | solution.py:170
  952.5 41.2 %collective-permute-start.38 = (bf16[352,2048]{1,0:T(8,128)(2,1)S(1)}, bf16[352,2048]{1,0:T(8,128)(2,1)}, u32[]{:S(2)}, u32[]{:S(2)}) collective-permute-start(bf16[352,2048]{1,0:T(8,128)(2,1)S(1)} %broadcast_select_fusion.2), channel_id=1, source_target_pairs={{0,16},{16,0},{1,17},{17,1},{2,18},{18,2},{3,19},{19,3},{4,20},{20... | collective-permute-start | bytes 4325384 | tf_op jit(solution)/shard_map/ppermute | solution.py:152
  974.7 49.9 %collective-permute-start.46 = (bf16[352,2048]{1,0:T(8,128)(2,1)S(1)}, bf16[352,2048]{1,0:T(8,128)(2,1)}, u32[]{:S(2)}, u32[]{:S(2)}) collective-permute-start(bf16[352,2048]{1,0:T(8,128)(2,1)S(1)} %broadcast_select_fusion), channel_id=1, source_target_pairs={{0,16},{16,0},{1,17},{17,1},{2,18},{18,2},{3,19},{19,3},{4,20},{20... | collective-permute-start | bytes 4325384 | tf_op jit(solution)/shard_map/ppermute | solution.py:152
  1032.6 133.1 %collective-permute-start.31 = (bf16[128,2048]{1,0:T(8,128)(2,1)}, bf16[128,2048]{1,0:T(8,128)(2,1)}, u32[]{:S(2)}, u32[]{:S(2)}) collective-permute-start(bf16[128,2048]{1,0:T(8,128)(2,1)} %slice.457), channel_id=1, source_target_pairs={{0,16},{16,0},{1,17},{17,1},{2,18},{18,2},{3,19},{19,3},{4,20},{20... | collective-permute-start | bytes 1572872 | tf_op jit(solution)/shard_map/ppermute | solution.py:152
  1039.5 121.5 %collective-permute-start.27 = (bf16[2048,128]{0,1:T(8,128)(2,1)S(1)}, bf16[2048,128]{0,1:T(8,128)(2,1)S(1)}, u32[]{:S(2)}, u32[]{:S(2)}) collective-permute-start(bf16[2048,128]{0,1:T(8,128)(2,1)S(1)} %slice.455), channel_id=1, source_target_pairs={{0,16},{16,0},{1,17},{17,1},{2,18},{18,2},{3,19},{19,3},{4,20},{20... | collective-permute-start | bytes 1572872 | tf_op jit(solution)/shard_map/ppermute | solution.py:152
  1048.4 111.3 %collective-permute-start.19 = (bf16[16,2048]{1,0:T(8,128)(2,1)S(1)}, bf16[16,2048]{1,0:T(8,128)(2,1)S(1)}, u32[]{:S(2)}, u32[]{:S(2)}) collective-permute-start(bf16[16,2048]{1,0:T(8,128)(2,1)S(1)} %get-tuple-element.165), channel_id=1, source_target_pairs={{0,16},{16,0},{1,17},{17,1},{2,18},{18,2},{3,19},{19,3},{4,20},{20... | collective-permute-start | bytes 196616 | tf_op jit(solution)/shard_map/ppermute | solution.py:152
  1204.2 44.5 %collective-permute-start.16 = (bf16[256,2048]{1,0:T(8,128)(2,1)}, bf16[256,2048]{1,0:T(8,128)(2,1)}, u32[]{:S(2)}, u32[]{:S(2)}) collective-permute-start(bf16[256,2048]{1,0:T(8,128)(2,1)} %get-tuple-element.157), channel_id=1, source_target_pairs={{0,0},{4,8},{8,4},{12,12},{1,1},{5,9},{9,5},{13,13},{2,2},{6,10},{... | collective-permute-start | bytes 3145736 | tf_op jit(solution)/shard_map/ppermute | solution.py:149
  (130 other events, 2774.6 us)
Sparse Core Ops, SparseCore 0:
  40.7 59.7 all-gather.6
  142.8 169.7 reduce-scatter.4
  314.2 80.5 all-gather.10
  396.2 56.3 all-gather.8
  499.8 166.0 reduce-scatter.8
  672.1 47.2 all-gather.12
  771.0 166.2 reduce-scatter.10
  939.6 170.9 reduce-scatter.6

commit v2 on v1

--- a/solution.py
+++ b/solution.py
@@ -9,6 +9,7 @@
 EPS = 1e-05
 
 ALL_AXES = ("y", "k", "h", "l", "x")
+FLIP = [(0, 1), (1, 0)]
 SQUARE = ("k", "l", "x")
 
 
@@ -142,8 +143,15 @@
     return (grad_query_rows, grad_keys.astype(jnp.bfloat16), grad_values.astype(jnp.bfloat16))
 
 
+def after(value, *others):
+    return lax.optimization_barrier((value, *others))[0]
+
+
 def make_body(y_size):
     y_pairs = [(i, i ^ 1) for i in range(y_size)]
+    owner_y_pairs = [
+        (i * 4 + kh, (i ^ 1) * 4 + kh) for i in range(y_size) for kh in (0, 3)
+    ]
 
     def trade(values):
         return lax.ppermute(values, ("k", "h"), [(0, 0), (1, 2), (2, 1), (3, 3)])
@@ -151,39 +159,64 @@
     def over_y(values):
         return lax.ppermute(values, "y", y_pairs)
 
-    def fetch_shard(own, axis):
+    def my_half(own, axis=0):
         half = own.shape[axis] // 2
-        mine = lax.dynamic_slice_in_dim(own, (lax.axis_index("y") % 2) * half, half, axis)
-        got = trade(mine)
-        other = over_y(got)
-        return jnp.concatenate([got, other], axis=axis)
-
-    def reduce_grad(part, axis):
-        half = part.shape[axis] // 2
-        mine = lax.slice_in_dim(part, 0, half, axis=axis)
-        other = lax.slice_in_dim(part, half, 2 * half, axis=axis)
-        total = mine + over_y(other)
+        return lax.dynamic_slice_in_dim(own, (lax.axis_index("y") % 2) * half, half, axis)
+
+    def scatter(lhs, product):
+        k, l, x = (lax.axis_index(name) for name in SQUARE)
+        blocks = lhs.reshape(2, 4, lhs.shape[0] // 8, lhs.shape[1])
+        rows = lhs.shape[0] // 8
+        half = rows // 2
+        for_twin = lax.dynamic_index_in_dim(blocks, 1 - k, 0, keepdims=False)
+        for_twin = product(for_twin.reshape(4 * rows, -1)).astype(jnp.bfloat16)
+        from_twin = lax.ppermute(for_twin, "k", FLIP).reshape(4, rows, -1)
+        mine = lax.dynamic_index_in_dim(blocks, k, 0, keepdims=False)
+
+        def block(dl, dx):
+            index = (l ^ dl) * 2 + (x ^ dx)
+            part = product(lax.dynamic_index_in_dim(mine, index, 0, keepdims=False))
+            return part + lax.dynamic_index_in_dim(from_twin, index, 0, keepdims=False)
+
+        diagonal = block(1, 1).astype(jnp.bfloat16)
+        along_x = block(0, 1)
+        along_l = block(1, 0)
+        got_top = lax.ppermute(diagonal[:half], "x", FLIP)
+        got_bottom = lax.ppermute(diagonal[half:], "l", FLIP)
+        x_top = lax.ppermute(along_x[:half].astype(jnp.bfloat16), "x", FLIP)
+        l_bottom = lax.ppermute(along_l[half:].astype(jnp.bfloat16), "l", FLIP)
+        own = block(0, 0)
+        x_bottom = lax.ppermute((along_x[half:] + got_bottom).astype(jnp.bfloat16), "x", FLIP)
+        l_top = lax.ppermute((along_l[:half] + got_top).astype(jnp.bfloat16), "l", FLIP)
+        top = own[:half] + x_top + l_top
+        bottom = own[half:] + x_bottom + l_bottom
+        return jnp.concatenate([top, bottom], axis=0)
+
+    def reduce_grad(other, mine_product):
+        total = (mine_product() + over_y(other)).astype(jnp.bfloat16)
+        y_total = total
         step = 2
         while step < y_size:
             total = total + lax.ppermute(total, "y", [(i, i ^ step) for i in range(y_size)])
             step *= 2
-        arrived = lax.ppermute(total, ("k", "h"), [(1, 0), (2, 3)])
-        total = total + arrived
-        twin = lax.ppermute(total, ("k", "h"), [(0, 2), (3, 1)])
-        mine = jnp.where(lax.axis_index("k") == lax.axis_index("h"), total, twin)
-        other = over_y(mine)
+        total = total + lax.ppermute(total, ("k", "h"), [(1, 0), (2, 3)])
+        back = lax.ppermute(total, ("y", "k", "h"), owner_y_pairs)
+        to_twin = [(0, 2), (3, 1)]
+        owner = lax.axis_index("k") == lax.axis_index("h")
+        mine = jnp.where(owner, total, lax.ppermute(total, ("k", "h"), to_twin))
+        theirs = jnp.where(owner, back, lax.ppermute(back, ("k", "h"), to_twin))
+        return y_total, mine, theirs
+
+    def in_order(mine, theirs, axis=0):
         first = lax.axis_index("y") % 2 == 0
         return jnp.where(
             first,
-            jnp.concatenate([mine, other], axis=axis),
-            jnp.concatenate([other, mine], axis=axis),
+            jnp.concatenate([mine, theirs], axis=axis),
+            jnp.concatenate([theirs, mine], axis=axis),
         ).astype(jnp.float32)
 
     def gather(rows):
         return lax.all_gather(rows, SQUARE, axis=0, tiled=True)
-
-    def scatter(parts):
-        return lax.psum_scatter(parts, SQUARE, scatter_dimension=0, tiled=True)
 
     def body(
         tokens,
@@ -199,104 +232,154 @@
         doc_ids,
         cotangent,
     ):
+        own_tokens = trade(tokens)
         doc_row = trade(doc_ids)[0]
-        own_tokens = trade(tokens)
         inputs = own_tokens.astype(jnp.float32)
-        own_grad = trade(cotangent)
-        wq = fetch_shard(w_query.T, 0)
-        wk = fetch_shard(w_key.T, 0)
-        wv = fetch_shard(w_value, 1)
-        wo = fetch_shard(w_out, 0)
-        wg = fetch_shard(w_gate.T, 0)
-        wu = fetch_shard(w_up.T, 0)
-        wd = fetch_shard(w_down, 0)
-        heads_here = wq.shape[0] // FEAT
-        wqk = jnp.concatenate([wq, wk], axis=0)
-
+        qkv_mine = trade(
+            jnp.concatenate([my_half(w_value, 1).T, my_half(w_query.T), my_half(w_key.T)], axis=0)
+        )
+        qkv_other = over_y(qkv_mine)
+        wide = qkv_mine.shape[0] - 2 * FEAT
+        w_qkv = jnp.concatenate(
+            [qkv_mine[:wide], qkv_other[:wide], qkv_mine[wide:], qkv_other[wide:]], axis=0
+        )
         normed_one, scale_one, low_one = norm_rows(inputs, gain_one)
         gathered_one = gather(low_one)
+
+        wo_half, gate_half, up_half, down_half, cotangent_in = lax.optimization_barrier(
+            (
+                my_half(w_out),
+                my_half(w_gate.T),
+                my_half(w_up.T),
+                my_half(w_down),
+                cotangent,
+                own_tokens,
+                qkv_mine,
+            )
+        )[:5]
+        wo_mine = trade(wo_half)
+        own_grad = trade(cotangent_in)
+        down_mine = trade(down_half)
+        gate_mine = trade(gate_half)
+        up_mine = trade(up_half)
+
+        def whole(mine):
+            return jnp.concatenate([mine, over_y(mine)], axis=0)
+
+        wo = whole(wo_mine)
+        wd = whole(down_mine)
+        wg = whole(gate_mine)
+        wu = whole(up_mine)
+
         group_rows = gathered_one.shape[0]
         block_rows = min(512, group_rows)
-        qk_flat = dot_nt(gathered_one, wqk).astype(jnp.bfloat16)
-        value_flat = dot_nn(gathered_one, wv).astype(jnp.bfloat16)
-        width = heads_here * FEAT
-        query_rows = qk_flat[:, :width].reshape(group_rows, heads_here, FEAT)
-        key_row_block = qk_flat[:, width:].reshape(group_rows, heads_here, FEAT)
-        value_rows = value_flat.reshape(group_rows, heads_here, HEAD_V)
+        qkv = dot_nt(gathered_one, w_qkv).astype(jnp.bfloat16)
+        value_rows = qkv[:, : 2 * HEAD_V].reshape(group_rows, 2, HEAD_V)
+        small = qkv[:, 2 * HEAD_V :].reshape(group_rows, 2, 2, FEAT)
+        query_rows = small[:, :, 0]
+        key_row_block = small[:, :, 1]
         mixed_blocks, denoms = attention_forward(
             query_rows, key_row_block, value_rows, doc_row, block_rows
         )
-        mixed_heads = mixed_blocks.reshape(group_rows, heads_here * HEAD_V)
-        attn_out = scatter(dot_nn(mixed_heads, wo).astype(jnp.bfloat16)).astype(jnp.float32)
+        mixed_heads = mixed_blocks.reshape(group_rows, 2 * HEAD_V)
+        grad_rows = gather(own_grad)
+        attn_out = scatter(mixed_heads, lambda rows: dot_nn(rows, wo))
         residual = inputs + attn_out
         normed_two, scale_two, low_two = norm_rows(residual, gain_two)
-        grad_rows = gather(own_grad)
         gathered_two = gather(low_two)
+        grad_hidden = dot_nt(grad_rows, wd)
         gate_pre = dot_nt(gathered_two, wg)
         upward = dot_nt(gathered_two, wu)
         sigmoid_gate = jax.nn.sigmoid(gate_pre)
         hidden = (gate_pre * sigmoid_gate * upward).astype(jnp.bfloat16)
-        grad_hidden = dot_nt(grad_rows, wd)
         slope_gate = sigmoid_gate * (1.0 + gate_pre * (1.0 - sigmoid_gate))
         grad_gate_act = (grad_hidden * upward * slope_gate).astype(jnp.bfloat16)
         grad_upward = (grad_hidden * (gate_pre * sigmoid_gate)).astype(jnp.bfloat16)
+        width = grad_upward.shape[1]
+
         grad_normed_two = scatter(
-            (dot_nn(grad_gate_act, wg) + dot_nn(grad_upward, wu)).astype(jnp.bfloat16)
-        ).astype(jnp.float32)
-        grad_gate_w = dot_tn(grad_gate_act, gathered_two).astype(jnp.bfloat16)
-        grad_up_w = dot_tn(grad_upward, gathered_two).astype(jnp.bfloat16)
-        grad_down_w = dot_tn(hidden, grad_rows).astype(jnp.bfloat16)
-        ffn_out = scatter(dot_nn(hidden, wd).astype(jnp.bfloat16)).astype(jnp.float32)
-        block_out = trade((residual + ffn_out).astype(jnp.bfloat16))
+            jnp.concatenate([grad_gate_act, grad_upward], axis=1),
+            lambda rows: dot_nn(rows[:, :width], wg) + dot_nn(rows[:, width:], wu),
+        )
+        grads = {}
+        half = width // 2
+        for name, acts, rows in (
+            ("gate", grad_gate_act, gathered_two),
+            ("up", grad_upward, gathered_two),
+            ("down", hidden, grad_rows),
+        ):
+            grads[name] = reduce_grad(
+                dot_tn(acts[:, half:], rows).astype(jnp.bfloat16),
+                lambda acts=acts, rows=rows: dot_tn(acts[:, :half], rows),
+            )[1:]
 
         gain_two_part = jnp.sum(grad_normed_two * normed_two, axis=0)
         grad_resid = own_grad.astype(jnp.float32) + norm_back(
             grad_normed_two, normed_two, scale_two, gain_two
         )
         grad_attn_rows = gather(grad_resid.astype(jnp.bfloat16))
+        ffn_out = scatter(hidden, lambda rows: dot_nn(rows, wd))
+        block_out = trade((residual + ffn_out).astype(jnp.bfloat16))
         grad_mixed = dot_nt(grad_attn_rows, wo).astype(jnp.bfloat16)
-        grad_out_w = dot_tn(mixed_heads, grad_attn_rows).astype(jnp.bfloat16)
+        grads["out"] = reduce_grad(
+            dot_tn(mixed_heads[:, HEAD_V:], grad_attn_rows).astype(jnp.bfloat16),
+            lambda: dot_tn(mixed_heads[:, :HEAD_V], grad_attn_rows),
+        )[1:]
         grad_query_rows, grad_key_rows, grad_value_rows = attention_backward(
             query_rows,
             key_row_block,
             value_rows,
             doc_row,
             denoms,
-            grad_mixed.reshape(group_rows, heads_here, HEAD_V),
+            grad_mixed.reshape(group_rows, 2, HEAD_V),
             block_rows,
         )
-        grad_qk_flat = jnp.concatenate(
-            [grad_query_rows.reshape(group_rows, -1), grad_key_rows.reshape(group_rows, -1)],
-            axis=1,
-        )
-        grad_value_flat = grad_value_rows.reshape(group_rows, heads_here * HEAD_V)
+        halves = [
+            jnp.concatenate(
+                [grad_value_rows[:, i], grad_query_rows[:, i], grad_key_rows[:, i]], axis=1
+            )
+            for i in (0, 1)
+        ]
         grad_normed_one = scatter(
-            (dot_nn(grad_qk_flat, wqk) + dot_nt(grad_value_flat, wv)).astype(jnp.bfloat16)
-        ).astype(jnp.float32)
-        grad_qk_w = dot_tn(grad_qk_flat, gathered_one)
-        grad_value_w = dot_tn(gathered_one, grad_value_flat)
+            jnp.concatenate(halves, axis=1),
+            lambda rows: dot_nn(rows[:, : rows.shape[1] // 2], qkv_mine)
+            + dot_nn(rows[:, rows.shape[1] // 2 :], qkv_other),
+        )
+        qkv_y, qkv_grad_mine, qkv_grad_other = reduce_grad(
+            dot_tn(halves[1], gathered_one).astype(jnp.bfloat16),
+            lambda: dot_tn(halves[0], gathered_one),
+        )
         gain_one_part = (
-            jnp.sum(grad_qk_w * wqk, axis=0) + jnp.sum(grad_value_w * wv, axis=1)
-        ) / gain_one
+            jnp.sum(qkv_y.astype(jnp.float32) * qkv_mine.astype(jnp.float32), axis=0) / gain_one
+        )
+        gain_grads = jnp.stack([gain_one_part, gain_two_part])
+        for name in ("k", "l", "x", "h"):
+            gain_grads = gain_grads + lax.ppermute(gain_grads, name, FLIP)
+        step = 1
+        while step < y_size:
+            gain_grads = gain_grads + lax.ppermute(
+                gain_grads, "y", [(i, i ^ step) for i in range(y_size)]
+            )
+            step *= 2
         grad_tokens = grad_resid + norm_back(grad_normed_one, normed_one, scale_one, gain_one)
         grad_tokens = trade(grad_tokens.astype(jnp.bfloat16)).astype(jnp.float32)
-        gain_parts = lax.all_gather(jnp.stack([gain_one_part, gain_two_part]), ALL_AXES)
-        gain_grads = jnp.sum(gain_parts, axis=0)
-        grad_qk_w = grad_qk_w.astype(jnp.bfloat16)
-        grad_query_w = reduce_grad(grad_qk_w[:width], 0)
-        grad_key_w = reduce_grad(grad_qk_w[width:], 0)
+        value_grad = in_order(qkv_grad_mine[:wide].T, qkv_grad_other[:wide].T, 1)
+        query_grad = in_order(
+            qkv_grad_mine[wide : wide + FEAT], qkv_grad_other[wide : wide + FEAT]
+        ).T
+        key_grad = in_order(qkv_grad_mine[wide + FEAT :], qkv_grad_other[wide + FEAT :]).T
         return (
             block_out,
             grad_tokens,
             gain_grads[0],
-            grad_query_w.T,
-            grad_key_w.T,
-            reduce_grad(grad_value_w.astype(jnp.bfloat16), 1),
-            reduce_grad(grad_out_w, 0),
+            query_grad,
+            key_grad,
+            value_grad,
+            in_order(*grads["out"]),
             gain_grads[1],
-            reduce_grad(grad_gate_w, 0).T,
-            reduce_grad(grad_up_w, 0).T,
-            reduce_grad(grad_down_w, 0),
+            in_order(*grads["gate"]).T,
+            in_order(*grads["up"]).T,
+            in_order(*grads["down"]),
         )
 
     return body

time: 1270 us -> 909 us (0.72)
  waiting for transfers between devices: 757 us -> 426 us
  blocking collectives: 110 us -> 0 us
  local copies, waits for them, and re-layouts: 26.7 us -> 109 us
  starting transfers between devices: 101 us -> 117 us
    reduce_scatter x4 -> x0, waiting for transfers between devices: 300 us -> none  [scatter(): return lax.psum_scatter(parts, SQUARE, scatter_dimension=0, tiled=True)]
    ppermute x14 -> x53, waiting for transfers between devices: 63.7 us -> 181 us  [the longest x5 37.1 us: reduce_grad(): mine = jnp.where(owner, total, lax.ppermute(total, ('k', 'h'), to_twin))]
    all_gather x1 -> x0, blocking collectives: 110 us -> none  [body(): lax.all_gather(jnp.stack([gain_one_part, gain_two_part]), ALL_AXES)]
    ppermute x21 -> x10, waiting for transfers between devices: 156 us -> 80.1 us  [over_y(): return lax.ppermute(values, 'y', y_pairs)]
    all_gather x4, waiting for transfers between devices: 52.4 us -> 3.94 us  [gather(): return lax.all_gather(rows, SQUARE, axis=0, tiled=True)]
    ppermute x14 -> x53, starting transfers between devices: 36.2 us -> 67.2 us  [the longest x5 14.5 us: reduce_grad(): total = total + lax.ppermute(total, ('k', 'h'), [(1, 0), (2, 3)])]
    dynamic_slice x7 -> x13, local copies, waits for them, and re-layouts: 4.1 us -> 32.8 us  [the longest x3 16.8 us: block(): part = product(lax.dynamic_index_in_dim(mine, index, 0, keepdims=False))]
    unnamed x209 -> x220, local copies, waits for them, and re-layouts: 16.9 us -> 42.6 us
  transfers between devices with their start and end apart: 55 -> 77, of which waited for: 28 -> 42; matrix products, arithmetic and copies ran while one was open for 10% -> 30% of each run, Pallas kernels for 0% -> 0%
where the time goes in v2:
time: 909 us; the launch traced here: 902 us
  waiting for transfers between devices  426 us (47%)
  matrix products  182 us (20%)
  starting transfers between devices  117 us (13%)
  local copies, waits for them, and re-layouts  109 us (12%)
  other arithmetic  52 us (6%)
  between operations  16.5 us (2%)
    ppermute x10, waiting for transfers between devices, trade(): return lax.ppermute(values, ('k', 'h'), [(0, 0), (1, 2), (2, 1), (3, 3)])  160 us
    ppermute x10, waiting for transfers between devices, over_y(): return lax.ppermute(values, 'y', y_pairs)  80.1 us
    dot_general x30, matrix products, dot_nn(): return jnp.dot(left_mat, right_mat, preferred_element_type=jnp.float32)  58.8 us
    dot_general x5, matrix products, dot_nt(): lax.dot_general(left_mat, right_mat, (((1,), (1,)), ((), ())), preferred_...  47.5 us
    unnamed x220, local copies, waits for them, and re-layouts  42.6 us
    ppermute x10, starting transfers between devices, trade(): return lax.ppermute(values, ('k', 'h'), [(0, 0), (1, 2), (2, 1), (3, 3)])  38.9 us
    dot_general x10, matrix products, dot_tn(): lax.dot_general(left_mat, right_mat, (((0,), (0,)), ((), ())), preferred_...  37.4 us
    ppermute x5, waiting for transfers between devices, reduce_grad(): mine = jnp.where(owner, total, lax.ppermute(total, ('k', 'h'), to_twin))  37.1 us
  transfers between devices with their start and end apart: 77, of which 42 were waited for; matrix products, arithmetic and copies ran while one was open for 30% of the time, Pallas kernels for 0%

profile of v2, /device:TPU:1, one launch (start us, length us, event | category | flops | bytes accessed | tf_op | source)
XLA Modules:
  0.0 901.6 jit_solution(17141495329557424418)
XLA Ops:
  13.1 23.9 %collective-permute-done = bf16[256,2048]{1,0:T(8,128)(2,1)S(1)} collective-permute-done((bf16[256,2048]{1,0:T(8,128)(2,1)}, bf16[256,2048]{1,0:T(8,128)(2,1)S(1)}, u32[]{:S(2)}, u32[]{:S(2)}) %collective-permute-start) | collective-permute-done | bytes 1048608 | tf_op jit(solution)/shard_map/ppermute | solution.py:157
  75.8 9.4 %collective-permute-done.4 = bf16[128,2048]{1,0:T(8,128)(2,1)S(1)} collective-permute-done((bf16[128,2048]{1,0:T(8,128)(2,1)}, bf16[128,2048]{1,0:T(8,128)(2,1)S(1)}, u32[]{:S(2)}, u32[]{:S(2)}) %collective-permute-start.4) | collective-permute-done | bytes 524320 | tf_op jit(solution)/shard_map/ppermute | solution.py:157
  93.6 12.4 %collective-permute-done.27 = bf16[256,2048]{1,0:T(8,128)(2,1)S(1)} collective-permute-done((bf16[256,2048]{1,0:T(8,128)(2,1)}, bf16[256,2048]{1,0:T(8,128)(2,1)S(1)}, u32[]{:S(2)}, u32[]{:S(2)}) %collective-permute-start.27) | collective-permute-done | bytes 1048608 | tf_op jit(solution)/shard_map/ppermute | solution.py:157
  172.5 10.0 %collective-permute-done.8 = bf16[128,2048]{1,0:T(8,128)(2,1)S(1)} collective-permute-done((bf16[128,2048]{1,0:T(8,128)(2,1)S(1)}, bf16[128,2048]{1,0:T(8,128)(2,1)S(1)}, u32[]{:S(2)}, u32[]{:S(2)}) %collective-permute-start.8) | collective-permute-done | bytes 524320 | tf_op jit(solution)/shard_map/ppermute | solution.py:184
  211.9 29.3 %collective-permute-done.15 = bf16[352,2048]{1,0:T(8,128)(2,1)S(1)} collective-permute-done((bf16[352,2048]{1,0:T(8,128)(2,1)}, bf16[352,2048]{1,0:T(8,128)(2,1)S(1)}, u32[]{:S(2)}, u32[]{:S(2)}) %collective-permute-start.15) | collective-permute-done | bytes 1441824 | tf_op jit(solution)/shard_map/ppermute | solution.py:157
  242.4 22.9 %collective-permute-done.17 = bf16[352,2048]{1,0:T(8,128)(2,1)S(1)} collective-permute-done((bf16[352,2048]{1,0:T(8,128)(2,1)}, bf16[352,2048]{1,0:T(8,128)(2,1)S(1)}, u32[]{:S(2)}, u32[]{:S(2)}) %collective-permute-start.17) | collective-permute-done | bytes 1441824 | tf_op jit(solution)/shard_map/ppermute | solution.py:157
  266.6 32.8 %collective-permute-done.13 = bf16[352,2048]{1,0:T(8,128)(2,1)S(1)} collective-permute-done((bf16[352,2048]{1,0:T(8,128)(2,1)}, bf16[352,2048]{1,0:T(8,128)(2,1)S(1)}, u32[]{:S(2)}, u32[]{:S(2)}) %collective-permute-start.13) | collective-permute-done | bytes 1441824 | tf_op jit(solution)/shard_map/ppermute | solution.py:157
  303.7 13.5 %collective-permute-done.14 = bf16[352,2048]{1,0:T(8,128)(2,1)S(1)} collective-permute-done((bf16[352,2048]{1,0:T(8,128)(2,1)S(1)}, bf16[352,2048]{1,0:T(8,128)(2,1)S(1)}, u32[]{:S(2)}, u32[]{:S(2)}) %collective-permute-start.14) | collective-permute-done | bytes 1441824 | tf_op jit(solution)/shard_map/ppermute | solution.py:160
  318.4 10.1 %fusion.191 = f32[2048,704]{0,1:T(8,128)} fusion(bf16[2048,2048]{1,0:T(8,128)(2,1)} %all-gather.9.cloned.1.call-done, bf16[704,2048]{1,0:T(8,128)(2,1)S(1)} %constant_dynamic-update-slice_fusion.6), kind=kOutput, calls=%fused_computation.380 | convolution fusion | flops 5905580032 | bytes 17039360 | tf_op jit(solution)/shard_map/dot_general | solution.py:39
  328.6 11.2 %fusion.190 = f32[2048,704]{0,1:T(8,128)} fusion(bf16[2048,2048]{1,0:T(8,128)(2,1)} %all-gather.7.cloned.1.call-done, bf16[704,2048]{1,0:T(8,128)(2,1)} %copy-done.2), kind=kOutput, calls=%fused_computation.379 | convolution fusion | flops 5905580032 | bytes 17039360 | tf_op jit(solution)/shard_map/dot_general | solution.py:39
  339.7 13.6 %multiply_convert_fusion.1 = (bf16[2048,704]{0,1:T(8,128)(2,1)}, bf16[2048,704]{0,1:T(8,128)(2,1)}, bf16[2048,704]{0,1:T(8,128)(2,1)}) fusion(f32[2048,704]{0,1:T(8,128)S(1)} %copy-done.79, f32[2048,704]{0,1:T(8,128)} %fusion.190, bf16[2048,2048]{1,0:T(8,128)(2,1)S(1)} %copy-done.71, bf16[704,2048]{1,0:T(8,128)(2,1)} %constant_dynamic-update-slice_fusion.2), kind=kOutput, calls=%fused_computation.10 | convolution fusion | flops 5927206912 | bytes 31457280 | tf_op jit(solution)/shard_map/dot_general | solution.py:39
  371.3 10.5 %reshape.660 = bf16[2,4,256,1408]{2,1,0,3:T(4,128)(2,1)} reshape(bf16[2048,1408]{0,1:T(8,128)(2,1)} %pad_maximum_fusion) | data formatting | bytes 11534336 | tf_op jit(solution)/shard_map/reshape | solution.py:168
  465.9 10.9 %collective-permute-done.30 = bf16[128,2048]{1,0:T(8,128)(2,1)S(1)} collective-permute-done((bf16[128,2048]{1,0:T(8,128)(2,1)S(1)}, bf16[128,2048]{1,0:T(8,128)(2,1)S(1)}, u32[]{:S(2)}, u32[]{:S(2)}) %collective-permute-start.30) | collective-permute-done | bytes 524320 | tf_op jit(solution)/shard_map/ppermute | solution.py:184
  490.2 9.4 %collective-permute-done.20 = bf16[128,2048]{1,0:T(8,128)(2,1)S(1)} collective-permute-done((bf16[128,2048]{1,0:T(8,128)(2,1)S(1)}, bf16[128,2048]{1,0:T(8,128)(2,1)S(1)}, u32[]{:S(2)}, u32[]{:S(2)}) %collective-permute-start.20) | collective-permute-done | bytes 524320 | tf_op jit(solution)/shard_map/ppermute | solution.py:186
  500.1 10.6 %collective-permute-done.24 = bf16[128,2048]{1,0:T(8,128)(2,1)S(1)} collective-permute-done((bf16[128,2048]{1,0:T(8,128)(2,1)S(1)}, bf16[128,2048]{1,0:T(8,128)(2,1)S(1)}, u32[]{:S(2)}, u32[]{:S(2)}) %collective-permute-start.24) | collective-permute-done | bytes 524320 | tf_op jit(solution)/shard_map/ppermute | solution.py:189
  535.9 16.1 %collective-permute-done.68 = bf16[352,2048]{1,0:T(8,128)(2,1)S(1)} collective-permute-done((bf16[352,2048]{1,0:T(8,128)(2,1)S(1)}, bf16[352,2048]{1,0:T(8,128)(2,1)S(1)}, u32[]{:S(2)}, u32[]{:S(2)}) %collective-permute-start.68) | collective-permute-done | bytes 1441824 | tf_op jit(solution)/shard_map/ppermute | solution.py:160
  559.6 23.2 %collective-permute-done.63 = bf16[352,2048]{1,0:T(8,128)(2,1)S(1)} collective-permute-done((bf16[352,2048]{1,0:T(8,128)(2,1)S(1)}, bf16[352,2048]{1,0:T(8,128)(2,1)S(1)}, u32[]{:S(2)}, u32[]{:S(2)}) %collective-permute-start.63) | collective-permute-done | bytes 1441824 | tf_op jit(solution)/shard_map/ppermute | solution.py:160
  590.0 23.7 %collective-permute-done.58 = bf16[352,2048]{1,0:T(8,128)(2,1)S(1)} collective-permute-done((bf16[352,2048]{1,0:T(8,128)(2,1)S(1)}, bf16[352,2048]{1,0:T(8,128)(2,1)S(1)}, u32[]{:S(2)}, u32[]{:S(2)}) %collective-permute-start.58) | collective-permute-done | bytes 1441824 | tf_op jit(solution)/shard_map/ppermute | solution.py:160
  626.9 9.9 %collective-permute-done.59 = bf16[352,2048]{1,0:T(8,128)(2,1)S(1)} collective-permute-done((bf16[352,2048]{1,0:T(8,128)(2,1)S(1)}, bf16[352,2048]{1,0:T(8,128)(2,1)S(1)}, u32[]{:S(2)}, u32[]{:S(2)}) %collective-permute-start.59) | collective-permute-done | bytes 1441824 | tf_op jit(solution)/shard_map/ppermute | solution.py:202
  649.3 22.2 %collective-permute-done.65 = bf16[352,2048]{1,0:T(8,128)(2,1)} collective-permute-done((bf16[352,2048]{1,0:T(8,128)(2,1)S(1)}, bf16[352,2048]{1,0:T(8,128)(2,1)}, u32[]{:S(2)}, u32[]{:S(2)}) %collective-permute-start.65) | collective-permute-done | bytes 1441824 | tf_op jit(solution)/shard_map/ppermute | solution.py:206
  769.3 15.3 %collective-permute-done.47 = f32[2,2048]{1,0:T(2,128)S(1)} collective-permute-done((f32[2,2048]{1,0:T(2,128)S(1)}, f32[2,2048]{1,0:T(2,128)S(1)}, u32[]{:S(2)}, u32[]{:S(2)}) %collective-permute-start.47) | collective-permute-done | bytes 16416 | tf_op jit(solution)/shard_map/ppermute | solution.py:357
  834.6 10.9 %collective-permute-done.37 = bf16[128,2048]{1,0:T(8,128)(2,1)S(1)} collective-permute-done((bf16[128,2048]{1,0:T(8,128)(2,1)S(1)}, bf16[128,2048]{1,0:T(8,128)(2,1)S(1)}, u32[]{:S(2)}, u32[]{:S(2)}) %collective-permute-start.37) | collective-permute-done | bytes 524320 | tf_op jit(solution)/shard_map/ppermute | solution.py:184
  847.4 9.3 %collective-permute-done.40 = bf16[128,2048]{1,0:T(8,128)(2,1)S(1)} collective-permute-done((bf16[128,2048]{1,0:T(8,128)(2,1)S(1)}, bf16[128,2048]{1,0:T(8,128)(2,1)S(1)}, u32[]{:S(2)}, u32[]{:S(2)}) %collective-permute-start.40) | collective-permute-done | bytes 524320 | tf_op jit(solution)/shard_map/ppermute | solution.py:189
  869.6 20.1 %collective-permute-done.42 = bf16[256,2048]{1,0:T(8,128)(2,1)} collective-permute-done((bf16[256,2048]{1,0:T(8,128)(2,1)}, bf16[256,2048]{1,0:T(8,128)(2,1)}, u32[]{:S(2)}, u32[]{:S(2)}) %collective-permute-start.42) | collective-permute-done | bytes 1048608 | tf_op jit(solution)/shard_map/ppermute | solution.py:157
  (565 shorter events, 503.8 us)
Async XLA Ops:
  7.2 104.4 %all-gather.5.cloned.1.call-start = ((), (), s32[]{:S(2)}) async-start(), calls=%async_computation | async-start | bytes 9437184 | tf_op jit(solution)/shard_map/all_gather | solution.py:219
  40.6 277.8 %all-gather.9.cloned.1.call-start = ((), (), s32[]{:S(2)}) async-start(), calls=%async_computation.2 | async-start | bytes 9437184 | tf_op jit(solution)/shard_map/all_gather | solution.py:219
  70.9 35.1 %collective-permute-start.27 = (bf16[256,2048]{1,0:T(8,128)(2,1)}, bf16[256,2048]{1,0:T(8,128)(2,1)S(1)}, u32[]{:S(2)}, u32[]{:S(2)}) collective-permute-start(bf16[256,2048]{1,0:T(8,128)(2,1)} %param.43), channel_id=1, source_target_pairs={{0,0},{4,8},{8,4},{12,12},{1,1},{5,9},{9,5},{13,13},{2,2},{6,10},{... | collective-permute-start | bytes 3145736 | tf_op jit(solution)/shard_map/ppermute | solution.py:157
  107.1 221.4 %all-gather.7.cloned.1.call-start = ((), (), s32[]{:S(2)}) async-start(), calls=%async_computation.1 | async-start | bytes 9437184 | tf_op jit(solution)/shard_map/all_gather | solution.py:219
  197.7 499.5 %all-gather.11.cloned.1.call-start = ((), (), s32[]{:S(2)}) async-start(), calls=%async_computation.3 | async-start | bytes 9437184 | tf_op jit(solution)/shard_map/all_gather | solution.py:219
  197.7 43.5 %collective-permute-start.15 = (bf16[352,2048]{1,0:T(8,128)(2,1)}, bf16[352,2048]{1,0:T(8,128)(2,1)S(1)}, u32[]{:S(2)}, u32[]{:S(2)}) collective-permute-start(bf16[352,2048]{1,0:T(8,128)(2,1)} %get-tuple-element.130), channel_id=1, source_target_pairs={{0,0},{4,8},{8,4},{12,12},{1,1},{5,9},{9,5},{13,13},{2,2},{6,10},{... | collective-permute-start | bytes 4325384 | tf_op jit(solution)/shard_map/ppermute | solution.py:157
  205.2 60.0 %collective-permute-start.17 = (bf16[352,2048]{1,0:T(8,128)(2,1)}, bf16[352,2048]{1,0:T(8,128)(2,1)S(1)}, u32[]{:S(2)}, u32[]{:S(2)}) collective-permute-start(bf16[352,2048]{1,0:T(8,128)(2,1)} %constant_dynamic-slice_fusion.15), channel_id=1, source_target_pairs={{0,0},{4,8},{8,4},{12,12},{1,1},{5,9},{9,5},{13,13},{2,2},{6,10},{... | collective-permute-start | bytes 4325384 | tf_op jit(solution)/shard_map/ppermute | solution.py:157
  207.2 92.2 %collective-permute-start.13 = (bf16[352,2048]{1,0:T(8,128)(2,1)}, bf16[352,2048]{1,0:T(8,128)(2,1)S(1)}, u32[]{:S(2)}, u32[]{:S(2)}) collective-permute-start(bf16[352,2048]{1,0:T(8,128)(2,1)} %get-tuple-element.129), channel_id=1, source_target_pairs={{0,0},{4,8},{8,4},{12,12},{1,1},{5,9},{9,5},{13,13},{2,2},{6,10},{... | collective-permute-start | bytes 4325384 | tf_op jit(solution)/shard_map/ppermute | solution.py:157
  241.2 60.9 %collective-permute-start.16 = (bf16[352,2048]{1,0:T(8,128)(2,1)S(1)}, bf16[352,2048]{1,0:T(8,128)(2,1)S(1)}, u32[]{:S(2)}, u32[]{:S(2)}) collective-permute-start(bf16[352,2048]{1,0:T(8,128)(2,1)S(1)} %collective-permute-done.15), channel_id=1, source_target_pairs={{0,16},{16,0},{1,17},{17,1},{2,18},{18,2},{3,19},{19,3},{4,20},{20... | collective-permute-start | bytes 4325384 | tf_op jit(solution)/shard_map/ppermute | solution.py:160
  265.2 37.0 %collective-permute-start.18 = (bf16[352,2048]{1,0:T(8,128)(2,1)S(1)}, bf16[352,2048]{1,0:T(8,128)(2,1)S(1)}, u32[]{:S(2)}, u32[]{:S(2)}) collective-permute-start(bf16[352,2048]{1,0:T(8,128)(2,1)S(1)} %collective-permute-done.17), channel_id=1, source_target_pairs={{0,16},{16,0},{1,17},{17,1},{2,18},{18,2},{3,19},{19,3},{4,20},{20... | collective-permute-start | bytes 4325384 | tf_op jit(solution)/shard_map/ppermute | solution.py:160
  368.1 66.7 %collective-permute-start.19 = (bf16[1024,2048]{1,0:T(8,128)(2,1)}, bf16[1024,2048]{1,0:T(8,128)(2,1)}, u32[]{:S(2)}, u32[]{:S(2)}) collective-permute-start(bf16[1024,2048]{1,0:T(8,128)(2,1)} %convolution_convert_fusion), channel_id=1, source_target_pairs={{0,8},{8,0},{1,9},{9,1},{2,10},{10,2},{3,11},{11,3},{4,12},{12,4},... | collective-permute-start | bytes 12582920 | tf_op jit(solution)/shard_map/ppermute | solution.py:173
  397.5 47.3 %collective-permute-start.28 = (bf16[1024,2048]{1,0:T(8,128)(2,1)}, bf16[1024,2048]{1,0:T(8,128)(2,1)}, u32[]{:S(2)}, u32[]{:S(2)}) collective-permute-start(bf16[1024,2048]{1,0:T(8,128)(2,1)} %add_convert_fusion.1), channel_id=1, source_target_pairs={{0,8},{8,0},{1,9},{9,1},{2,10},{10,2},{3,11},{11,3},{4,12},{12,4},... | collective-permute-start | bytes 12582920 | tf_op jit(solution)/shard_map/ppermute | solution.py:173
  437.2 40.5 %collective-permute-start.23 = (bf16[128,2048]{1,0:T(8,128)(2,1)S(1)}, bf16[128,2048]{1,0:T(8,128)(2,1)S(1)}, u32[]{:S(2)}, u32[]{:S(2)}) collective-permute-start(bf16[128,2048]{1,0:T(8,128)(2,1)S(1)} %get-tuple-element.213), channel_id=1, source_target_pairs={{0,2},{2,0},{1,3},{3,1},{4,6},{6,4},{5,7},{7,5},{8,10},{10,8},{9,1... | collective-permute-start | bytes 1572872 | tf_op jit(solution)/shard_map/ppermute | solution.py:185
  439.6 38.6 %collective-permute-start.21 = (bf16[128,2048]{1,0:T(8,128)(2,1)S(1)}, bf16[128,2048]{1,0:T(8,128)(2,1)S(1)}, u32[]{:S(2)}, u32[]{:S(2)}) collective-permute-start(bf16[128,2048]{1,0:T(8,128)(2,1)S(1)} %get-tuple-element.212), channel_id=1, source_target_pairs={{0,1},{1,0},{2,3},{3,2},{4,5},{5,4},{6,7},{7,6},{8,9},{9,8},{10,11... | collective-permute-start | bytes 1572872 | tf_op jit(solution)/shard_map/ppermute | solution.py:184
  531.1 51.7 %collective-permute-start.63 = (bf16[352,2048]{1,0:T(8,128)(2,1)S(1)}, bf16[352,2048]{1,0:T(8,128)(2,1)S(1)}, u32[]{:S(2)}, u32[]{:S(2)}) collective-permute-start(bf16[352,2048]{1,0:T(8,128)(2,1)S(1)} %convolution_convert_fusion.3), channel_id=1, source_target_pairs={{0,16},{16,0},{1,17},{17,1},{2,18},{18,2},{3,19},{19,3},{4,20},{20... | collective-permute-start | bytes 4325384 | tf_op jit(solution)/shard_map/ppermute | solution.py:160
  534.4 79.3 %collective-permute-start.58 = (bf16[352,2048]{1,0:T(8,128)(2,1)S(1)}, bf16[352,2048]{1,0:T(8,128)(2,1)S(1)}, u32[]{:S(2)}, u32[]{:S(2)}) collective-permute-start(bf16[352,2048]{1,0:T(8,128)(2,1)S(1)} %convolution_convert_fusion.4), channel_id=1, source_target_pairs={{0,16},{16,0},{1,17},{17,1},{2,18},{18,2},{3,19},{19,3},{4,20},{20... | collective-permute-start | bytes 4325384 | tf_op jit(solution)/shard_map/ppermute | solution.py:160
  555.7 65.2 %collective-permute-start.69 = (bf16[352,2048]{1,0:T(8,128)(2,1)S(1)}, bf16[352,2048]{1,0:T(8,128)(2,1)S(1)}, u32[]{:S(2)}, u32[]{:S(2)}) collective-permute-start(bf16[352,2048]{1,0:T(8,128)(2,1)S(1)} %add_convert_fusion.2), channel_id=1, source_target_pairs={{4,0},{8,12},{5,1},{9,13},{6,2},{10,14},{7,3},{11,15},{20,16},{24,... | collective-permute-start | bytes 4325384 | tf_op jit(solution)/shard_map/ppermute | solution.py:202
  586.0 38.5 %collective-permute-start.64 = (bf16[352,2048]{1,0:T(8,128)(2,1)S(1)}, bf16[352,2048]{1,0:T(8,128)(2,1)S(1)}, u32[]{:S(2)}, u32[]{:S(2)}) collective-permute-start(bf16[352,2048]{1,0:T(8,128)(2,1)S(1)} %add_convert_fusion.3), channel_id=1, source_target_pairs={{4,0},{8,12},{5,1},{9,13},{6,2},{10,14},{7,3},{11,15},{20,16},{24,... | collective-permute-start | bytes 4325384 | tf_op jit(solution)/shard_map/ppermute | solution.py:202
  642.5 32.7 %collective-permute-start.60 = (bf16[352,2048]{1,0:T(8,128)(2,1)}, bf16[352,2048]{1,0:T(8,128)(2,1)}, u32[]{:S(2)}, u32[]{:S(2)}) collective-permute-start(bf16[352,2048]{1,0:T(8,128)(2,1)} %add.671), channel_id=1, source_target_pairs={{0,8},{12,4},{1,9},{13,5},{2,10},{14,6},{3,11},{15,7},{16,24},{28,... | collective-permute-start | bytes 4325384 | tf_op jit(solution)/shard_map/ppermute | solution.py:206
  643.9 35.3 %collective-permute-start.72 = (bf16[352,2048]{1,0:T(8,128)(2,1)}, bf16[352,2048]{1,0:T(8,128)(2,1)S(1)}, u32[]{:S(2)}, u32[]{:S(2)}) collective-permute-start(bf16[352,2048]{1,0:T(8,128)(2,1)} %collective-permute-done.71), channel_id=1, source_target_pairs={{0,8},{12,4},{1,9},{13,5},{2,10},{14,6},{3,11},{15,7},{16,24},{28,... | collective-permute-start | bytes 4325384 | tf_op jit(solution)/shard_map/ppermute | solution.py:207
  645.2 37.7 %collective-permute-start.67 = (bf16[352,2048]{1,0:T(8,128)(2,1)}, bf16[352,2048]{1,0:T(8,128)(2,1)S(1)}, u32[]{:S(2)}, u32[]{:S(2)}) collective-permute-start(bf16[352,2048]{1,0:T(8,128)(2,1)} %collective-permute-done.66), channel_id=1, source_target_pairs={{0,8},{12,4},{1,9},{13,5},{2,10},{14,6},{3,11},{15,7},{16,24},{28,... | collective-permute-start | bytes 4325384 | tf_op jit(solution)/shard_map/ppermute | solution.py:207
  646.5 42.9 %collective-permute-start.62 = (bf16[352,2048]{1,0:T(8,128)(2,1)}, bf16[352,2048]{1,0:T(8,128)(2,1)S(1)}, u32[]{:S(2)}, u32[]{:S(2)}) collective-permute-start(bf16[352,2048]{1,0:T(8,128)(2,1)} %collective-permute-done.61), channel_id=1, source_target_pairs={{0,8},{12,4},{1,9},{13,5},{2,10},{14,6},{3,11},{15,7},{16,24},{28,... | collective-permute-start | bytes 4325384 | tf_op jit(solution)/shard_map/ppermute | solution.py:207
  709.4 51.6 %collective-permute-start.53 = (bf16[128,2048]{1,0:T(8,128)(2,1)S(1)}, bf16[128,2048]{1,0:T(8,128)(2,1)}, u32[]{:S(2)}, u32[]{:S(2)}) collective-permute-start(bf16[128,2048]{1,0:T(8,128)(2,1)S(1)} %convolution_convert_fusion.8), channel_id=1, source_target_pairs={{0,16},{16,0},{1,17},{17,1},{2,18},{18,2},{3,19},{19,3},{4,20},{20... | collective-permute-start | bytes 1572872 | tf_op jit(solution)/shard_map/ppermute | solution.py:160
  746.0 73.6 %collective-permute-start.35 = (bf16[1024,2048]{1,0:T(8,128)(2,1)S(1)}, bf16[1024,2048]{1,0:T(8,128)(2,1)S(1)}, u32[]{:S(2)}, u32[]{:S(2)}) collective-permute-start(bf16[1024,2048]{1,0:T(8,128)(2,1)S(1)} %add_convert_fusion), channel_id=1, source_target_pairs={{0,8},{8,0},{1,9},{9,1},{2,10},{10,2},{3,11},{11,3},{4,12},{12,4},... | collective-permute-start | bytes 12582920 | tf_op jit(solution)/shard_map/ppermute | solution.py:173
  (151 other events, 1845.8 us)
Sparse Core Ops, SparseCore 0:
  40.8 70.8 all-gather.4
  113.2 48.3 all-gather.8
  197.8 83.0 all-gather.6
  514.9 50.3 all-gather.10

commit v3 on v1

v3 whole, which is shorter than its diff:
```python
import functools

import jax
import jax.numpy as jnp
from jax import lax
from jax.experimental import pallas as pl
from jax.experimental.pallas import tpu as pltpu
from jax.sharding import Mesh
from jax.sharding import PartitionSpec as P

FEAT = 16
HEAD_V = 128
EPS = 1e-05
VALUES = 2 * HEAD_V
FEATS = 2 * FEAT
NO_COST = pl.CostEstimate(flops=1, bytes_accessed=1, transcendentals=0)

ALL_AXES = ("y", "k", "h", "l", "x")
FLIP = [(0, 1), (1, 0)]
SQUARE = ("k", "l", "x")


def norm_rows(values, gain_vec):
    row_scale = lax.rsqrt(jnp.mean(values * values, axis=-1, keepdims=True) + EPS)
    normed = values * row_scale
    return (normed, row_scale, (normed * gain_vec).astype(jnp.bfloat16))


def norm_back(grad_normed, normed, row_scale, gain_vec):
    weighted = grad_normed * gain_vec
    inner_mean = jnp.mean(weighted * normed, axis=-1, keepdims=True)
    return row_scale * (weighted - normed * inner_mean)


def dot_nn(left_mat, right_mat):
    return jnp.dot(left_mat, right_mat, preferred_element_type=jnp.float32)


def dot_tn(left_mat, right_mat):
    return lax.dot_general(
        left_mat, right_mat, (((0,), (0,)), ((), ())), preferred_element_type=jnp.float32
    )


def dot_nt(left_mat, right_mat):
    return lax.dot_general(
        left_mat, right_mat, (((1,), (1,)), ((), ())), preferred_element_type=jnp.float32
    )


def head_lanes(values, head):
    lane = lax.broadcasted_iota(jnp.int32, values.shape, 1)
    return jnp.where((lane >= head * FEAT) & (lane < (head + 1) * FEAT), values, jnp.zeros_like(values))

def scores(query, keys, ends_ref, i, j, block):
    score = dot_nt(query, keys) * 0.25
    t = i * block + lax.broadcasted_iota(jnp.int32, score.shape, 0)
    u = j * block + lax.broadcasted_iota(jnp.int32, score.shape, 1)
    ends = ends_ref[:, pl.ds(pl.multiple_of(j * block, block), block)]
    allowed = (t >= u) & (t <= ends)
    return score, allowed, jnp.where(allowed, 1.0 + score + 0.5 * score * score, 0.0)

def forward_kernel(
    first_ref,
    twin_at_ref,
    own_at_ref,
    is_own_ref,
    twin_ref,
    own_ref,
    weight_ref,
    ends_ref,
    qkv_ref,
    mixed_ref,
    ratio_ref,
    denom_ref,
    key_ref,
    numer_ref,
    sum_ref,
):
    i = pl.program_id(0)
    block = own_ref.shape[0]
    here = pl.ds(pl.multiple_of(i * block, block), block)

    def project(rows_ref):
        qkv_ref[here] = dot_nt(rows_ref[...], weight_ref[...]).astype(jnp.bfloat16)

    pl.when(is_own_ref[i] == 1)(lambda: project(own_ref))
    pl.when(is_own_ref[i] == 0)(lambda: project(twin_ref))
    key_ref[here] = qkv_ref[here, VALUES + FEATS :]
    query = qkv_ref[here, VALUES : VALUES + FEATS]
    own = [head_lanes(query, head) for head in range(2)]
    numer_ref[...] = jnp.zeros_like(numer_ref)
    sum_ref[...] = jnp.zeros_like(sum_ref)

    def step(j, carry):
        there = pl.ds(pl.multiple_of(j * block, block), block)
        for head in range(2):
            columns = pl.ds(head * HEAD_V, HEAD_V)
            _, _, kernel = scores(own[head], key_ref[there], ends_ref, i, j, block)
            folded = kernel[:, :128]
            for c in range(1, block // 128):
                folded = folded + kernel[:, c * 128 : (c + 1) * 128]
            sum_ref[:, pl.ds(head * 128, 128)] += folded
            numer_ref[:, columns] += dot_nn(kernel.astype(jnp.bfloat16), qkv_ref[there, columns])
        return carry

    lax.fori_loop(first_ref[i], i + 1, step, 0)
    for head in range(2):
        columns = pl.ds(head * HEAD_V, HEAD_V)
        denom = jnp.sum(sum_ref[:, pl.ds(head * 128, 128)], axis=1, keepdims=True)
        ratio = numer_ref[:, columns] / denom
        mixed_ref[:, columns] = ratio.astype(jnp.bfloat16)
        ratio_ref[:, columns] = ratio
        denom_ref[:, columns] = jnp.broadcast_to(denom, ratio.shape)

def attention_rows(first, places, ends, twin, own, weight):
    half_rows, model = own.shape
    group_rows = 2 * half_rows
    block = group_rows // 8
    width = VALUES + 2 * FEATS

    def by_rows(columns):
        return pl.BlockSpec((block, columns), lambda i, *_: (i, 0))

    def whole(shape):
        return pl.BlockSpec(shape, lambda i, *_: (0, 0))

    return pl.pallas_call(
        forward_kernel,
        out_shape=[
            jax.ShapeDtypeStruct((group_rows, width), jnp.bfloat16),
            jax.ShapeDtypeStruct((group_rows, VALUES), jnp.bfloat16),
            jax.ShapeDtypeStruct((group_rows, VALUES), jnp.float32),
            jax.ShapeDtypeStruct((group_rows, VALUES), jnp.float32),
        ],
        grid_spec=pltpu.PrefetchScalarGridSpec(
            num_scalar_prefetch=4,
            grid=(8,),
            in_specs=[
                pl.BlockSpec((block, model), lambda i, f, twin_at, own_at, s: (twin_at[i], 0)),
                pl.BlockSpec((block, model), lambda i, f, twin_at, own_at, s: (own_at[i], 0)),
                whole((width, model)),
                whole((1, group_rows)),
            ],
            out_specs=[
                whole((group_rows, width)),
                by_rows(VALUES),
                by_rows(VALUES),
                by_rows(VALUES),
            ],
            scratch_shapes=[
                pltpu.VMEM((group_rows, FEATS), jnp.bfloat16),
                pltpu.VMEM((block, VALUES), jnp.float32),
                pltpu.VMEM((block, 256), jnp.float32),
            ],
        ),
        compiler_params=pltpu.CompilerParams(vmem_limit_bytes=32 << 20),
        cost_estimate=NO_COST,
        name="attention_rows",
    )(first, *places, twin, own, weight, ends)


def backward_kernel(
    first_ref,
    place_ref,
    attn_ref,
    weight_ref,
    qkv_ref,
    ratio_ref,
    denom_ref,
    ends_ref,
    grad_ref,
    key_ref,
    key_sum,
    value_sum,
    query_sum,
):
    i = pl.program_id(0)
    block = attn_ref.shape[0]
    here = pl.ds(pl.multiple_of(i * block, block), block)
    @pl.when(i == 0)
    def _():
        key_ref[...] = qkv_ref[:, VALUES + FEATS:]
        key_sum[...] = jnp.zeros_like(key_sum)
        value_sum[...] = jnp.zeros_like(value_sum)
    mixed_grad = dot_nt(attn_ref[...], weight_ref[...]).astype(jnp.bfloat16).astype(jnp.float32)
    query = qkv_ref[here, VALUES : VALUES + FEATS]
    own = [head_lanes(query, head) for head in range(2)]
    numer_grads, denom_grads = [], []
    for head in range(2):
        columns = pl.ds(head * HEAD_V, HEAD_V)
        grad = mixed_grad[:, head * HEAD_V : (head + 1) * HEAD_V]
        denom = denom_ref[:, columns]
        numer_grads.append((grad / denom).astype(jnp.bfloat16))
        denom_grads.append(-jnp.sum(grad * ratio_ref[:, columns], axis=1, keepdims=True) / denom[:, :1])
    query_sum[...] = jnp.zeros_like(query_sum)

    def step(j, carry):
        there = pl.ds(pl.multiple_of(j * block, block), block)
        keys = key_ref[there]
        key_grads = None
        for head in range(2):
            columns = pl.ds(head * HEAD_V, HEAD_V)
            score, allowed, kernel = scores(own[head], keys, ends_ref, i, j, block)
            kernel_grad = dot_nt(numer_grads[head], qkv_ref[there, columns]) + denom_grads[head]
            score_grad = jnp.where(allowed, kernel_grad * (1.0 + score), 0.0).astype(jnp.bfloat16)
            query_sum[:, pl.ds(head * 128, FEATS)] += dot_nn(score_grad, keys)
            key_grad = dot_tn(score_grad, own[head])
            key_grads = key_grad if key_grads is None else key_grads + key_grad
            value_sum[there, columns] += dot_tn(kernel.astype(jnp.bfloat16), numer_grads[head])
        key_sum[there] += key_grads
        return carry

    lax.fori_loop(first_ref[i], i + 1, step, 0)
    totals = [query_sum[:, pl.ds(head * 128, FEATS)] for head in range(2)]
    query_grad = (head_lanes(totals[0], 0) + head_lanes(totals[1], 1)) * 0.25
    placed = pl.ds(pl.multiple_of(place_ref[i] * block, block), block)
    grad_ref[placed, VALUES : VALUES + FEATS] = query_grad.astype(jnp.bfloat16)

    @pl.when(i == pl.num_programs(0) - 1)
    def _():
        def store(j, carry):
            there = pl.ds(pl.multiple_of(j * block, block), block)
            placed = pl.ds(pl.multiple_of(place_ref[j] * block, block), block)
            grad_ref[placed, :VALUES] = value_sum[there].astype(jnp.bfloat16)
            grad_ref[placed, VALUES + FEATS :] = (key_sum[there] * 0.25).astype(jnp.bfloat16)
            return carry

        lax.fori_loop(0, pl.num_programs(0), store, 0)

def attention_back(first, place, ends, attn_rows, weight, qkv, ratio, denom):
    group_rows, model = attn_rows.shape
    block = group_rows // 8
    width = VALUES + 2 * FEATS

    def by_rows(columns):
        return pl.BlockSpec((block, columns), lambda i, *_: (i, 0))

    def whole(shape):
        return pl.BlockSpec(shape, lambda i, *_: (0, 0))

    return pl.pallas_call(
        backward_kernel,
        out_shape=jax.ShapeDtypeStruct((group_rows, width), jnp.bfloat16),
        grid_spec=pltpu.PrefetchScalarGridSpec(
            num_scalar_prefetch=2,
            grid=(8,),
            in_specs=[
                by_rows(model),
                whole((VALUES, model)),
                whole((group_rows, width)),
                by_rows(VALUES),
                by_rows(VALUES),
                whole((1, group_rows)),
            ],
            out_specs=whole((group_rows, width)),
            scratch_shapes=[
                pltpu.VMEM((group_rows, FEATS), jnp.bfloat16),
                pltpu.VMEM((group_rows, FEATS), jnp.float32),
                pltpu.VMEM((group_rows, VALUES), jnp.float32),
                pltpu.VMEM((block, 256), jnp.float32),
            ],
        ),
        compiler_params=pltpu.CompilerParams(vmem_limit_bytes=40 << 20),
        cost_estimate=NO_COST,
        name="attention_back",
    )(first, place, attn_rows, weight, qkv, ratio, denom, ends)


def bounds(doc_row):
    group_rows = doc_row.shape[0]; block = group_rows // 8
    ends = jnp.sum(doc_row[:, None] <= doc_row[None, :], axis=0, dtype=jnp.int32) - 1
    starts = block * jnp.arange(8, dtype=jnp.int32)
    first = jnp.sum(ends[block - 1 :: block][None, :] < starts[:, None], axis=1, dtype=jnp.int32)
    return first, ends.reshape(1, group_rows)


def ffn_kernel(pieces, order_ref, rows_ref, grad_ref, *refs):
    weights = refs[:4]
    act_grad_ref, hidden_ref, part_ref, held, sems = refs[-5:]

    @pl.when(pl.program_id(0) == 0)
    def _():
        copies = [
            pltpu.make_async_copy(ref, held.at[pl.ds(i * pieces, pieces)], sems.at[i])
            for i, ref in enumerate(weights)
        ]
        for copy in copies:
            copy.start()
        for copy in copies:
            copy.wait()

    rows = rows_ref[...]
    for half in range(2):
        at = 2 * half * pieces
        gate = dot_nt(held[pl.ds(at, pieces)], rows)
        up = dot_nt(held[pl.ds(at + pieces, pieces)], rows)
        grad = grad_ref[pl.ds(half * pieces, pieces)]
        sigmoid = jax.nn.sigmoid(gate)
        act = gate * sigmoid
        hidden_ref[pl.ds(half * pieces, pieces)] = (act * up).astype(jnp.bfloat16)
        act_grad_ref[pl.ds(at, pieces)] = (
            grad * up * (sigmoid * (1.0 + gate * (1.0 - sigmoid)))
        ).astype(jnp.bfloat16)
        act_grad_ref[pl.ds(at + pieces, pieces)] = (grad * act).astype(jnp.bfloat16)
    part_ref[...] = dot_tn(act_grad_ref[...], held[...]).astype(jnp.bfloat16)


def ffn_rows(order, rows, grad_hidden, weights, earlier=()):
    group_rows, model = rows.shape
    pieces = weights[0].shape[0]
    block = group_rows // 8
    blocks = order.shape[0]
    anywhere = pl.BlockSpec(memory_space=pl.ANY)
    return pl.pallas_call(
        functools.partial(ffn_kernel, pieces),
        out_shape=[
            jax.ShapeDtypeStruct((4 * pieces, group_rows), jnp.bfloat16),
            jax.ShapeDtypeStruct((2 * pieces, group_rows), jnp.bfloat16),
            jax.ShapeDtypeStruct((blocks * block, model), jnp.bfloat16),
        ],
        grid_spec=pltpu.PrefetchScalarGridSpec(
            num_scalar_prefetch=1,
            grid=(blocks,),
            in_specs=[
                pl.BlockSpec((block, model), lambda i, o: (o[i], 0)),
                pl.BlockSpec((2 * pieces, block), lambda i, o: (0, o[i])),
                *[anywhere] * (4 + len(earlier)),
            ],
            out_specs=[
                pl.BlockSpec((4 * pieces, block), lambda i, o: (0, o[i])),
                pl.BlockSpec((2 * pieces, block), lambda i, o: (0, o[i])),
                pl.BlockSpec((block, model), lambda i, o: (i, 0)),
            ],
            scratch_shapes=[
                pltpu.VMEM((4 * pieces, model), jnp.bfloat16),
                pltpu.SemaphoreType.DMA((4,)),
            ],
        ),
        input_output_aliases={7 + i: i for i in range(len(earlier))},
        compiler_params=pltpu.CompilerParams(vmem_limit_bytes=44 << 20),
        cost_estimate=NO_COST,
        name="ffn_rows",
    )(order, rows, grad_hidden, *weights, *earlier)


def product_kernel(turned, order_ref, rows_ref, weight_ref, part_ref):
    product = dot_tn if turned else dot_nn
    part_ref[...] = product(rows_ref[...], weight_ref[...]).astype(jnp.bfloat16)


def product_rows(order, rows, weight, turned=False):
    group_rows = rows.shape[1 if turned else 0]
    depth, model = weight.shape
    block = group_rows // 8
    blocks = order.shape[0]
    if turned:
        rows_spec = pl.BlockSpec((depth, block), lambda i, o: (0, o[i]))
    else:
        rows_spec = pl.BlockSpec((block, depth), lambda i, o: (o[i], 0))
    return pl.pallas_call(
        functools.partial(product_kernel, turned),
        out_shape=jax.ShapeDtypeStruct((blocks * block, model), jnp.bfloat16),
        grid_spec=pltpu.PrefetchScalarGridSpec(
            num_scalar_prefetch=1,
            grid=(blocks,),
            in_specs=[rows_spec, pl.BlockSpec((depth, model), lambda i, o: (0, 0))],
            out_specs=pl.BlockSpec((block, model), lambda i, o: (i, 0)),
        ),
        compiler_params=pltpu.CompilerParams(vmem_limit_bytes=24 << 20),
        cost_estimate=NO_COST,
        name="product_rows",
    )(order, rows, weight)


def sync(*values):
    return lax.optimization_barrier(values)


def after(value, *others):
    return lax.optimization_barrier((value, *others))[0]


def make_body(y_size):
    y_pairs = [(i, i ^ 1) for i in range(y_size)]
    owner_y_pairs = [(i * 4 + kh, (i ^ 1) * 4 + kh) for i in range(y_size) for kh in (0, 3)]

    def trade(values):
        return lax.ppermute(values, ("k", "h"), [(0, 0), (1, 2), (2, 1), (3, 3)])

    def over_y(values):
        return lax.ppermute(values, "y", y_pairs)

    def over_h(values):
        return lax.ppermute(values, ("k", "h"), [(1, 0), (2, 3)])

    def over_owners(values):
        return lax.ppermute(values, ("y", "k", "h"), owner_y_pairs)

    def from_owner(values):
        twin = lax.ppermute(values, ("k", "h"), [(0, 2), (3, 1)])
        return jnp.where(lax.axis_index("k") == lax.axis_index("h"), values, twin)

    def all_y(total):
        step = 2
        while step < y_size:
            total = total + lax.ppermute(total, "y", [(i, i ^ step) for i in range(y_size)])
            step *= 2
        return total

    def my_half(own, axis=0):
        half = own.shape[axis] // 2
        return lax.dynamic_slice_in_dim(own, (lax.axis_index("y") % 2) * half, half, axis)

    def orders():
        k, l, x = (lax.axis_index(name) for name in SQUARE)
        chips = jnp.array([3, 1, 2, 0], jnp.int32) ^ (2 * l + x)
        return (chips + 4 * (1 - k), chips + 4 * k)

    def places():
        k, l, x = (lax.axis_index(name) for name in SQUARE)
        index = jnp.arange(8, dtype=jnp.int32)

        def slot(block):
            chip = (block % 4) ^ (2 * l + x)
            return jnp.where((chip == 0) | (chip == 3), 3 - chip, chip)

        first_twin = 4 * (1 - k)
        twin_at = slot(jnp.clip(index, first_twin, first_twin + 3))
        own_at = slot(jnp.clip(index, 4 * k, 4 * k + 3))
        is_own = (index // 4 == k).astype(jnp.int32)
        return (twin_at, own_at, is_own), slot(index) + 4 * is_own

    def low(*values):
        return jnp.concatenate(values, axis=0).astype(jnp.bfloat16)

    def scatter_first(mine, from_twin):
        rows = mine.shape[0] // 4
        half = rows // 2

        def chip(start, stop):
            return mine[start:stop].astype(jnp.float32) + from_twin[start:stop]

        first_x = low(chip(0, half), chip(rows, rows + half))
        first_l = low(chip(half, rows), chip(2 * rows + half, 3 * rows))
        rest = (
            chip(rows + half, 2 * rows),
            chip(2 * rows, 2 * rows + half),
            chip(3 * rows, 4 * rows),
        )
        return sync(first_x, first_l), rest

    def scatter_last(got_x, got_l, rest):
        half = got_x.shape[0] // 2
        return sync(low(rest[0] + got_l[:half]), low(rest[1] + got_x[:half]))

    def scatter_end(got_x, got_l, last_x, last_l, rest):
        half = got_x.shape[0] // 2
        own_top = rest[2][:half] + got_x[half:] + last_l
        own_bottom = rest[2][half:] + last_x + got_l[half:]
        return jnp.concatenate([own_top, own_bottom], axis=0)

    def flip(values, name):
        return lax.ppermute(values, name, FLIP)

    def in_order(mine, theirs, axis=0):
        first = lax.axis_index("y") % 2 == 0
        return jnp.where(
            first,
            jnp.concatenate([mine, theirs], axis=axis),
            jnp.concatenate([theirs, mine], axis=axis),
        ).astype(jnp.float32)

    def gather(rows):
        return lax.all_gather(rows, SQUARE, axis=0, tiled=True)

    def low_dot(left, right):
        return dot_nn(left, right).astype(jnp.bfloat16)

    def body(
        tokens,
        gain_one,
        w_query,
        w_key,
        w_value,
        w_out,
        gain_two,
        w_gate,
        w_up,
        w_down,
        doc_ids,
        cotangent,
    ):
        for_twin, for_own = orders()
        halves_at, place = places()
        stacked = jnp.arange(4, dtype=jnp.int32)
        qkv_size = HEAD_V + 2 * FEAT
        head_size = qkv_size + HEAD_V
        head_half = jnp.concatenate(
            [
                my_half(w_value, 1).T,
                my_half(w_query.T),
                my_half(w_key.T),
                my_half(w_out),
                jnp.broadcast_to(doc_ids.astype(jnp.bfloat16), (16, doc_ids.shape[1])),
            ],
            axis=0,
        )
        down_half, gate_half, up_half = my_half(w_down), my_half(w_gate.T), my_half(w_up.T)
        own_tokens = trade(tokens)
        own_tokens = after(own_tokens, head_half, down_half, gate_half, up_half)
        inputs = own_tokens.astype(jnp.float32)
        normed_one, scale_one, low_one = norm_rows(inputs, gain_one)

        head_mine = trade(after(head_half, low_one))
        from_x, from_l, head_mine = sync(flip(low_one, "x"), flip(low_one, "l"), head_mine)
        half = low_one.shape[0] // 2
        qkv_other = over_y(head_mine[:qkv_size])
        own_grad = trade(after(cotangent, head_mine))
        d_top = flip(from_l[:half], "x")
        d_bottom = flip(from_x[half:], "l")
        stack_own = jnp.concatenate([d_top, d_bottom, from_x, from_l, low_one], axis=0)
        stack_own, qkv_other = sync(stack_own, qkv_other)
        stack_twin = flip(stack_own, "k")
        wo_other = over_y(after(head_mine[qkv_size:head_size], qkv_other))
        first, ends = bounds(head_mine[head_size].astype(jnp.int32))
        w_qkv = jnp.concatenate(
            [
                head_mine[:HEAD_V],
                qkv_other[:HEAD_V],
                head_mine[HEAD_V : HEAD_V + FEAT],
                qkv_other[HEAD_V : HEAD_V + FEAT],
                head_mine[HEAD_V + FEAT : qkv_size],
                qkv_other[HEAD_V + FEAT : qkv_size],
            ],
            axis=0,
        )
        stack_twin, w_qkv, own_grad, first = sync(stack_twin, w_qkv, own_grad, first)

        grad_rows = gather(own_grad)
        down_mine = trade(after(down_half, own_grad))
        qkv, mixed_heads, ratio, denom = attention_rows(
            first, halves_at, ends, stack_twin, stack_own, w_qkv
        )
        wo = jnp.concatenate([head_mine[qkv_size:head_size], wo_other], axis=0)
        mixed_heads, down_mine, wo = sync(mixed_heads, down_mine, wo)

        from_twin = flip(product_rows(for_twin, mixed_heads, wo), "k")
        down_other = over_y(down_mine)
        gate_mine = trade(after(gate_half, down_mine))
        (first_x, first_l), rest = scatter_first(
            product_rows(for_own, mixed_heads, wo), from_twin
        )
        got_x, got_l, down_other, gate_mine = sync(
            flip(first_x, "x"), flip(first_l, "l"), down_other, gate_mine
        )
        to_x, to_l = scatter_last(got_x, got_l, rest)
        up_mine = trade(after(up_half, gate_mine))
        gate_other = over_y(gate_mine)
        attn_out = scatter_end(got_x, got_l, flip(to_x, "x"), flip(to_l, "l"), rest)

        residual = inputs + attn_out
        normed_two, scale_two, low_two = norm_rows(residual, gain_two)
        gathered_two = gather(low_two)
        wd = jnp.concatenate([down_mine, down_other], axis=0)
        grad_hidden = dot_nt(wd, after(grad_rows, up_mine, low_two))
        up_other = over_y(up_mine)
        gathered_two, up_other, gate_other, grad_hidden = sync(
            gathered_two, up_other, gate_other, grad_hidden
        )

        weights = (gate_mine, up_mine, gate_other, up_other)
        *acts, parts_twin = ffn_rows(for_twin, gathered_two, grad_hidden, weights)
        from_twin = flip(parts_twin, "k")
        act_grad, hidden, parts_own = ffn_rows(
            for_own, gathered_two, grad_hidden, weights, tuple(acts)
        )
        units = hidden.shape[0] // 2
        unit_acts = {
            "gate": (act_grad[:units], act_grad[2 * units : 3 * units]),
            "up": (act_grad[units : 2 * units], act_grad[3 * units :]),
            "down": (hidden[:units], hidden[units:]),
        }
        unit_rows = {"gate": gathered_two, "up": gathered_two, "down": grad_rows}

        def other_part(name, *deps):
            return low_dot(after(unit_acts[name][1], *deps), unit_rows[name])

        def y_total(name, arrived):
            return all_y((dot_nn(unit_acts[name][0], unit_rows[name]) + arrived).astype(jnp.bfloat16))

        (first_x, first_l), rest = scatter_first(parts_own, from_twin)
        down_part = other_part("down", first_x)
        down_y = over_y(down_part)
        gate_part = other_part("gate", down_part)
        up_part = other_part("up", gate_part)
        got_x, got_l, gate_part, up_part = sync(
            flip(first_x, "x"), flip(first_l, "l"), gate_part, up_part
        )
        to_x, to_l = scatter_last(got_x, got_l, rest)
        late_hidden = after(hidden, to_x)
        ffn_twin = product_rows(for_twin, late_hidden, wd, turned=True)
        ffn_own = product_rows(for_own, late_hidden, wd, turned=True)
        grad_normed_two = scatter_end(got_x, got_l, flip(to_x, "x"), flip(to_l, "l"), rest)
        grad_normed_two, down_y, ffn_twin, ffn_own = sync(
            grad_normed_two, down_y, ffn_twin, ffn_own
        )

        gate_y = over_y(gate_part)
        up_y = over_y(up_part)
        gain_two_part = jnp.sum(grad_normed_two * normed_two, axis=0)
        grad_resid = own_grad.astype(jnp.float32) + norm_back(
            grad_normed_two, normed_two, scale_two, gain_two
        )
        low_resid = grad_resid.astype(jnp.bfloat16)
        grad_attn_rows = gather(low_resid)
        down_total = y_total("down", after(down_y, low_resid))
        down_h = over_h(down_total)
        ffn_from_twin = flip(after(ffn_twin, low_resid), "k")
        (first_x, first_l), rest = scatter_first(ffn_own, ffn_from_twin)
        grad_attn_rows, gate_y, down_h, first_x, first_l = sync(
            grad_attn_rows, gate_y, down_h, first_x, first_l
        )

        gate_total = y_total("gate", gate_y)
        gate_h = over_h(gate_total)
        down_total = down_total + down_h
        down_back = over_owners(down_total)
        grad_qkv = attention_back(
            first, place, ends, after(grad_attn_rows, gate_total), wo, qkv, ratio, denom
        )
        grad_qkv, got_x, got_l, up_y, gate_h, down_back = sync(
            grad_qkv, flip(first_x, "x"), flip(first_l, "l"), up_y, gate_h, down_back
        )

        half_rows = stack_own.shape[0]
        to_x, to_l = scatter_last(got_x, got_l, rest)
        from_twin = flip(product_rows(stacked, grad_qkv, w_qkv), "k")
        one_own = product_rows(stacked + 4, grad_qkv, w_qkv)
        ffn_out = scatter_end(got_x, got_l, flip(to_x, "x"), flip(to_l, "l"), rest)
        (first_x, first_l), rest = scatter_first(one_own, from_twin)
        up_total = y_total("up", after(up_y, first_x))
        up_h = over_h(up_total)
        late_qkv = after(grad_qkv, up_total)
        qkv_part = dot_tn(late_qkv[:half_rows], stack_twin) + dot_tn(
            late_qkv[half_rows:], stack_own
        )
        out_part = dot_tn(after(mixed_heads, up_total), grad_attn_rows)

        def one_head(which):
            at_query = VALUES + which * FEAT
            return jnp.concatenate(
                [
                    qkv_part[which * HEAD_V : (which + 1) * HEAD_V],
                    qkv_part[at_query : at_query + FEAT],
                    qkv_part[at_query + FEATS : at_query + FEATS + FEAT],
                    out_part[which * HEAD_V : (which + 1) * HEAD_V],
                ],
                axis=0,
            )

        head_y = over_y(one_head(1).astype(jnp.bfloat16))
        block_out = trade((residual + ffn_out).astype(jnp.bfloat16))
        got_x, got_l, block_out = sync(flip(first_x, "x"), flip(first_l, "l"), block_out)
        to_x, to_l = scatter_last(got_x, got_l, rest)
        gate_total = gate_total + gate_h
        gate_back = over_owners(gate_total)
        grad_normed_one = scatter_end(got_x, got_l, flip(to_x, "x"), flip(to_l, "l"), rest)
        grad_normed_one, head_y, gate_back = sync(grad_normed_one, head_y, gate_back)

        grad_tokens = grad_resid + norm_back(grad_normed_one, normed_one, scale_one, gain_one)
        low_tokens = grad_tokens.astype(jnp.bfloat16)
        grad_tokens = trade(low_tokens).astype(jnp.float32)
        head_total = all_y((one_head(0) + head_y).astype(jnp.bfloat16))
        head_h = over_h(head_total)
        gain_one_part = jnp.sum(after(qkv_part, low_tokens) * w_qkv, axis=0) / gain_one
        gain_grads = jnp.stack([gain_one_part, gain_two_part])
        for name in ("k", "x", "l", "h"):
            gain_grads = gain_grads + flip(gain_grads, name)
        step = 1
        while step < y_size:
            gain_grads = gain_grads + lax.ppermute(
                gain_grads, "y", [(i, i ^ step) for i in range(y_size)]
            )
            step *= 2
        up_total = up_total + up_h
        up_back = over_owners(up_total)
        down_total, down_back = from_owner(down_total), from_owner(down_back)
        gate_total, gate_back = from_owner(gate_total), from_owner(gate_back)
        up_total = from_owner(up_total)
        head_total = head_total + head_h
        head_back = over_owners(head_total)
        head_total = from_owner(head_total)
        up_back = from_owner(up_back)
        head_back = from_owner(head_back)

        def head_grad(start, stop):
            return in_order(head_total[start:stop], head_back[start:stop])

        return (
            block_out,
            grad_tokens,
            gain_grads[0],
            head_grad(HEAD_V, HEAD_V + FEAT).T,
            head_grad(HEAD_V + FEAT, qkv_size).T,
            in_order(head_total[:HEAD_V].T, head_back[:HEAD_V].T, 1),
            head_grad(qkv_size, head_size),
            gain_grads[1],
            in_order(gate_total, gate_back).T,
            in_order(up_total, up_back).T,
            in_order(down_total, down_back),
        )

    return body


def solution(mesh):
    dp_size, tensor_size = mesh.devices.shape
    fine = Mesh(mesh.devices.reshape(dp_size // 2, 2, 2, 2, tensor_size // 4), ALL_AXES)
    rows = P(ALL_AXES, None)
    shard = ("h", "l", "x")
    in_specs = (
        rows,
        P(),
        P(None, shard),
        P(None, shard),
        P(None, shard),
        P(shard, None),
        P(),
        P(None, shard),
        P(None, shard),
        P(shard, None),
        P(("y", "k"), None),
        rows,
    )
    out_specs = (
        rows,
        rows,
        P(),
        P(None, shard),
        P(None, shard),
        P(None, shard),
        P(shard, None),
        P(),
        P(None, shard),
        P(None, shard),
        P(shard, None),
    )
    return jax.shard_map(
        make_body(dp_size // 2), mesh=fine, in_specs=in_specs, out_specs=out_specs, check_vma=False
    )
```

time: 1270 us -> 781 us (0.61)
  waiting for transfers between devices: 757 us -> 347 us
  matrix products: 185 us -> 57.7 us
  Pallas kernels: 0 us -> 110 us
  blocking collectives: 110 us -> 0 us
  starting transfers between devices: 101 us -> 129 us
  local copies, waits for them, and re-layouts: 26.7 us -> 48.1 us
    reduce_scatter x4 -> x0, waiting for transfers between devices: 300 us -> none  [scatter(): return lax.psum_scatter(parts, SQUARE, scatter_dimension=0, tiled=True)]
    ppermute x14 -> x46, waiting for transfers between devices: 63.7 us -> 208 us  [the longest x29 149 us: flip(): return lax.ppermute(values, name, FLIP)]
    ppermute x21 -> x9, waiting for transfers between devices: 156 us -> 38.7 us  [over_y(): return lax.ppermute(values, 'y', y_pairs)]
    all_gather x1 -> x0, blocking collectives: 110 us -> none  [body(): lax.all_gather(jnp.stack([gain_one_part, gain_two_part]), ALL_AXES)]
    pallas_call x0 -> x10, Pallas kernels: none -> 110 us  [the longest x2 40.3 us: ffn_rows(): pl.pallas_call(functools.partial(ffn_kernel, pieces), out_shape=[jax.Shap...]
    ppermute x12 -> x8, waiting for transfers between devices: 185 us -> 96.7 us  [trade(): return lax.ppermute(values, ('k', 'h'), [(0, 0), (1, 2), (2, 1), (3, 3)])]
    all_gather x4 -> x3, waiting for transfers between devices: 52.4 us -> 3.78 us  [gather(): return lax.all_gather(rows, SQUARE, axis=0, tiled=True)]
    dot_general x6 -> x1, matrix products: 54.9 us -> 10.5 us  [dot_nt(): lax.dot_general(left_mat, right_mat, (((1,), (1,)), ((), ())), preferred_...]
  transfers between devices with their start and end apart: 55 -> 66, of which waited for: 28 -> 30; matrix products, arithmetic and copies ran while one was open for 10% -> 17% of each run, Pallas kernels for 0% -> 11%
where the time goes in v3:
time: 781 us; the launch traced here: 768 us
  waiting for transfers between devices  347 us (44%)
  starting transfers between devices  129 us (17%)
  Pallas kernels  110 us (14%)
  other arithmetic  60.4 us (8%)
  matrix products  57.7 us (7%)
  local copies, waits for them, and re-layouts  48.1 us (6%)
  between operations  16 us (2%)
    ppermute x29, waiting for transfers between devices, flip(): return lax.ppermute(values, name, FLIP)  149 us
    ppermute x8, waiting for transfers between devices, trade(): return lax.ppermute(values, ('k', 'h'), [(0, 0), (1, 2), (2, 1), (3, 3)])  96.7 us
    ppermute x8, starting transfers between devices, trade(): return lax.ppermute(values, ('k', 'h'), [(0, 0), (1, 2), (2, 1), (3, 3)])  49 us
    pallas_call x2, Pallas kernels, ffn_rows(): pl.pallas_call(functools.partial(ffn_kernel, pieces), out_shape=[jax.Shap...  40.3 us
    ppermute x9, waiting for transfers between devices, over_y(): return lax.ppermute(values, 'y', y_pairs)  38.7 us
    dot_general x6, matrix products, dot_nn(): return jnp.dot(left_mat, right_mat, preferred_element_type=jnp.float32)  37.4 us
    unnamed x164, local copies, waits for them, and re-layouts  33.6 us
    ppermute x4, starting transfers between devices, over_h(): return lax.ppermute(values, ('k', 'h'), [(1, 0), (2, 3)])  31.8 us
  transfers between devices with their start and end apart: 66, of which 30 were waited for; matrix products, arithmetic and copies ran while one was open for 17% of the time, Pallas kernels for 11%

profile of v3, /device:TPU:1, one launch (start us, length us, event | category | flops | bytes accessed | tf_op | source)
XLA Modules:
  0.0 767.8 jit_solution(4960073084605381378)
XLA Ops:
  26.9 10.3 %collective-permute-done = bf16[256,2048]{1,0:T(8,128)(2,1)} collective-permute-done((bf16[256,2048]{1,0:T(8,128)(2,1)}, bf16[256,2048]{1,0:T(8,128)(2,1)}, u32[]{:S(2)}, u32[]{:S(2)}) %collective-permute-start) | collective-permute-done | bytes 1048608 | tf_op jit(solution)/shard_map/ppermute | solution.py:389
  47.2 14.0 %collective-permute-done.1 = bf16[256,2048]{1,0:T(8,128)(2,1)S(1)} collective-permute-done((bf16[256,2048]{1,0:T(8,128)(2,1)S(1)}, bf16[256,2048]{1,0:T(8,128)(2,1)S(1)}, u32[]{:S(2)}, u32[]{:S(2)}) %collective-permute-start.1) | collective-permute-done | bytes 1048608 | tf_op jit(solution)/shard_map/ppermute | solution.py:464
  61.2 20.1 %collective-permute-done.2 = bf16[256,2048]{1,0:T(8,128)(2,1)S(1)} collective-permute-done((bf16[256,2048]{1,0:T(8,128)(2,1)S(1)}, bf16[256,2048]{1,0:T(8,128)(2,1)S(1)}, u32[]{:S(2)}, u32[]{:S(2)}) %collective-permute-start.2) | collective-permute-done | bytes 1048608 | tf_op jit(solution)/shard_map/ppermute | solution.py:464
  106.0 18.8 %collective-permute-done.8 = bf16[256,2048]{1,0:T(8,128)(2,1)S(1)} collective-permute-done((bf16[256,2048]{1,0:T(8,128)(2,1)}, bf16[256,2048]{1,0:T(8,128)(2,1)S(1)}, u32[]{:S(2)}, u32[]{:S(2)}) %collective-permute-start.8) | collective-permute-done | bytes 1048608 | tf_op jit(solution)/shard_map/ppermute | solution.py:389
  137.1 21.8 %attention_rows.1 = (bf16[2048,320]{1,0:T(8,128)(2,1)S(1)}, bf16[2048,256]{1,0:T(8,128)(2,1)S(1)}, f32[2048,256]{1,0:T(8,128)S(1)}, f32[2048,256]{1,0:T(8,128)S(1)}) custom-call(s32[8]{0:T(128)S(1)} %convert_reduce_fusion.2.first_ref, s32[8]{0:T(128)S(1)} %get-tuple-element.272.twin_at_ref, s32[8]{0:T(128)S(1)} %get-tuple-element.271.own_at_ref, ...), custom_call_target="tpu_custom_call" | custom-call | flops 1 | bytes 1 | tf_op jit(solution)/shard_map/attention_rows/pallas_call | solution.py:128
  175.8 28.9 %collective-permute-done.15.refs_0_ = bf16[352,2048]{1,0:T(8,128)(2,1)S(1)} collective-permute-done((bf16[352,2048]{1,0:T(8,128)(2,1)S(1)}, bf16[352,2048]{1,0:T(8,128)(2,1)S(1)}, u32[]{:S(2)}, u32[]{:S(2)}) %collective-permute-start.15) | collective-permute-done | bytes 1441824 | tf_op jit(solution)/shard_map/ppermute | solution.py:389
  204.7 18.9 %collective-permute-done.13 = bf16[256,2048]{1,0:T(8,128)(2,1)S(1)} collective-permute-done((bf16[256,2048]{1,0:T(8,128)(2,1)S(1)}, bf16[256,2048]{1,0:T(8,128)(2,1)S(1)}, u32[]{:S(2)}, u32[]{:S(2)}) %collective-permute-start.13) | collective-permute-done | bytes 1048608 | tf_op jit(solution)/shard_map/ppermute | solution.py:464
  226.5 10.8 %collective-permute-done.16 = bf16[128,2048]{1,0:T(8,128)(2,1)S(1)} collective-permute-done((bf16[128,2048]{1,0:T(8,128)(2,1)S(1)}, bf16[128,2048]{1,0:T(8,128)(2,1)S(1)}, u32[]{:S(2)}, u32[]{:S(2)}) %collective-permute-start.16) | collective-permute-done | bytes 524320 | tf_op jit(solution)/shard_map/ppermute | solution.py:464
  251.5 35.0 %collective-permute-done.18.refs_1_ = bf16[352,2048]{1,0:T(8,128)(2,1)} collective-permute-done((bf16[352,2048]{1,0:T(8,128)(2,1)}, bf16[352,2048]{1,0:T(8,128)(2,1)}, u32[]{:S(2)}, u32[]{:S(2)}) %collective-permute-start.18) | collective-permute-done | bytes 1441824 | tf_op jit(solution)/shard_map/ppermute | solution.py:389
  287.5 10.5 %fusion.47.grad_ref = f32[704,2048]{1,0:T(8,128)} fusion(bf16[704,2048]{1,0:T(8,128)(2,1)S(1)} %constant_dynamic-update-slice_fusion.6.weight_ref, bf16[2048,2048]{1,0:T(8,128)(2,1)} %all-gather.6.cloned.1.call-done), kind=kOutput, calls=%fused_computation.187 | convolution fusion | flops 5905580032 | bytes 17039360 | tf_op jit(solution)/shard_map/dot_general | solution.py:46
  297.9 15.2 %collective-permute-done.19.refs_3_ = bf16[352,2048]{1,0:T(8,128)(2,1)} collective-permute-done((bf16[352,2048]{1,0:T(8,128)(2,1)}, bf16[352,2048]{1,0:T(8,128)(2,1)}, u32[]{:S(2)}, u32[]{:S(2)}) %collective-permute-start.19) | collective-permute-done | bytes 1441824 | tf_op jit(solution)/shard_map/ppermute | solution.py:392
  314.5 20.1 %ffn_rows.2 = (bf16[1408,2048]{1,0:T(8,128)(2,1)}, bf16[704,2048]{1,0:T(8,128)(2,1)S(1)}, bf16[1024,2048]{1,0:T(8,128)(2,1)}) custom-call(s32[4]{0:T(128)S(1)} %get-tuple-element.268.order_ref, bf16[2048,2048]{1,0:T(8,128)(2,1)} %all-gather.4.cloned.1.call-done.rows_ref, f32[704,2048]{1,0:T(8,128)} %fusion.47.grad_ref, bf16[352,2048]{1,0:T(8,128)(2,1)S(1)} %copy-done.14, ...), custom_call_target="tpu_custom_call" | custom-call | flops 1 | bytes 1 | tf_op jit(solution)/shard_map/ffn_rows/pallas_call | solution.py:315
  334.7 20.1 %ffn_rows.3 = (bf16[1408,2048]{1,0:T(8,128)(2,1)}, bf16[704,2048]{1,0:T(8,128)(2,1)S(1)}, bf16[1024,2048]{1,0:T(8,128)(2,1)}) custom-call(s32[4]{0:T(128)S(1)} %get-tuple-element.267.order_ref, bf16[2048,2048]{1,0:T(8,128)(2,1)} %all-gather.4.cloned.1.call-done.rows_ref, f32[704,2048]{1,0:T(8,128)} %fusion.47.grad_ref, ...), custom_call_target="tpu_custom_call", output_to_operand_aliasing={{0}: (7, {}), {1}: (8, {})} | custom-call | flops 1 | bytes 1 | tf_op jit(solution)/shard_map/ffn_rows/pallas_call | solution.py:315
  431.8 16.6 %collective-permute-done.27 = bf16[352,2048]{1,0:T(8,128)(2,1)} collective-permute-done((bf16[352,2048]{1,0:T(8,128)(2,1)}, bf16[352,2048]{1,0:T(8,128)(2,1)}, u32[]{:S(2)}, u32[]{:S(2)}) %collective-permute-start.27) | collective-permute-done | bytes 1441824 | tf_op jit(solution)/shard_map/ppermute | solution.py:392
  448.4 23.1 %collective-permute-done.28 = bf16[352,2048]{1,0:T(8,128)(2,1)} collective-permute-done((bf16[352,2048]{1,0:T(8,128)(2,1)S(1)}, bf16[352,2048]{1,0:T(8,128)(2,1)}, u32[]{:S(2)}, u32[]{:S(2)}) %collective-permute-start.28) | collective-permute-done | bytes 1441824 | tf_op jit(solution)/shard_map/ppermute | solution.py:395
  495.3 26.6 %attention_back.1.rows_ref = bf16[2048,320]{1,0:T(8,128)(2,1)S(1)} custom-call(s32[8]{0:T(128)S(1)} %convert_reduce_fusion.2.first_ref, s32[8]{0:T(128)S(1)} %fusion.29.place_ref, bf16[2048,2048]{1,0:T(8,128)(2,1)} %all-gather.8.cloned.1.call-done.attn_ref, bf16[256,2048]{1,0:T(8,128)(2,1)S(1)} %copy-done.10, bf16[2048,320]{1,0:T(8,128)(2,1)S(1)} %copy-done.21, ...), custom_call_target="tpu_custom_call" | custom-call | flops 1 | bytes 1 | tf_op jit(solution)/shard_map/attention_back/pallas_call | solution.py:242
  521.9 11.6 %collective-permute-done.31 = bf16[256,2048]{1,0:T(8,128)(2,1)S(1)} collective-permute-done((bf16[256,2048]{1,0:T(8,128)(2,1)S(1)}, bf16[256,2048]{1,0:T(8,128)(2,1)S(1)}, u32[]{:S(2)}, u32[]{:S(2)}) %collective-permute-start.31) | collective-permute-done | bytes 1048608 | tf_op jit(solution)/shard_map/ppermute | solution.py:464
  592.4 13.2 %collective-permute-done.37 = bf16[256,2048]{1,0:T(8,128)(2,1)S(1)} collective-permute-done((bf16[256,2048]{1,0:T(8,128)(2,1)}, bf16[256,2048]{1,0:T(8,128)(2,1)S(1)}, u32[]{:S(2)}, u32[]{:S(2)}) %collective-permute-start.37) | collective-permute-done | bytes 1048608 | tf_op jit(solution)/shard_map/ppermute | solution.py:464
  607.1 12.2 %collective-permute-done.41 = bf16[128,2048]{1,0:T(8,128)(2,1)S(1)} collective-permute-done((bf16[128,2048]{1,0:T(8,128)(2,1)S(1)}, bf16[128,2048]{1,0:T(8,128)(2,1)S(1)}, u32[]{:S(2)}, u32[]{:S(2)}) %collective-permute-start.41) | collective-permute-done | bytes 524320 | tf_op jit(solution)/shard_map/ppermute | solution.py:464
  640.1 15.5 %collective-permute-done.48 = f32[2,2048]{1,0:T(2,128)S(1)} collective-permute-done((f32[2,2048]{1,0:T(2,128)S(1)}, f32[2,2048]{1,0:T(2,128)S(1)}, u32[]{:S(2)}, u32[]{:S(2)}) %collective-permute-start.48) | collective-permute-done | bytes 16416 | tf_op jit(solution)/shard_map/ppermute | solution.py:464
  658.6 18.2 %collective-permute-start.45 = (bf16[256,2048]{1,0:T(8,128)(2,1)S(1)}, bf16[256,2048]{1,0:T(8,128)(2,1)S(1)}, u32[]{:S(2)}, u32[]{:S(2)}) collective-permute-start(bf16[256,2048]{1,0:T(8,128)(2,1)S(1)} %copy-done.46), channel_id=1, source_target_pairs={{0,0},{4,8},{8,4},{12,12},{1,1},{5,9},{9,5},{13,13},{2,2},{6,10},{... | collective-permute-start | bytes 3145736 | tf_op jit(solution)/shard_map/ppermute | solution.py:389
  680.0 16.9 %collective-permute-start.51 = (bf16[288,2048]{1,0:T(8,128)(2,1)S(1)}, bf16[288,2048]{1,0:T(8,128)(2,1)S(1)}, u32[]{:S(2)}, u32[]{:S(2)}) collective-permute-start(bf16[288,2048]{1,0:T(8,128)(2,1)S(1)} %fusion.4), channel_id=1, source_target_pairs={{4,0},{8,12},{5,1},{9,13},{6,2},{10,14},{7,3},{11,15},{20,16},{24,... | collective-permute-start | bytes 3538952 | tf_op jit(solution)/shard_map/ppermute | solution.py:395
  718.7 12.2 %collective-permute-done.52 = bf16[288,2048]{1,0:T(8,128)(2,1)S(1)} collective-permute-done((bf16[288,2048]{1,0:T(8,128)(2,1)S(1)}, bf16[288,2048]{1,0:T(8,128)(2,1)S(1)}, u32[]{:S(2)}, u32[]{:S(2)}) %collective-permute-start.52) | collective-permute-done | bytes 1179680 | tf_op jit(solution)/shard_map/ppermute | solution.py:401
  738.9 11.5 %collective-permute-done.54 = bf16[288,2048]{1,0:T(8,128)(2,1)S(1)} collective-permute-done((bf16[288,2048]{1,0:T(8,128)(2,1)S(1)}, bf16[288,2048]{1,0:T(8,128)(2,1)S(1)}, u32[]{:S(2)}, u32[]{:S(2)}) %collective-permute-start.54) | collective-permute-done | bytes 1179680 | tf_op jit(solution)/shard_map/ppermute | solution.py:401
  (406 shorter events, 329.9 us)
Async XLA Ops:
  7.2 280.3 %all-gather.6.cloned.1.call-start = ((), (), s32[]{:S(2)}) async-start(), calls=%async_computation.1 | async-start | bytes 9437184 | tf_op jit(solution)/shard_map/all_gather | solution.py:475
  40.2 41.1 %collective-permute-start.3 = (bf16[304,2048]{1,0:T(8,128)(2,1)S(1)}, bf16[304,2048]{1,0:T(8,128)(2,1)S(1)}, u32[]{:S(2)}, u32[]{:S(2)}) collective-permute-start(bf16[304,2048]{1,0:T(8,128)(2,1)S(1)} %constant_dynamic-update-slice_fusion), channel_id=1, source_target_pairs={{0,0},{4,8},{8,4},{12,12},{1,1},{5,9},{9,5},{13,13},{2,2},{6,10},{... | collective-permute-start | bytes 3735560 | tf_op jit(solution)/shard_map/ppermute | solution.py:389
  43.4 37.9 %collective-permute-start.2 = (bf16[256,2048]{1,0:T(8,128)(2,1)S(1)}, bf16[256,2048]{1,0:T(8,128)(2,1)S(1)}, u32[]{:S(2)}, u32[]{:S(2)}) collective-permute-start(bf16[256,2048]{1,0:T(8,128)(2,1)S(1)} %fusion.5), channel_id=1, source_target_pairs={{0,2},{2,0},{1,3},{3,1},{4,6},{6,4},{5,7},{7,5},{8,10},{10,8},{9,1... | collective-permute-start | bytes 3145736 | tf_op jit(solution)/shard_map/ppermute | solution.py:464
  125.8 187.4 %all-gather.4.cloned.1.call-start = ((), (), s32[]{:S(2)}) async-start(), calls=%async_computation | async-start | bytes 9437184 | tf_op jit(solution)/shard_map/all_gather | solution.py:475
  125.8 35.7 %collective-permute-start.9 = (bf16[352,2048]{1,0:T(8,128)(2,1)}, bf16[352,2048]{1,0:T(8,128)(2,1)}, u32[]{:S(2)}, u32[]{:S(2)}) collective-permute-start(bf16[352,2048]{1,0:T(8,128)(2,1)} %constant_dynamic-slice_fusion), channel_id=1, source_target_pairs={{0,0},{4,8},{8,4},{12,12},{1,1},{5,9},{9,5},{13,13},{2,2},{6,10},{... | collective-permute-start | bytes 4325384 | tf_op jit(solution)/shard_map/ppermute | solution.py:389
  166.3 38.3 %collective-permute-start.14 = (bf16[352,2048]{1,0:T(8,128)(2,1)}, bf16[352,2048]{1,0:T(8,128)(2,1)S(1)}, u32[]{:S(2)}, u32[]{:S(2)}) collective-permute-start(bf16[352,2048]{1,0:T(8,128)(2,1)} %collective-permute-done.9), channel_id=1, source_target_pairs={{0,16},{16,0},{1,17},{17,1},{2,18},{18,2},{3,19},{19,3},{4,20},{20... | collective-permute-start | bytes 4325384 | tf_op jit(solution)/shard_map/ppermute | solution.py:392
  167.6 37.1 %collective-permute-start.15 = (bf16[352,2048]{1,0:T(8,128)(2,1)S(1)}, bf16[352,2048]{1,0:T(8,128)(2,1)S(1)}, u32[]{:S(2)}, u32[]{:S(2)}) collective-permute-start(bf16[352,2048]{1,0:T(8,128)(2,1)S(1)} %copy-done.43), channel_id=1, source_target_pairs={{0,0},{4,8},{8,4},{12,12},{1,1},{5,9},{9,5},{13,13},{2,2},{6,10},{... | collective-permute-start | bytes 4325384 | tf_op jit(solution)/shard_map/ppermute | solution.py:389
  175.8 47.8 %collective-permute-start.13 = (bf16[256,2048]{1,0:T(8,128)(2,1)S(1)}, bf16[256,2048]{1,0:T(8,128)(2,1)S(1)}, u32[]{:S(2)}, u32[]{:S(2)}) collective-permute-start(bf16[256,2048]{1,0:T(8,128)(2,1)S(1)} %pad_maximum_fusion.5), channel_id=1, source_target_pairs={{0,2},{2,0},{1,3},{3,1},{4,6},{6,4},{5,7},{7,5},{8,10},{10,8},{9,1... | collective-permute-start | bytes 3145736 | tf_op jit(solution)/shard_map/ppermute | solution.py:464
  241.9 233.5 %all-gather.8.cloned.1.call-start = ((), (), s32[]{:S(2)}) async-start(), calls=%async_computation.2 | async-start | bytes 9437184 | tf_op jit(solution)/shard_map/all_gather | solution.py:475
  241.9 44.7 %collective-permute-start.18 = (bf16[352,2048]{1,0:T(8,128)(2,1)}, bf16[352,2048]{1,0:T(8,128)(2,1)}, u32[]{:S(2)}, u32[]{:S(2)}) collective-permute-start(bf16[352,2048]{1,0:T(8,128)(2,1)} %get-tuple-element.127), channel_id=1, source_target_pairs={{0,0},{4,8},{8,4},{12,12},{1,1},{5,9},{9,5},{13,13},{2,2},{6,10},{... | collective-permute-start | bytes 4325384 | tf_op jit(solution)/shard_map/ppermute | solution.py:389
  248.6 49.4 %collective-permute-start.20 = (bf16[352,2048]{1,0:T(8,128)(2,1)}, bf16[352,2048]{1,0:T(8,128)(2,1)}, u32[]{:S(2)}, u32[]{:S(2)}) collective-permute-start(bf16[352,2048]{1,0:T(8,128)(2,1)} %copy-done.13), channel_id=1, source_target_pairs={{0,16},{16,0},{1,17},{17,1},{2,18},{18,2},{3,19},{19,3},{4,20},{20... | collective-permute-start | bytes 4325384 | tf_op jit(solution)/shard_map/ppermute | solution.py:392
  366.6 41.2 %collective-permute-start.26 = (bf16[352,2048]{1,0:T(8,128)(2,1)S(1)}, bf16[352,2048]{1,0:T(8,128)(2,1)S(1)}, u32[]{:S(2)}, u32[]{:S(2)}) collective-permute-start(bf16[352,2048]{1,0:T(8,128)(2,1)S(1)} %convolution_convert_fusion.2), channel_id=1, source_target_pairs={{0,16},{16,0},{1,17},{17,1},{2,18},{18,2},{3,19},{19,3},{4,20},{20... | collective-permute-start | bytes 4325384 | tf_op jit(solution)/shard_map/ppermute | solution.py:392
  422.3 49.3 %collective-permute-start.28 = (bf16[352,2048]{1,0:T(8,128)(2,1)S(1)}, bf16[352,2048]{1,0:T(8,128)(2,1)}, u32[]{:S(2)}, u32[]{:S(2)}) collective-permute-start(bf16[352,2048]{1,0:T(8,128)(2,1)S(1)} %add_convert_fusion.2), channel_id=1, source_target_pairs={{4,0},{8,12},{5,1},{9,13},{6,2},{10,14},{7,3},{11,15},{20,16},{24,... | collective-permute-start | bytes 4325384 | tf_op jit(solution)/shard_map/ppermute | solution.py:395
  426.6 95.3 %collective-permute-start.32 = (bf16[352,2048]{1,0:T(8,128)(2,1)}, bf16[352,2048]{1,0:T(8,128)(2,1)}, u32[]{:S(2)}, u32[]{:S(2)}) collective-permute-start(bf16[352,2048]{1,0:T(8,128)(2,1)} %convolution_convert_fusion), channel_id=1, source_target_pairs={{0,16},{16,0},{1,17},{17,1},{2,18},{18,2},{3,19},{19,3},{4,20},{20... | collective-permute-start | bytes 4325384 | tf_op jit(solution)/shard_map/ppermute | solution.py:392
  478.5 55.0 %collective-permute-start.34 = (bf16[352,2048]{1,0:T(8,128)(2,1)}, bf16[352,2048]{1,0:T(8,128)(2,1)}, u32[]{:S(2)}, u32[]{:S(2)}) collective-permute-start(bf16[352,2048]{1,0:T(8,128)(2,1)} %add.362), channel_id=1, source_target_pairs={{0,16},{12,28},{16,0},{28,12},{1,17},{13,29},{17,1},{29,13},{2,18}... | collective-permute-start | bytes 4325384 | tf_op jit(solution)/shard_map/ppermute | solution.py:398
  488.7 44.9 %collective-permute-start.33 = (bf16[352,2048]{1,0:T(8,128)(2,1)S(1)}, bf16[352,2048]{1,0:T(8,128)(2,1)S(1)}, u32[]{:S(2)}, u32[]{:S(2)}) collective-permute-start(bf16[352,2048]{1,0:T(8,128)(2,1)S(1)} %add_convert_fusion.1), channel_id=1, source_target_pairs={{4,0},{8,12},{5,1},{9,13},{6,2},{10,14},{7,3},{11,15},{20,16},{24,... | collective-permute-start | bytes 4325384 | tf_op jit(solution)/shard_map/ppermute | solution.py:395
  495.3 38.3 %collective-permute-start.31 = (bf16[256,2048]{1,0:T(8,128)(2,1)S(1)}, bf16[256,2048]{1,0:T(8,128)(2,1)S(1)}, u32[]{:S(2)}, u32[]{:S(2)}) collective-permute-start(bf16[256,2048]{1,0:T(8,128)(2,1)S(1)} %copy-done.47), channel_id=1, source_target_pairs={{0,2},{2,0},{1,3},{3,1},{4,6},{6,4},{5,7},{7,5},{8,10},{10,8},{9,1... | collective-permute-start | bytes 3145736 | tf_op jit(solution)/shard_map/ppermute | solution.py:464
  541.2 91.0 %collective-permute-start.61 = (bf16[352,2048]{1,0:T(8,128)(2,1)}, bf16[352,2048]{1,0:T(8,128)(2,1)}, u32[]{:S(2)}, u32[]{:S(2)}) collective-permute-start(bf16[352,2048]{1,0:T(8,128)(2,1)} %add.362), channel_id=1, source_target_pairs={{0,8},{12,4},{1,9},{13,5},{2,10},{14,6},{3,11},{15,7},{16,24},{28,... | collective-permute-start | bytes 4325384 | tf_op jit(solution)/shard_map/ppermute | solution.py:401
  547.5 72.5 %collective-permute-start.44 = (bf16[352,2048]{1,0:T(8,128)(2,1)}, bf16[352,2048]{1,0:T(8,128)(2,1)S(1)}, u32[]{:S(2)}, u32[]{:S(2)}) collective-permute-start(bf16[352,2048]{1,0:T(8,128)(2,1)} %add.388), channel_id=1, source_target_pairs={{0,16},{12,28},{16,0},{28,12},{1,17},{13,29},{17,1},{29,13},{2,18}... | collective-permute-start | bytes 4325384 | tf_op jit(solution)/shard_map/ppermute | solution.py:398
  583.2 36.9 %collective-permute-start.43 = (bf16[288,2048]{1,0:T(8,128)(2,1)S(1)}, bf16[288,2048]{1,0:T(8,128)(2,1)S(1)}, u32[]{:S(2)}, u32[]{:S(2)}) collective-permute-start(bf16[288,2048]{1,0:T(8,128)(2,1)S(1)} %pad_maximum_fusion.2), channel_id=1, source_target_pairs={{0,16},{16,0},{1,17},{17,1},{2,18},{18,2},{3,19},{19,3},{4,20},{20... | collective-permute-start | bytes 3538952 | tf_op jit(solution)/shard_map/ppermute | solution.py:392
  629.0 48.7 %collective-permute-start.55 = (bf16[352,2048]{1,0:T(8,128)(2,1)}, bf16[352,2048]{1,0:T(8,128)(2,1)S(1)}, u32[]{:S(2)}, u32[]{:S(2)}) collective-permute-start(bf16[352,2048]{1,0:T(8,128)(2,1)} %add.388), channel_id=1, source_target_pairs={{0,8},{12,4},{1,9},{13,5},{2,10},{14,6},{3,11},{15,7},{16,24},{28,... | collective-permute-start | bytes 4325384 | tf_op jit(solution)/shard_map/ppermute | solution.py:401
  656.4 56.2 %collective-permute-start.58 = (bf16[352,2048]{1,0:T(8,128)(2,1)S(1)}, bf16[352,2048]{1,0:T(8,128)(2,1)S(1)}, u32[]{:S(2)}, u32[]{:S(2)}) collective-permute-start(bf16[352,2048]{1,0:T(8,128)(2,1)S(1)} %add.397), channel_id=1, source_target_pairs={{0,8},{12,4},{1,9},{13,5},{2,10},{14,6},{3,11},{15,7},{16,24},{28,... | collective-permute-start | bytes 4325384 | tf_op jit(solution)/shard_map/ppermute | solution.py:401
  657.8 55.0 %collective-permute-start.59 = (bf16[352,2048]{1,0:T(8,128)(2,1)S(1)}, bf16[352,2048]{1,0:T(8,128)(2,1)S(1)}, u32[]{:S(2)}, u32[]{:S(2)}) collective-permute-start(bf16[352,2048]{1,0:T(8,128)(2,1)S(1)} %add.397), channel_id=1, source_target_pairs={{0,16},{12,28},{16,0},{28,12},{1,17},{13,29},{17,1},{29,13},{2,18}... | collective-permute-start | bytes 4325384 | tf_op jit(solution)/shard_map/ppermute | solution.py:398
  658.6 42.5 %collective-permute-start.45 = (bf16[256,2048]{1,0:T(8,128)(2,1)S(1)}, bf16[256,2048]{1,0:T(8,128)(2,1)S(1)}, u32[]{:S(2)}, u32[]{:S(2)}) collective-permute-start(bf16[256,2048]{1,0:T(8,128)(2,1)S(1)} %copy-done.46), channel_id=1, source_target_pairs={{0,0},{4,8},{8,4},{12,12},{1,1},{5,9},{9,5},{13,13},{2,2},{6,10},{... | collective-permute-start | bytes 3145736 | tf_op jit(solution)/shard_map/ppermute | solution.py:389
  (117 other events, 1659.8 us)
Sparse Core Ops, SparseCore 0:
  125.9 88.4 all-gather.5
  241.8 62.1 all-gather.3
  412.7 62.6 all-gather.7

commit v4 on v3

--- a/solution.py
+++ b/solution.py
@@ -373,6 +373,190 @@
     )(order, rows, weight)
 
 
+def unit_kernel(with_arrived, acts_ref, rows_ref, *refs):
+    total = dot_nn(acts_ref[...], rows_ref[...])
+    if with_arrived:
+        total = total + refs[0][...]
+    refs[-1][...] = total.astype(jnp.bfloat16)
+
+
+def unit_grad(acts, piece, pieces, rows, arrived=None):
+    units = acts.shape[0] // pieces
+    group_rows, model = rows.shape
+    columns = model // 4
+    part = pl.BlockSpec((units, columns), lambda i: (0, i))
+    return pl.pallas_call(
+        functools.partial(unit_kernel, arrived is not None),
+        out_shape=jax.ShapeDtypeStruct((units, model), jnp.bfloat16),
+        grid=(4,),
+        in_specs=[
+            pl.BlockSpec((units, group_rows), lambda i: (piece, 0)),
+            pl.BlockSpec((group_rows, columns), lambda i: (0, i)),
+            *([] if arrived is None else [part]),
+        ],
+        out_specs=part,
+        compiler_params=pltpu.CompilerParams(vmem_limit_bytes=24 << 20),
+        cost_estimate=NO_COST,
+        name="unit_grad",
+    )(acts, rows, *([] if arrived is None else [arrived]))
+
+
+def hidden_kernel(mine_ref, other_ref, rows_ref, grad_ref):
+    half = mine_ref.shape[0]
+    grad_ref[pl.ds(0, half)] = dot_nt(mine_ref[...], rows_ref[...])
+    grad_ref[pl.ds(half, half)] = dot_nt(other_ref[...], rows_ref[...])
+
+
+def hidden_grad(mine, other, rows):
+    half, model = mine.shape
+    group_rows = rows.shape[0]
+    block = group_rows // 4
+    weight = pl.BlockSpec((half, model), lambda i: (0, 0))
+    return pl.pallas_call(
+        hidden_kernel,
+        out_shape=jax.ShapeDtypeStruct((2 * half, group_rows), jnp.float32),
+        grid=(4,),
+        in_specs=[weight, weight, pl.BlockSpec((block, model), lambda i: (i, 0))],
+        out_specs=pl.BlockSpec((2 * half, block), lambda i: (0, i)),
+        compiler_params=pltpu.CompilerParams(vmem_limit_bytes=28 << 20),
+        cost_estimate=NO_COST,
+        name="hidden_grad",
+    )(mine, other, rows)
+
+
+def head_kernel(
+    qkv_ref, twin_ref, own_ref, mixed_ref, attn_ref, weight_ref, gain_ref, mine_ref, other_ref, sum_ref
+):
+    half = twin_ref.shape[0]
+    qkv = dot_tn(qkv_ref[pl.ds(0, half)], twin_ref[...]) + dot_tn(
+        qkv_ref[pl.ds(half, half)], own_ref[...]
+    )
+    out = dot_tn(mixed_ref[...], attn_ref[...])
+    gain_grad = jnp.sum(qkv * weight_ref[...].astype(jnp.float32), axis=0, keepdims=True)
+    sum_ref[...] = gain_grad / gain_ref[...]
+    for which, ref in enumerate((mine_ref, other_ref)):
+        at = VALUES + which * FEAT
+        ref[pl.ds(0, HEAD_V)] = qkv[which * HEAD_V : (which + 1) * HEAD_V].astype(ref.dtype)
+        ref[pl.ds(HEAD_V, FEAT)] = qkv[at : at + FEAT].astype(ref.dtype)
+        ref[pl.ds(HEAD_V + FEAT, FEAT)] = qkv[at + FEATS : at + FEATS + FEAT].astype(ref.dtype)
+        ref[pl.ds(HEAD_V + 2 * FEAT, HEAD_V)] = out[which * HEAD_V : (which + 1) * HEAD_V].astype(
+            ref.dtype
+        )
+
+
+def head_grads(qkv, twin, own, mixed, attn_rows, weight, gain):
+    group_rows, model = attn_rows.shape
+    columns = model // 4
+    size = 2 * HEAD_V + 2 * FEAT
+
+    def whole(values):
+        return pl.BlockSpec(values.shape, lambda i: (0, 0))
+
+    def part(rows):
+        return pl.BlockSpec((rows, columns), lambda i: (0, i))
+
+    return pl.pallas_call(
+        head_kernel,
+        out_shape=[
+            jax.ShapeDtypeStruct((size, model), jnp.float32),
+            jax.ShapeDtypeStruct((size, model), jnp.bfloat16),
+            jax.ShapeDtypeStruct((1, model), jnp.float32),
+        ],
+        grid=(4,),
+        in_specs=[
+            whole(qkv),
+            part(group_rows // 2),
+            part(group_rows // 2),
+            whole(mixed),
+            part(group_rows),
+            part(weight.shape[0]),
+            part(1),
+        ],
+        out_specs=[part(size), part(size), part(1)],
+        compiler_params=pltpu.CompilerParams(vmem_limit_bytes=32 << 20),
+        cost_estimate=NO_COST,
+        name="head_grads",
+    )(qkv, twin, own, mixed, attn_rows, weight, gain.reshape(1, model))
+
+
+def chosen(flags_ref, own_ref, twin_ref):
+    return jnp.where(flags_ref[1] == 1, own_ref[...], twin_ref[...]).astype(jnp.float32)
+
+
+def finish_kernel(flags_ref, mine_ref, mine_twin_ref, theirs_ref, theirs_twin_ref, grad_ref):
+    half = mine_ref.shape[0]
+    mine, theirs = pl.ds(flags_ref[0] * half, half), pl.ds((1 - flags_ref[0]) * half, half)
+    grad_ref[mine] = chosen(flags_ref, mine_ref, mine_twin_ref)
+    grad_ref[theirs] = chosen(flags_ref, theirs_ref, theirs_twin_ref)
+
+
+def finish_unit(flags, *parts):
+    half, model = parts[0].shape
+    columns = model // 4
+    part = pl.BlockSpec((half, columns), lambda i, f: (0, i))
+    return pl.pallas_call(
+        finish_kernel,
+        out_shape=jax.ShapeDtypeStruct((2 * half, model), jnp.float32),
+        grid_spec=pltpu.PrefetchScalarGridSpec(
+            num_scalar_prefetch=1,
+            grid=(4,),
+            in_specs=[part] * 4,
+            out_specs=pl.BlockSpec((2 * half, columns), lambda i, f: (0, i)),
+        ),
+        compiler_params=pltpu.CompilerParams(vmem_limit_bytes=24 << 20),
+        cost_estimate=NO_COST,
+        name="finish_unit",
+    )(flags, *parts)
+
+
+def finish_head_kernel(
+    flags_ref, mine_ref, mine_twin_ref, theirs_ref, theirs_twin_ref, query_ref, key_ref, value_ref, out_ref
+):
+    halves = (
+        (flags_ref[0], chosen(flags_ref, mine_ref, mine_twin_ref)),
+        (1 - flags_ref[0], chosen(flags_ref, theirs_ref, theirs_twin_ref)),
+    )
+    for at, grads in halves:
+        features = pl.ds(pl.multiple_of(at * FEAT, FEAT), FEAT)
+        values = pl.ds(pl.multiple_of(at * HEAD_V, HEAD_V), HEAD_V)
+        value_ref[:, values] = grads[:HEAD_V].T
+        query_ref[features] = grads[HEAD_V : HEAD_V + FEAT]
+        key_ref[features] = grads[HEAD_V + FEAT : HEAD_V + 2 * FEAT]
+        out_ref[values] = grads[HEAD_V + 2 * FEAT :]
+
+
+def finish_head(flags, *parts):
+    size, model = parts[0].shape
+    columns = model // 4
+
+    def part(rows):
+        return pl.BlockSpec((rows, columns), lambda i, f: (0, i))
+
+    return pl.pallas_call(
+        finish_head_kernel,
+        out_shape=[
+            jax.ShapeDtypeStruct((FEATS, model), jnp.float32),
+            jax.ShapeDtypeStruct((FEATS, model), jnp.float32),
+            jax.ShapeDtypeStruct((model, VALUES), jnp.float32),
+            jax.ShapeDtypeStruct((VALUES, model), jnp.float32),
+        ],
+        grid_spec=pltpu.PrefetchScalarGridSpec(
+            num_scalar_prefetch=1,
+            grid=(4,),
+            in_specs=[part(size)] * 4,
+            out_specs=[
+                part(FEATS),
+                part(FEATS),
+                pl.BlockSpec((columns, VALUES), lambda i, f: (i, 0)),
+                part(VALUES),
+            ],
+        ),
+        compiler_params=pltpu.CompilerParams(vmem_limit_bytes=24 << 20),
+        cost_estimate=NO_COST,
+        name="finish_head",
+    )(flags, *parts)
+
+
 def sync(*values):
     return lax.optimization_barrier(values)
 
@@ -385,6 +569,8 @@
     y_pairs = [(i, i ^ 1) for i in range(y_size)]
     owner_y_pairs = [(i * 4 + kh, (i ^ 1) * 4 + kh) for i in range(y_size) for kh in (0, 3)]
 
+    cross_pairs = [(i * 4 + kh, (i ^ 1) * 4 + (kh ^ 2)) for i in range(y_size) for kh in (0, 3)]
+
     def trade(values):
         return lax.ppermute(values, ("k", "h"), [(0, 0), (1, 2), (2, 1), (3, 3)])
 
@@ -397,9 +583,11 @@
     def over_owners(values):
         return lax.ppermute(values, ("y", "k", "h"), owner_y_pairs)
 
-    def from_owner(values):
-        twin = lax.ppermute(values, ("k", "h"), [(0, 2), (3, 1)])
-        return jnp.where(lax.axis_index("k") == lax.axis_index("h"), values, twin)
+    def to_twin(values):
+        return lax.ppermute(values, ("k", "h"), [(0, 2), (3, 1)])
+
+    def across(values):
+        return lax.ppermute(values, ("y", "k", "h"), cross_pairs)
 
     def all_y(total):
         step = 2
@@ -462,14 +650,6 @@
 
     def flip(values, name):
         return lax.ppermute(values, name, FLIP)
-
-    def in_order(mine, theirs, axis=0):
-        first = lax.axis_index("y") % 2 == 0
-        return jnp.where(
-            first,
-            jnp.concatenate([mine, theirs], axis=axis),
-            jnp.concatenate([theirs, mine], axis=axis),
-        ).astype(jnp.float32)
 
     def gather(rows):
         return lax.all_gather(rows, SQUARE, axis=0, tiled=True)
@@ -496,6 +676,7 @@
         stacked = jnp.arange(4, dtype=jnp.int32)
         qkv_size = HEAD_V + 2 * FEAT
         head_size = qkv_size + HEAD_V
+        own_tokens = trade(tokens)
         head_half = jnp.concatenate(
             [
                 my_half(w_value, 1).T,
@@ -507,16 +688,17 @@
             axis=0,
         )
         down_half, gate_half, up_half = my_half(w_down), my_half(w_gate.T), my_half(w_up.T)
-        own_tokens = trade(tokens)
         own_tokens = after(own_tokens, head_half, down_half, gate_half, up_half)
         inputs = own_tokens.astype(jnp.float32)
         normed_one, scale_one, low_one = norm_rows(inputs, gain_one)
 
         head_mine = trade(after(head_half, low_one))
-        from_x, from_l, head_mine = sync(flip(low_one, "x"), flip(low_one, "l"), head_mine)
+        from_x, from_l, head_mine, own_grad = sync(
+            flip(low_one, "x"), flip(low_one, "l"), head_mine, trade(after(cotangent, low_one))
+        )
+        grad_rows = gather(own_grad)
         half = low_one.shape[0] // 2
         qkv_other = over_y(head_mine[:qkv_size])
-        own_grad = trade(after(cotangent, head_mine))
         d_top = flip(from_l[:half], "x")
         d_bottom = flip(from_x[half:], "l")
         stack_own = jnp.concatenate([d_top, d_bottom, from_x, from_l, low_one], axis=0)
@@ -535,15 +717,14 @@
             ],
             axis=0,
         )
-        stack_twin, w_qkv, own_grad, first = sync(stack_twin, w_qkv, own_grad, first)
-
-        grad_rows = gather(own_grad)
+        stack_twin, w_qkv, first = sync(stack_twin, w_qkv, first)
+
         down_mine = trade(after(down_half, own_grad))
         qkv, mixed_heads, ratio, denom = attention_rows(
             first, halves_at, ends, stack_twin, stack_own, w_qkv
         )
+        mixed_heads, down_mine, wo_other = sync(mixed_heads, down_mine, wo_other)
         wo = jnp.concatenate([head_mine[qkv_size:head_size], wo_other], axis=0)
-        mixed_heads, down_mine, wo = sync(mixed_heads, down_mine, wo)
 
         from_twin = flip(product_rows(for_twin, mixed_heads, wo), "k")
         down_other = over_y(down_mine)
@@ -551,19 +732,18 @@
         (first_x, first_l), rest = scatter_first(
             product_rows(for_own, mixed_heads, wo), from_twin
         )
-        got_x, got_l, down_other, gate_mine = sync(
-            flip(first_x, "x"), flip(first_l, "l"), down_other, gate_mine
-        )
+        got_x, got_l, down_other = sync(flip(first_x, "x"), flip(first_l, "l"), down_other)
         to_x, to_l = scatter_last(got_x, got_l, rest)
+        attn_out = scatter_end(got_x, got_l, flip(to_x, "x"), flip(to_l, "l"), rest)
+        attn_out, gate_mine = sync(attn_out, gate_mine)
         up_mine = trade(after(up_half, gate_mine))
         gate_other = over_y(gate_mine)
-        attn_out = scatter_end(got_x, got_l, flip(to_x, "x"), flip(to_l, "l"), rest)
 
         residual = inputs + attn_out
         normed_two, scale_two, low_two = norm_rows(residual, gain_two)
         gathered_two = gather(low_two)
         wd = jnp.concatenate([down_mine, down_other], axis=0)
-        grad_hidden = dot_nt(wd, after(grad_rows, up_mine, low_two))
+        grad_hidden = hidden_grad(down_mine, down_other, after(grad_rows, low_two, up_mine))
         up_other = over_y(up_mine)
         gathered_two, up_other, gate_other, grad_hidden = sync(
             gathered_two, up_other, gate_other, grad_hidden
@@ -575,19 +755,18 @@
         act_grad, hidden, parts_own = ffn_rows(
             for_own, gathered_two, grad_hidden, weights, tuple(acts)
         )
-        units = hidden.shape[0] // 2
-        unit_acts = {
-            "gate": (act_grad[:units], act_grad[2 * units : 3 * units]),
-            "up": (act_grad[units : 2 * units], act_grad[3 * units :]),
-            "down": (hidden[:units], hidden[units:]),
-        }
         unit_rows = {"gate": gathered_two, "up": gathered_two, "down": grad_rows}
+        unit_at = {"gate": (0, 2, 4), "up": (1, 3, 4), "down": (0, 1, 2)}
 
         def other_part(name, *deps):
-            return low_dot(after(unit_acts[name][1], *deps), unit_rows[name])
+            _, piece, pieces = unit_at[name]
+            acts = after(hidden if pieces == 2 else act_grad, *deps)
+            return unit_grad(acts, piece, pieces, unit_rows[name])
 
         def y_total(name, arrived):
-            return all_y((dot_nn(unit_acts[name][0], unit_rows[name]) + arrived).astype(jnp.bfloat16))
+            piece, _, pieces = unit_at[name]
+            acts = hidden if pieces == 2 else act_grad
+            return all_y(unit_grad(acts, piece, pieces, unit_rows[name], arrived))
 
         (first_x, first_l), rest = scatter_first(parts_own, from_twin)
         down_part = other_part("down", first_x)
@@ -617,64 +796,81 @@
         down_total = y_total("down", after(down_y, low_resid))
         down_h = over_h(down_total)
         ffn_from_twin = flip(after(ffn_twin, low_resid), "k")
-        (first_x, first_l), rest = scatter_first(ffn_own, ffn_from_twin)
-        grad_attn_rows, gate_y, down_h, first_x, first_l = sync(
-            grad_attn_rows, gate_y, down_h, first_x, first_l
-        )
-
-        gate_total = y_total("gate", gate_y)
+        (ffn_x, ffn_l), ffn_rest = scatter_first(ffn_own, ffn_from_twin)
+        gate_total = y_total("gate", after(gate_y, down_total))
         gate_h = over_h(gate_total)
-        down_total = down_total + down_h
-        down_back = over_owners(down_total)
+        up_total = y_total("up", after(up_y, gate_total))
+        up_h = over_h(up_total)
+        grad_attn_rows, up_total, ffn_x, ffn_l = sync(grad_attn_rows, up_total, ffn_x, ffn_l)
+
         grad_qkv = attention_back(
-            first, place, ends, after(grad_attn_rows, gate_total), wo, qkv, ratio, denom
-        )
-        grad_qkv, got_x, got_l, up_y, gate_h, down_back = sync(
-            grad_qkv, flip(first_x, "x"), flip(first_l, "l"), up_y, gate_h, down_back
-        )
-
-        half_rows = stack_own.shape[0]
-        to_x, to_l = scatter_last(got_x, got_l, rest)
+            first, place, ends, grad_attn_rows, wo, qkv, ratio, denom
+        )
+        grad_qkv, down_h, gate_h = sync(grad_qkv, down_h, gate_h)
+
         from_twin = flip(product_rows(stacked, grad_qkv, w_qkv), "k")
         one_own = product_rows(stacked + 4, grad_qkv, w_qkv)
-        ffn_out = scatter_end(got_x, got_l, flip(to_x, "x"), flip(to_l, "l"), rest)
         (first_x, first_l), rest = scatter_first(one_own, from_twin)
-        up_total = y_total("up", after(up_y, first_x))
-        up_h = over_h(up_total)
-        late_qkv = after(grad_qkv, up_total)
-        qkv_part = dot_tn(late_qkv[:half_rows], stack_twin) + dot_tn(
-            late_qkv[half_rows:], stack_own
-        )
-        out_part = dot_tn(after(mixed_heads, up_total), grad_attn_rows)
-
-        def one_head(which):
-            at_query = VALUES + which * FEAT
-            return jnp.concatenate(
-                [
-                    qkv_part[which * HEAD_V : (which + 1) * HEAD_V],
-                    qkv_part[at_query : at_query + FEAT],
-                    qkv_part[at_query + FEATS : at_query + FEATS + FEAT],
-                    out_part[which * HEAD_V : (which + 1) * HEAD_V],
-                ],
-                axis=0,
-            )
-
-        head_y = over_y(one_head(1).astype(jnp.bfloat16))
-        block_out = trade((residual + ffn_out).astype(jnp.bfloat16))
-        got_x, got_l, block_out = sync(flip(first_x, "x"), flip(first_l, "l"), block_out)
+        head_part, head_other, gain_one_part = head_grads(
+            after(grad_qkv, first_x),
+            stack_twin,
+            stack_own,
+            mixed_heads,
+            grad_attn_rows,
+            w_qkv,
+            gain_one,
+        )
+        head_y = over_y(head_other)
+        down_total = after(down_total, head_other) + down_h
+        down_back = over_owners(down_total)
+        got_x, got_l, up_h = sync(flip(first_x, "x"), flip(first_l, "l"), up_h)
         to_x, to_l = scatter_last(got_x, got_l, rest)
-        gate_total = gate_total + gate_h
+        gain_grads = jnp.concatenate([gain_one_part, gain_two_part[None]], axis=0)
+        gate_total = after(gate_total, to_x) + gate_h
         gate_back = over_owners(gate_total)
         grad_normed_one = scatter_end(got_x, got_l, flip(to_x, "x"), flip(to_l, "l"), rest)
-        grad_normed_one, head_y, gate_back = sync(grad_normed_one, head_y, gate_back)
+        grad_normed_one, ffn_x, ffn_l = sync(grad_normed_one, ffn_x, ffn_l)
 
         grad_tokens = grad_resid + norm_back(grad_normed_one, normed_one, scale_one, gain_one)
         low_tokens = grad_tokens.astype(jnp.bfloat16)
-        grad_tokens = trade(low_tokens).astype(jnp.float32)
-        head_total = all_y((one_head(0) + head_y).astype(jnp.bfloat16))
+        grad_tokens = trade(low_tokens)
+        head_total = all_y((after(head_part, low_tokens) + head_y).astype(jnp.bfloat16))
         head_h = over_h(head_total)
-        gain_one_part = jnp.sum(after(qkv_part, low_tokens) * w_qkv, axis=0) / gain_one
-        gain_grads = jnp.stack([gain_one_part, gain_two_part])
+        flags = jnp.stack(
+            [lax.axis_index("y") % 2, (lax.axis_index("k") == lax.axis_index("h")).astype(jnp.int32)]
+        )
+
+        def spread(total, back):
+            return total, to_twin(total), back, to_twin(back)
+
+        down_parts, gate_parts = spread(down_total, down_back), spread(gate_total, gate_back)
+        grad_tokens, head_h, up_total, got_x, got_l, *parts = sync(
+            grad_tokens,
+            head_h,
+            up_total,
+            flip(ffn_x, "x"),
+            flip(ffn_l, "l"),
+            *down_parts,
+            *gate_parts,
+        )
+        head_total = head_total + head_h
+        head_back, head_cross = over_owners(head_total), across(head_total)
+        up_total = up_total + up_h
+        up_back = over_owners(up_total)
+        to_x, to_l = scatter_last(got_x, got_l, ffn_rest)
+        last_x, last_l, down_grad, gate_grad, up_back = sync(
+            flip(to_x, "x"),
+            flip(to_l, "l"),
+            finish_unit(flags, *parts[:4]),
+            finish_unit(flags, *parts[4:]),
+            up_back,
+        )
+        ffn_out = scatter_end(got_x, got_l, last_x, last_l, ffn_rest)
+        block_out = trade((residual + ffn_out).astype(jnp.bfloat16))
+        up_grad = finish_unit(flags, *spread(up_total, up_back))
+        query_grad, key_grad, value_grad, out_grad = finish_head(
+            flags, head_total, to_twin(head_total), head_back, head_cross
+        )
         for name in ("k", "x", "l", "h"):
             gain_grads = gain_grads + flip(gain_grads, name)
         step = 1
@@ -683,32 +879,19 @@
                 gain_grads, "y", [(i, i ^ step) for i in range(y_size)]
             )
             step *= 2
-        up_total = up_total + up_h
-        up_back = over_owners(up_total)
-        down_total, down_back = from_owner(down_total), from_owner(down_back)
-        gate_total, gate_back = from_owner(gate_total), from_owner(gate_back)
-        up_total = from_owner(up_total)
-        head_total = head_total + head_h
-        head_back = over_owners(head_total)
-        head_total = from_owner(head_total)
-        up_back = from_owner(up_back)
-        head_back = from_owner(head_back)
-
-        def head_grad(start, stop):
-            return in_order(head_total[start:stop], head_back[start:stop])
 
         return (
             block_out,
-            grad_tokens,
+            grad_tokens.astype(jnp.float32),
             gain_grads[0],
-            head_grad(HEAD_V, HEAD_V + FEAT).T,
-            head_grad(HEAD_V + FEAT, qkv_size).T,
-            in_order(head_total[:HEAD_V].T, head_back[:HEAD_V].T, 1),
-            head_grad(qkv_size, head_size),
+            query_grad.T,
+            key_grad.T,
+            value_grad,
+            out_grad,
             gain_grads[1],
-            in_order(gate_total, gate_back).T,
-            in_order(up_total, up_back).T,
-            in_order(down_total, down_back),
+            gate_grad.T,
+            up_grad.T,
+            down_grad,
         )
 
     return body

time: 781 us -> 733 us (0.939)
  Pallas kernels: 110 us -> 176 us
  matrix products: 57.7 us -> 0 us
  waiting for transfers between devices: 347 us -> 298 us
  starting transfers between devices: 129 us -> 111 us
  local copies, waits for them, and re-layouts: 48.1 us -> 64 us
    pallas_call x0 -> x12, Pallas kernels: none -> 63.5 us  [the longest x6 29 us: unit_grad(): pl.pallas_call(functools.partial(unit_kernel, arrived is not None), out_s...]
    dot_general x10 -> x0, matrix products: 57.7 us -> none  [the longest x6 37.4 us: dot_nn(): return jnp.dot(left_mat, right_mat, preferred_element_type=jnp.float32)]
    ppermute x29, waiting for transfers between devices: 149 us -> 102 us  [flip(): return lax.ppermute(values, name, FLIP)]
    ppermute x8, waiting for transfers between devices: 96.7 us -> 130 us  [trade(): return lax.ppermute(values, ('k', 'h'), [(0, 0), (1, 2), (2, 1), (3, 3)])]
    ppermute x8, waiting for transfers between devices: 28 us -> 0.02 us  [the longest x7 0.02 us: to_twin(): return lax.ppermute(values, ('k', 'h'), [(0, 2), (3, 1)])]
    ppermute x4, waiting for transfers between devices: 30.6 us -> 3.31 us  [over_h(): return lax.ppermute(values, ('k', 'h'), [(1, 0), (2, 3)])]
    ppermute x9, waiting for transfers between devices: 38.7 us -> 62.6 us  [over_y(): return lax.ppermute(values, 'y', y_pairs)]
    unnamed x164 -> x159, local copies, waits for them, and re-layouts: 33.6 us -> 52 us
  transfers between devices with their start and end apart: 66 -> 66, of which waited for: 30 -> 24; matrix products, arithmetic and copies ran while one was open for 17% -> 10% of each run, Pallas kernels for 11% -> 21%
where the time goes in v4:
time: 733 us; the launch traced here: 721 us
  waiting for transfers between devices  298 us (41%)
  Pallas kernels  176 us (24%)
  starting transfers between devices  111 us (15%)
  local copies, waits for them, and re-layouts  64 us (9%)
  other arithmetic  56.1 us (8%)
  between operations  15.7 us (2%)
    ppermute x8, waiting for transfers between devices, trade(): return lax.ppermute(values, ('k', 'h'), [(0, 0), (1, 2), (2, 1), (3, 3)])  130 us
    ppermute x29, waiting for transfers between devices, flip(): return lax.ppermute(values, name, FLIP)  102 us
    ppermute x9, waiting for transfers between devices, over_y(): return lax.ppermute(values, 'y', y_pairs)  62.6 us
    unnamed x159, local copies, waits for them, and re-layouts  52 us
    pallas_call x2, Pallas kernels, ffn_rows(): pl.pallas_call(functools.partial(ffn_kernel, pieces), out_shape=[jax.Shap...  41.3 us
    ppermute x8, starting transfers between devices, trade(): return lax.ppermute(values, ('k', 'h'), [(0, 0), (1, 2), (2, 1), (3, 3)])  33.6 us
    pallas_call x6, Pallas kernels, unit_grad(): pl.pallas_call(functools.partial(unit_kernel, arrived is not None), out_s...  29 us
    pallas_call x1, Pallas kernels, attention_back(): pl.pallas_call(backward_kernel, out_shape=jax.ShapeDtypeStruct((group_row...  27.3 us
  transfers between devices with their start and end apart: 66, of which 24 were waited for; matrix products, arithmetic and copies ran while one was open for 10% of the time, Pallas kernels for 21%

profile of v4, /device:TPU:1, one launch (start us, length us, event | category | flops | bytes accessed | tf_op | source)
XLA Modules:
  0.0 721.0 jit_solution(6047516487903613342)
XLA Ops:
  27.4 9.7 %collective-permute-done = bf16[256,2048]{1,0:T(8,128)(2,1)} collective-permute-done((bf16[256,2048]{1,0:T(8,128)(2,1)}, bf16[256,2048]{1,0:T(8,128)(2,1)}, u32[]{:S(2)}, u32[]{:S(2)}) %collective-permute-start) | collective-permute-done | bytes 1048608 | tf_op jit(solution)/shard_map/ppermute | solution.py:575
  50.1 46.3 %collective-permute-done.4 = bf16[256,2048]{1,0:T(8,128)(2,1)S(1)} collective-permute-done((bf16[256,2048]{1,0:T(8,128)(2,1)S(1)}, bf16[256,2048]{1,0:T(8,128)(2,1)S(1)}, u32[]{:S(2)}, u32[]{:S(2)}) %collective-permute-start.4) | collective-permute-done | bytes 1048608 | tf_op jit(solution)/shard_map/ppermute | solution.py:575
  126.7 22.5 %attention_rows.1 = (bf16[2048,320]{1,0:T(8,128)(2,1)S(1)}, bf16[2048,256]{1,0:T(8,128)(2,1)S(1)}, f32[2048,256]{1,0:T(8,128)S(1)}, f32[2048,256]{1,0:T(8,128)S(1)}) custom-call(s32[8]{0:T(128)S(1)} %convert_reduce_fusion.2.first_ref, s32[8]{0:T(128)S(1)} %get-tuple-element.280.twin_at_ref, s32[8]{0:T(128)S(1)} %get-tuple-element.279.own_at_ref, ...), custom_call_target="tpu_custom_call" | custom-call | flops 1 | bytes 1 | tf_op jit(solution)/shard_map/attention_rows/pallas_call | solution.py:128
  150.4 10.0 %collective-permute-done.9.mine_ref = bf16[352,2048]{1,0:T(8,128)(2,1)S(1)} collective-permute-done((bf16[352,2048]{1,0:T(8,128)(2,1)}, bf16[352,2048]{1,0:T(8,128)(2,1)S(1)}, u32[]{:S(2)}, u32[]{:S(2)}) %collective-permute-start.9) | collective-permute-done | bytes 1441824 | tf_op jit(solution)/shard_map/ppermute | solution.py:575
  178.7 17.0 %collective-permute-done.14.other_ref = bf16[352,2048]{1,0:T(8,128)(2,1)S(1)} collective-permute-done((bf16[352,2048]{1,0:T(8,128)(2,1)S(1)}, bf16[352,2048]{1,0:T(8,128)(2,1)S(1)}, u32[]{:S(2)}, u32[]{:S(2)}) %collective-permute-start.14) | collective-permute-done | bytes 1441824 | tf_op jit(solution)/shard_map/ppermute | solution.py:578
  195.8 19.1 %collective-permute-done.13 = bf16[256,2048]{1,0:T(8,128)(2,1)S(1)} collective-permute-done((bf16[256,2048]{1,0:T(8,128)(2,1)S(1)}, bf16[256,2048]{1,0:T(8,128)(2,1)S(1)}, u32[]{:S(2)}, u32[]{:S(2)}) %collective-permute-start.13) | collective-permute-done | bytes 1048608 | tf_op jit(solution)/shard_map/ppermute | solution.py:652
  216.3 11.7 %collective-permute-done.15 = bf16[128,2048]{1,0:T(8,128)(2,1)S(1)} collective-permute-done((bf16[128,2048]{1,0:T(8,128)(2,1)S(1)}, bf16[128,2048]{1,0:T(8,128)(2,1)S(1)}, u32[]{:S(2)}, u32[]{:S(2)}) %collective-permute-start.15) | collective-permute-done | bytes 524320 | tf_op jit(solution)/shard_map/ppermute | solution.py:652
  238.5 36.8 %collective-permute-done.18.refs_1_ = bf16[352,2048]{1,0:T(8,128)(2,1)} collective-permute-done((bf16[352,2048]{1,0:T(8,128)(2,1)}, bf16[352,2048]{1,0:T(8,128)(2,1)}, u32[]{:S(2)}, u32[]{:S(2)}) %collective-permute-start.18) | collective-permute-done | bytes 1441824 | tf_op jit(solution)/shard_map/ppermute | solution.py:575
  279.6 7.3 %hidden_grad.1.grad_ref = f32[704,2048]{1,0:T(8,128)S(1)} custom-call(bf16[352,2048]{1,0:T(8,128)(2,1)S(1)} %collective-permute-done.9.mine_ref, bf16[352,2048]{1,0:T(8,128)(2,1)S(1)} %collective-permute-done.14.other_ref, bf16[2048,2048]{1,0:T(8,128)(2,1)S(1)} %copy-done.4), custom_call_target="tpu_custom_call" | custom-call | flops 1 | bytes 1 | tf_op jit(solution)/shard_map/hidden_grad/pallas_call | solution.py:415
  289.4 12.4 %collective-permute-done.19.refs_3_ = bf16[352,2048]{1,0:T(8,128)(2,1)} collective-permute-done((bf16[352,2048]{1,0:T(8,128)(2,1)}, bf16[352,2048]{1,0:T(8,128)(2,1)}, u32[]{:S(2)}, u32[]{:S(2)}) %collective-permute-start.19) | collective-permute-done | bytes 1441824 | tf_op jit(solution)/shard_map/ppermute | solution.py:578
  301.8 20.6 %ffn_rows.2 = (bf16[1408,2048]{1,0:T(8,128)(2,1)}, bf16[704,2048]{1,0:T(8,128)(2,1)S(1)}, bf16[1024,2048]{1,0:T(8,128)(2,1)}) custom-call(s32[4]{0:T(128)S(1)} %get-tuple-element.278.order_ref, bf16[2048,2048]{1,0:T(8,128)(2,1)} %all-gather.4.cloned.1.call-done.rows_ref, f32[704,2048]{1,0:T(8,128)} %copy-done.8, ...), custom_call_target="tpu_custom_call" | custom-call | flops 1 | bytes 1 | tf_op jit(solution)/shard_map/ffn_rows/pallas_call | solution.py:315
  322.5 20.6 %ffn_rows.3 = (bf16[1408,2048]{1,0:T(8,128)(2,1)}, bf16[704,2048]{1,0:T(8,128)(2,1)S(1)}, bf16[1024,2048]{1,0:T(8,128)(2,1)}) custom-call(s32[4]{0:T(128)S(1)} %get-tuple-element.277.order_ref, bf16[2048,2048]{1,0:T(8,128)(2,1)} %all-gather.4.cloned.1.call-done.rows_ref, f32[704,2048]{1,0:T(8,128)} %copy-done.8, ...), custom_call_target="tpu_custom_call", output_to_operand_aliasing={{0}: (7, {}), {1}: (8, {})} | custom-call | flops 1 | bytes 1 | tf_op jit(solution)/shard_map/ffn_rows/pallas_call | solution.py:315
  415.8 15.8 %collective-permute-done.29.refs_0_ = bf16[352,2048]{1,0:T(8,128)(2,1)S(1)} collective-permute-done((bf16[352,2048]{1,0:T(8,128)(2,1)}, bf16[352,2048]{1,0:T(8,128)(2,1)S(1)}, u32[]{:S(2)}, u32[]{:S(2)}) %collective-permute-start.29) | collective-permute-done | bytes 1441824 | tf_op jit(solution)/shard_map/ppermute | solution.py:578
  445.3 17.3 %collective-permute-done.28.refs_0_ = bf16[352,2048]{1,0:T(8,128)(2,1)S(1)} collective-permute-done((bf16[352,2048]{1,0:T(8,128)(2,1)}, bf16[352,2048]{1,0:T(8,128)(2,1)S(1)}, u32[]{:S(2)}, u32[]{:S(2)}) %collective-permute-start.28) | collective-permute-done | bytes 1441824 | tf_op jit(solution)/shard_map/ppermute | solution.py:578
  476.4 27.3 %attention_back.1.rows_ref.qkv_ref = bf16[2048,320]{1,0:T(8,128)(2,1)S(1)} custom-call(s32[8]{0:T(128)S(1)} %convert_reduce_fusion.2.first_ref, s32[8]{0:T(128)S(1)} %fusion.20.place_ref, bf16[2048,2048]{1,0:T(8,128)(2,1)} %all-gather.8.cloned.1.call-done.attn_ref, bf16[256,2048]{1,0:T(8,128)(2,1)S(1)} %copy-done.15, bf16[2048,320]{1,0:T(8,128)(2,1)S(1)} %copy-done.32, ...), custom_call_target="tpu_custom_call" | custom-call | flops 1 | bytes 1 | tf_op jit(solution)/shard_map/attention_back/pallas_call | solution.py:242
  519.4 9.1 %head_grads.1 = (f32[288,2048]{1,0:T(8,128)S(1)}, bf16[288,2048]{1,0:T(8,128)(2,1)S(1)}, f32[1,2048]{1,0:T(1,128)S(1)}) custom-call(bf16[2048,320]{1,0:T(8,128)(2,1)S(1)} %attention_back.1.rows_ref.qkv_ref, bf16[1024,2048]{1,0:T(8,128)(2,1)} %collective-permute-done.8.twin_ref, bf16[1024,2048]{1,0:T(8,128)(2,1)} %constant_dynamic-update-slice_fusion.1.own_ref, ...), custom_call_target="tpu_custom_call" | custom-call | flops 1 | bytes 1 | tf_op jit(solution)/shard_map/head_grads/pallas_call | solution.py:458
  538.4 19.4 %collective-permute-done.34 = bf16[256,2048]{1,0:T(8,128)(2,1)S(1)} collective-permute-done((bf16[256,2048]{1,0:T(8,128)(2,1)S(1)}, bf16[256,2048]{1,0:T(8,128)(2,1)S(1)}, u32[]{:S(2)}, u32[]{:S(2)}) %collective-permute-start.34) | collective-permute-done | bytes 1048608 | tf_op jit(solution)/shard_map/ppermute | solution.py:652
  562.9 9.5 %collective-permute-done.36 = bf16[128,2048]{1,0:T(8,128)(2,1)S(1)} collective-permute-done((bf16[128,2048]{1,0:T(8,128)(2,1)S(1)}, bf16[128,2048]{1,0:T(8,128)(2,1)S(1)}, u32[]{:S(2)}, u32[]{:S(2)}) %collective-permute-start.36) | collective-permute-done | bytes 524320 | tf_op jit(solution)/shard_map/ppermute | solution.py:652
  592.1 10.2 %collective-permute-start.40 = (bf16[288,2048]{1,0:T(8,128)(2,1)}, bf16[288,2048]{1,0:T(8,128)(2,1)}, u32[]{:S(2)}, u32[]{:S(2)}) collective-permute-start(bf16[288,2048]{1,0:T(8,128)(2,1)} %add_convert_fusion), channel_id=1, source_target_pairs={{4,0},{8,12},{5,1},{9,13},{6,2},{10,14},{7,3},{11,15},{20,16},{24,... | collective-permute-start | bytes 3538952 | tf_op jit(solution)/shard_map/ppermute | solution.py:581
  604.4 10.9 %collective-permute-done.38 = bf16[256,2048]{1,0:T(8,128)(2,1)} collective-permute-done((bf16[256,2048]{1,0:T(8,128)(2,1)S(1)}, bf16[256,2048]{1,0:T(8,128)(2,1)}, u32[]{:S(2)}, u32[]{:S(2)}) %collective-permute-start.38) | collective-permute-done | bytes 1048608 | tf_op jit(solution)/shard_map/ppermute | solution.py:575
  620.1 7.9 %collective-permute-done.41 = bf16[256,2048]{1,0:T(8,128)(2,1)S(1)} collective-permute-done((bf16[256,2048]{1,0:T(8,128)(2,1)S(1)}, bf16[256,2048]{1,0:T(8,128)(2,1)S(1)}, u32[]{:S(2)}, u32[]{:S(2)}) %collective-permute-start.41) | collective-permute-done | bytes 1048608 | tf_op jit(solution)/shard_map/ppermute | solution.py:652
  629.7 16.6 %collective-permute-done.42 = bf16[256,2048]{1,0:T(8,128)(2,1)} collective-permute-done((bf16[256,2048]{1,0:T(8,128)(2,1)}, bf16[256,2048]{1,0:T(8,128)(2,1)}, u32[]{:S(2)}, u32[]{:S(2)}) %collective-permute-start.42) | collective-permute-done | bytes 1048608 | tf_op jit(solution)/shard_map/ppermute | solution.py:652
  679.0 7.0 collective-permute-start.52
  693.0 16.2 %collective-permute-done.52 = bf16[256,2048]{1,0:T(8,128)(2,1)S(1)} collective-permute-done((bf16[256,2048]{1,0:T(8,128)(2,1)S(1)}, bf16[256,2048]{1,0:T(8,128)(2,1)S(1)}, u32[]{:S(2)}, u32[]{:S(2)}) %collective-permute-start.52) | collective-permute-done | bytes 1048608 | tf_op jit(solution)/shard_map/ppermute | solution.py:575
  (374 shorter events, 304.0 us)
Async XLA Ops:
  7.2 268.8 %all-gather.6.cloned.1.call-start = ((), (), s32[]{:S(2)}) async-start(), calls=%async_computation.1 | async-start | bytes 9437184 | tf_op jit(solution)/shard_map/all_gather | solution.py:655
  41.2 55.3 %collective-permute-start.3 = (bf16[304,2048]{1,0:T(8,128)(2,1)}, bf16[304,2048]{1,0:T(8,128)(2,1)S(1)}, u32[]{:S(2)}, u32[]{:S(2)}) collective-permute-start(bf16[304,2048]{1,0:T(8,128)(2,1)} %constant_dynamic-update-slice_fusion), channel_id=1, source_target_pairs={{0,0},{4,8},{8,4},{12,12},{1,1},{5,9},{9,5},{13,13},{2,2},{6,10},{... | collective-permute-start | bytes 3735560 | tf_op jit(solution)/shard_map/ppermute | solution.py:575
  43.1 53.3 %collective-permute-start.4 = (bf16[256,2048]{1,0:T(8,128)(2,1)S(1)}, bf16[256,2048]{1,0:T(8,128)(2,1)S(1)}, u32[]{:S(2)}, u32[]{:S(2)}) collective-permute-start(bf16[256,2048]{1,0:T(8,128)(2,1)S(1)} %copy-done.65), channel_id=1, source_target_pairs={{0,0},{4,8},{8,4},{12,12},{1,1},{5,9},{9,5},{13,13},{2,2},{6,10},{... | collective-permute-start | bytes 3145736 | tf_op jit(solution)/shard_map/ppermute | solution.py:575
  47.7 48.8 %collective-permute-start.2 = (bf16[256,2048]{1,0:T(8,128)(2,1)}, bf16[256,2048]{1,0:T(8,128)(2,1)}, u32[]{:S(2)}, u32[]{:S(2)}) collective-permute-start(bf16[256,2048]{1,0:T(8,128)(2,1)} %fusion.3), channel_id=1, source_target_pairs={{0,2},{2,0},{1,3},{3,1},{4,6},{6,4},{5,7},{7,5},{8,10},{10,8},{9,1... | collective-permute-start | bytes 3145736 | tf_op jit(solution)/shard_map/ppermute | solution.py:652
  48.9 47.5 %collective-permute-start.1 = (bf16[256,2048]{1,0:T(8,128)(2,1)}, bf16[256,2048]{1,0:T(8,128)(2,1)}, u32[]{:S(2)}, u32[]{:S(2)}) collective-permute-start(bf16[256,2048]{1,0:T(8,128)(2,1)} %fusion.3), channel_id=1, source_target_pairs={{0,1},{1,0},{2,3},{3,2},{4,5},{5,4},{6,7},{7,6},{8,9},{9,8},{10,11... | collective-permute-start | bytes 3145736 | tf_op jit(solution)/shard_map/ppermute | solution.py:652
  101.9 199.9 %all-gather.4.cloned.1.call-start = ((), (), s32[]{:S(2)}) async-start(), calls=%async_computation | async-start | bytes 9437184 | tf_op jit(solution)/shard_map/all_gather | solution.py:655
  121.0 39.4 %collective-permute-start.9 = (bf16[352,2048]{1,0:T(8,128)(2,1)}, bf16[352,2048]{1,0:T(8,128)(2,1)S(1)}, u32[]{:S(2)}, u32[]{:S(2)}) collective-permute-start(bf16[352,2048]{1,0:T(8,128)(2,1)} %constant_dynamic-slice_fusion), channel_id=1, source_target_pairs={{0,0},{4,8},{8,4},{12,12},{1,1},{5,9},{9,5},{13,13},{2,2},{6,10},{... | collective-permute-start | bytes 4325384 | tf_op jit(solution)/shard_map/ppermute | solution.py:575
  172.2 42.7 %collective-permute-start.13 = (bf16[256,2048]{1,0:T(8,128)(2,1)S(1)}, bf16[256,2048]{1,0:T(8,128)(2,1)S(1)}, u32[]{:S(2)}, u32[]{:S(2)}) collective-permute-start(bf16[256,2048]{1,0:T(8,128)(2,1)S(1)} %pad_maximum_fusion.5), channel_id=1, source_target_pairs={{0,2},{2,0},{1,3},{3,1},{4,6},{6,4},{5,7},{7,5},{8,10},{10,8},{9,1... | collective-permute-start | bytes 3145736 | tf_op jit(solution)/shard_map/ppermute | solution.py:652
  176.3 52.5 %collective-permute-start.17 = (bf16[352,2048]{1,0:T(8,128)(2,1)S(1)}, bf16[352,2048]{1,0:T(8,128)(2,1)}, u32[]{:S(2)}, u32[]{:S(2)}) collective-permute-start(bf16[352,2048]{1,0:T(8,128)(2,1)S(1)} %copy-done.54), channel_id=1, source_target_pairs={{0,0},{4,8},{8,4},{12,12},{1,1},{5,9},{9,5},{13,13},{2,2},{6,10},{... | collective-permute-start | bytes 4325384 | tf_op jit(solution)/shard_map/ppermute | solution.py:575
  233.0 238.8 %all-gather.8.cloned.1.call-start = ((), (), s32[]{:S(2)}) async-start(), calls=%async_computation.2 | async-start | bytes 9437184 | tf_op jit(solution)/shard_map/all_gather | solution.py:655
  233.0 42.3 %collective-permute-start.18 = (bf16[352,2048]{1,0:T(8,128)(2,1)}, bf16[352,2048]{1,0:T(8,128)(2,1)}, u32[]{:S(2)}, u32[]{:S(2)}) collective-permute-start(bf16[352,2048]{1,0:T(8,128)(2,1)} %get-tuple-element.151), channel_id=1, source_target_pairs={{0,0},{4,8},{8,4},{12,12},{1,1},{5,9},{9,5},{13,13},{2,2},{6,10},{... | collective-permute-start | bytes 4325384 | tf_op jit(solution)/shard_map/ppermute | solution.py:575
  237.2 52.2 %collective-permute-start.20 = (bf16[352,2048]{1,0:T(8,128)(2,1)}, bf16[352,2048]{1,0:T(8,128)(2,1)}, u32[]{:S(2)}, u32[]{:S(2)}) collective-permute-start(bf16[352,2048]{1,0:T(8,128)(2,1)} %collective-permute-done.17.refs_0_), channel_id=1, source_target_pairs={{0,16},{16,0},{1,17},{17,1},{2,18},{18,2},{3,19},{19,3},{4,20},{20... | collective-permute-start | bytes 4325384 | tf_op jit(solution)/shard_map/ppermute | solution.py:578
  395.9 71.2 %collective-permute-start.27 = (bf16[1024,2048]{1,0:T(8,128)(2,1)}, bf16[1024,2048]{1,0:T(8,128)(2,1)S(1)}, u32[]{:S(2)}, u32[]{:S(2)}) collective-permute-start(bf16[1024,2048]{1,0:T(8,128)(2,1)} %copy-done.26), channel_id=1, source_target_pairs={{0,8},{8,0},{1,9},{9,1},{2,10},{10,2},{3,11},{11,3},{4,12},{12,4},... | collective-permute-start | bytes 12582920 | tf_op jit(solution)/shard_map/ppermute | solution.py:652
  399.4 63.2 %collective-permute-start.28 = (bf16[352,2048]{1,0:T(8,128)(2,1)}, bf16[352,2048]{1,0:T(8,128)(2,1)S(1)}, u32[]{:S(2)}, u32[]{:S(2)}) collective-permute-start(bf16[352,2048]{1,0:T(8,128)(2,1)} %unit_grad.8), channel_id=1, source_target_pairs={{0,16},{16,0},{1,17},{17,1},{2,18},{18,2},{3,19},{19,3},{4,20},{20... | collective-permute-start | bytes 4325384 | tf_op jit(solution)/shard_map/ppermute | solution.py:578
  411.0 92.6 %collective-permute-start.30 = (bf16[352,2048]{1,0:T(8,128)(2,1)S(1)}, bf16[352,2048]{1,0:T(8,128)(2,1)}, u32[]{:S(2)}, u32[]{:S(2)}) collective-permute-start(bf16[352,2048]{1,0:T(8,128)(2,1)S(1)} %unit_grad.9), channel_id=1, source_target_pairs={{4,0},{8,12},{5,1},{9,13},{6,2},{10,14},{7,3},{11,15},{20,16},{24,... | collective-permute-start | bytes 4325384 | tf_op jit(solution)/shard_map/ppermute | solution.py:581
  440.5 63.2 %collective-permute-start.31 = (bf16[352,2048]{1,0:T(8,128)(2,1)}, bf16[352,2048]{1,0:T(8,128)(2,1)}, u32[]{:S(2)}, u32[]{:S(2)}) collective-permute-start(bf16[352,2048]{1,0:T(8,128)(2,1)} %unit_grad.10), channel_id=1, source_target_pairs={{4,0},{8,12},{5,1},{9,13},{6,2},{10,14},{7,3},{11,15},{20,16},{24,... | collective-permute-start | bytes 4325384 | tf_op jit(solution)/shard_map/ppermute | solution.py:581
  517.4 40.4 %collective-permute-start.34 = (bf16[256,2048]{1,0:T(8,128)(2,1)S(1)}, bf16[256,2048]{1,0:T(8,128)(2,1)S(1)}, u32[]{:S(2)}, u32[]{:S(2)}) collective-permute-start(bf16[256,2048]{1,0:T(8,128)(2,1)S(1)} %pad_maximum_fusion.11), channel_id=1, source_target_pairs={{0,2},{2,0},{1,3},{3,1},{4,6},{6,4},{5,7},{7,5},{8,10},{10,8},{9,1... | collective-permute-start | bytes 3145736 | tf_op jit(solution)/shard_map/ppermute | solution.py:652
  518.5 39.3 %collective-permute-start.33 = (bf16[256,2048]{1,0:T(8,128)(2,1)S(1)}, bf16[256,2048]{1,0:T(8,128)(2,1)}, u32[]{:S(2)}, u32[]{:S(2)}) collective-permute-start(bf16[256,2048]{1,0:T(8,128)(2,1)S(1)} %pad_maximum_fusion.10), channel_id=1, source_target_pairs={{0,1},{1,0},{2,3},{3,2},{4,5},{5,4},{6,7},{7,6},{8,9},{9,8},{10,11... | collective-permute-start | bytes 3145736 | tf_op jit(solution)/shard_map/ppermute | solution.py:652
  528.6 54.5 %collective-permute-start.39 = (bf16[288,2048]{1,0:T(8,128)(2,1)S(1)}, bf16[288,2048]{1,0:T(8,128)(2,1)S(1)}, u32[]{:S(2)}, u32[]{:S(2)}) collective-permute-start(bf16[288,2048]{1,0:T(8,128)(2,1)S(1)} %get-tuple-element.203), channel_id=1, source_target_pairs={{0,16},{16,0},{1,17},{17,1},{2,18},{18,2},{3,19},{19,3},{4,20},{20... | collective-permute-start | bytes 3538952 | tf_op jit(solution)/shard_map/ppermute | solution.py:578
  531.7 55.1 %collective-permute-start.44 = (bf16[352,2048]{1,0:T(8,128)(2,1)S(1)}, bf16[352,2048]{1,0:T(8,128)(2,1)}, u32[]{:S(2)}, u32[]{:S(2)}) collective-permute-start(bf16[352,2048]{1,0:T(8,128)(2,1)S(1)} %add.358.mine_ref), channel_id=1, source_target_pairs={{0,16},{12,28},{16,0},{28,12},{1,17},{13,29},{17,1},{29,13},{2,18}... | collective-permute-start | bytes 4325384 | tf_op jit(solution)/shard_map/ppermute | solution.py:584
  536.8 54.2 %collective-permute-start.43 = (bf16[352,2048]{1,0:T(8,128)(2,1)S(1)}, bf16[352,2048]{1,0:T(8,128)(2,1)S(1)}, u32[]{:S(2)}, u32[]{:S(2)}) collective-permute-start(bf16[352,2048]{1,0:T(8,128)(2,1)S(1)} %add.358.mine_ref), channel_id=1, source_target_pairs={{0,8},{12,4},{1,9},{13,5},{2,10},{14,6},{3,11},{15,7},{16,24},{28,... | collective-permute-start | bytes 4325384 | tf_op jit(solution)/shard_map/ppermute | solution.py:587
  586.8 59.4 %collective-permute-start.45 = (bf16[352,2048]{1,0:T(8,128)(2,1)}, bf16[352,2048]{1,0:T(8,128)(2,1)}, u32[]{:S(2)}, u32[]{:S(2)}) collective-permute-start(bf16[352,2048]{1,0:T(8,128)(2,1)} %collective-permute-done.44.theirs_ref), channel_id=1, source_target_pairs={{0,8},{12,4},{1,9},{13,5},{2,10},{14,6},{3,11},{15,7},{16,24},{28,... | collective-permute-start | bytes 4325384 | tf_op jit(solution)/shard_map/ppermute | solution.py:587
  588.3 58.0 %collective-permute-start.48 = (bf16[352,2048]{1,0:T(8,128)(2,1)}, bf16[352,2048]{1,0:T(8,128)(2,1)}, u32[]{:S(2)}, u32[]{:S(2)}) collective-permute-start(bf16[352,2048]{1,0:T(8,128)(2,1)} %collective-permute-done.47.theirs_ref), channel_id=1, source_target_pairs={{0,8},{12,4},{1,9},{13,5},{2,10},{14,6},{3,11},{15,7},{16,24},{28,... | collective-permute-start | bytes 4325384 | tf_op jit(solution)/shard_map/ppermute | solution.py:587
  592.1 54.1 %collective-permute-start.40 = (bf16[288,2048]{1,0:T(8,128)(2,1)}, bf16[288,2048]{1,0:T(8,128)(2,1)}, u32[]{:S(2)}, u32[]{:S(2)}) collective-permute-start(bf16[288,2048]{1,0:T(8,128)(2,1)} %add_convert_fusion), channel_id=1, source_target_pairs={{4,0},{8,12},{5,1},{9,13},{6,2},{10,14},{7,3},{11,15},{20,16},{24,... | collective-permute-start | bytes 3538952 | tf_op jit(solution)/shard_map/ppermute | solution.py:581
  (114 other events, 1662.1 us)
Sparse Core Ops, SparseCore 0:
  102.0 61.8 all-gather.5
  233.1 61.0 all-gather.3
  396.0 71.2 all-gather.7

commit v5 on v4

--- a/solution.py
+++ b/solution.py
@@ -56,7 +56,7 @@
     score = dot_nt(query, keys) * 0.25
     t = i * block + lax.broadcasted_iota(jnp.int32, score.shape, 0)
     u = j * block + lax.broadcasted_iota(jnp.int32, score.shape, 1)
-    ends = ends_ref[:, pl.ds(pl.multiple_of(j * block, block), block)]
+    ends = ends_ref[:, pl.ds(pl.multiple_of(jnp.minimum(j, i) * block, block), block)]
     allowed = (t >= u) & (t <= ends)
     return score, allowed, jnp.where(allowed, 1.0 + score + 0.5 * score * score, 0.0)
 
@@ -92,19 +92,22 @@
     numer_ref[...] = jnp.zeros_like(numer_ref)
     sum_ref[...] = jnp.zeros_like(sum_ref)
 
-    def step(j, carry):
-        there = pl.ds(pl.multiple_of(j * block, block), block)
+    def step(pair, carry):
         for head in range(2):
             columns = pl.ds(head * HEAD_V, HEAD_V)
-            _, _, kernel = scores(own[head], key_ref[there], ends_ref, i, j, block)
-            folded = kernel[:, :128]
-            for c in range(1, block // 128):
-                folded = folded + kernel[:, c * 128 : (c + 1) * 128]
+            folded, numer = None, None
+            for j in (first_ref[i] + 2 * pair, first_ref[i] + 2 * pair + 1):
+                there = pl.ds(pl.multiple_of(jnp.minimum(j, i) * block, block), block)
+                _, _, kernel = scores(own[head], key_ref[there], ends_ref, i, j, block)
+                parts = [kernel[:, c * 128 : (c + 1) * 128] for c in range(block // 128)]
+                part = dot_nn(kernel.astype(jnp.bfloat16), qkv_ref[there, columns])
+                folded = sum(parts) if folded is None else folded + sum(parts)
+                numer = part if numer is None else numer + part
             sum_ref[:, pl.ds(head * 128, 128)] += folded
-            numer_ref[:, columns] += dot_nn(kernel.astype(jnp.bfloat16), qkv_ref[there, columns])
+            numer_ref[:, columns] += numer
         return carry
 
-    lax.fori_loop(first_ref[i], i + 1, step, 0)
+    lax.fori_loop(0, (i + 2 - first_ref[i]) // 2, step, 0)
     for head in range(2):
         columns = pl.ds(head * HEAD_V, HEAD_V)
         denom = jnp.sum(sum_ref[:, pl.ds(head * 128, 128)], axis=1, keepdims=True)
@@ -287,12 +290,18 @@
         ]
         for copy in copies:
             copy.start()
-        for copy in copies:
-            copy.wait()
 
     rows = rows_ref[...]
     for half in range(2):
         at = 2 * half * pieces
+
+        @pl.when(pl.program_id(0) == 0)
+        def _(half=half):
+            for i in (2 * half, 2 * half + 1):
+                pltpu.make_async_copy(
+                    weights[i], held.at[pl.ds(i * pieces, pieces)], sems.at[i]
+                ).wait()
+
         gate = dot_nt(held[pl.ds(at, pieces)], rows)
         up = dot_nt(held[pl.ds(at + pieces, pieces)], rows)
         grad = grad_ref[pl.ds(half * pieces, pieces)]
@@ -723,12 +732,13 @@
         qkv, mixed_heads, ratio, denom = attention_rows(
             first, halves_at, ends, stack_twin, stack_own, w_qkv
         )
-        mixed_heads, down_mine, wo_other = sync(mixed_heads, down_mine, wo_other)
+        mixed_heads, wo_other = sync(mixed_heads, wo_other)
         wo = jnp.concatenate([head_mine[qkv_size:head_size], wo_other], axis=0)
 
         from_twin = flip(product_rows(for_twin, mixed_heads, wo), "k")
+        from_twin, down_mine = sync(from_twin, down_mine)
         down_other = over_y(down_mine)
-        gate_mine = trade(after(gate_half, down_mine))
+        gate_mine = trade(after(gate_half, mixed_heads))
         (first_x, first_l), rest = scatter_first(
             product_rows(for_own, mixed_heads, wo), from_twin
         )

time: 733 us -> 732 us (level)
  starting transfers between devices: 111 us -> 121 us
  Pallas kernels: 176 us -> 168 us
    ppermute x9, waiting for transfers between devices: 62.6 us -> 33.2 us  [over_y(): return lax.ppermute(values, 'y', y_pairs)]
    ppermute x8, waiting for transfers between devices: 130 us -> 155 us  [trade(): return lax.ppermute(values, ('k', 'h'), [(0, 0), (1, 2), (2, 1), (3, 3)])]
    ppermute x4, starting transfers between devices: 23.6 us -> 37.4 us  [over_h(): return lax.ppermute(values, ('k', 'h'), [(1, 0), (2, 3)])]
    ppermute x8, starting transfers between devices: 33.6 us -> 45.6 us  [trade(): return lax.ppermute(values, ('k', 'h'), [(0, 0), (1, 2), (2, 1), (3, 3)])]
    ppermute x29, starting transfers between devices: 26.4 us -> 15.4 us  [flip(): return lax.ppermute(values, name, FLIP)]
    unnamed x159 -> x157, local copies, waits for them, and re-layouts: 52 us -> 50.2 us
  transfers between devices with their start and end apart: 66 -> 66, of which waited for: 24 -> 23; matrix products, arithmetic and copies ran while one was open for 10% -> 10% of each run, Pallas kernels for 21% -> 20%
where the time goes in v5:
time: 732 us; the launch traced here: 719 us
  waiting for transfers between devices  296 us (40%)
  Pallas kernels  168 us (23%)
  starting transfers between devices  121 us (17%)
  local copies, waits for them, and re-layouts  62.3 us (9%)
  other arithmetic  56.2 us (8%)
  between operations  15.6 us (2%)
    ppermute x8, waiting for transfers between devices, trade(): return lax.ppermute(values, ('k', 'h'), [(0, 0), (1, 2), (2, 1), (3, 3)])  155 us
    ppermute x29, waiting for transfers between devices, flip(): return lax.ppermute(values, name, FLIP)  101 us
    unnamed x157, local copies, waits for them, and re-layouts  50.2 us
    ppermute x8, starting transfers between devices, trade(): return lax.ppermute(values, ('k', 'h'), [(0, 0), (1, 2), (2, 1), (3, 3)])  45.6 us
    pallas_call x2, Pallas kernels, ffn_rows(): pl.pallas_call(functools.partial(ffn_kernel, pieces), out_shape=[jax.Shap...  41 us
    ppermute x4, starting transfers between devices, over_h(): return lax.ppermute(values, ('k', 'h'), [(1, 0), (2, 3)])  37.4 us
    ppermute x9, waiting for transfers between devices, over_y(): return lax.ppermute(values, 'y', y_pairs)  33.2 us
    pallas_call x6, Pallas kernels, unit_grad(): pl.pallas_call(functools.partial(unit_kernel, arrived is not None), out_s...  29 us
  transfers between devices with their start and end apart: 66, of which 23 were waited for; matrix products, arithmetic and copies ran while one was open for 10% of the time, Pallas kernels for 20%

profile of v5, /device:TPU:1, one launch (start us, length us, event | category | flops | bytes accessed | tf_op | source)
XLA Modules:
  0.0 718.7 jit_solution(11627604248325976195)
XLA Ops:
  27.4 9.7 %collective-permute-done = bf16[256,2048]{1,0:T(8,128)(2,1)} collective-permute-done((bf16[256,2048]{1,0:T(8,128)(2,1)}, bf16[256,2048]{1,0:T(8,128)(2,1)}, u32[]{:S(2)}, u32[]{:S(2)}) %collective-permute-start) | collective-permute-done | bytes 1048608 | tf_op jit(solution)/shard_map/ppermute | solution.py:584
  50.1 46.3 %collective-permute-done.4 = bf16[256,2048]{1,0:T(8,128)(2,1)S(1)} collective-permute-done((bf16[256,2048]{1,0:T(8,128)(2,1)S(1)}, bf16[256,2048]{1,0:T(8,128)(2,1)S(1)}, u32[]{:S(2)}, u32[]{:S(2)}) %collective-permute-start.4) | collective-permute-done | bytes 1048608 | tf_op jit(solution)/shard_map/ppermute | solution.py:584
  126.3 18.1 %attention_rows.1 = (bf16[2048,320]{1,0:T(8,128)(2,1)S(1)}, bf16[2048,256]{1,0:T(8,128)(2,1)S(1)}, f32[2048,256]{1,0:T(8,128)S(1)}, f32[2048,256]{1,0:T(8,128)S(1)}) custom-call(s32[8]{0:T(128)S(1)} %convert_reduce_fusion.2.first_ref, s32[8]{0:T(128)S(1)} %get-tuple-element.282.twin_at_ref, s32[8]{0:T(128)S(1)} %get-tuple-element.281.own_at_ref, ...), custom_call_target="tpu_custom_call" | custom-call | flops 1 | bytes 1 | tf_op jit(solution)/shard_map/attention_rows/pallas_call | solution.py:131
  155.8 29.9 %collective-permute-done.11.mine_ref = bf16[352,2048]{1,0:T(8,128)(2,1)S(1)} collective-permute-done((bf16[352,2048]{1,0:T(8,128)(2,1)S(1)}, bf16[352,2048]{1,0:T(8,128)(2,1)S(1)}, u32[]{:S(2)}, u32[]{:S(2)}) %collective-permute-start.11) | collective-permute-done | bytes 1441824 | tf_op jit(solution)/shard_map/ppermute | solution.py:584
  193.8 14.1 %collective-permute-done.12 = bf16[256,2048]{1,0:T(8,128)(2,1)S(1)} collective-permute-done((bf16[256,2048]{1,0:T(8,128)(2,1)S(1)}, bf16[256,2048]{1,0:T(8,128)(2,1)S(1)}, u32[]{:S(2)}, u32[]{:S(2)}) %collective-permute-start.12) | collective-permute-done | bytes 1048608 | tf_op jit(solution)/shard_map/ppermute | solution.py:661
  207.8 13.5 %collective-permute-done.13 = bf16[256,2048]{1,0:T(8,128)(2,1)S(1)} collective-permute-done((bf16[256,2048]{1,0:T(8,128)(2,1)S(1)}, bf16[256,2048]{1,0:T(8,128)(2,1)S(1)}, u32[]{:S(2)}, u32[]{:S(2)}) %collective-permute-start.13) | collective-permute-done | bytes 1048608 | tf_op jit(solution)/shard_map/ppermute | solution.py:661
  224.2 7.4 %collective-permute-done.15 = bf16[128,2048]{1,0:T(8,128)(2,1)S(1)} collective-permute-done((bf16[128,2048]{1,0:T(8,128)(2,1)S(1)}, bf16[128,2048]{1,0:T(8,128)(2,1)S(1)}, u32[]{:S(2)}, u32[]{:S(2)}) %collective-permute-start.15) | collective-permute-done | bytes 524320 | tf_op jit(solution)/shard_map/ppermute | solution.py:661
  241.3 38.3 %collective-permute-done.18.refs_1_ = bf16[352,2048]{1,0:T(8,128)(2,1)} collective-permute-done((bf16[352,2048]{1,0:T(8,128)(2,1)}, bf16[352,2048]{1,0:T(8,128)(2,1)}, u32[]{:S(2)}, u32[]{:S(2)}) %collective-permute-start.18) | collective-permute-done | bytes 1441824 | tf_op jit(solution)/shard_map/ppermute | solution.py:584
  283.2 7.1 hidden_grad.1.grad_ref
  299.3 20.5 %ffn_rows.2 = (bf16[1408,2048]{1,0:T(8,128)(2,1)}, bf16[704,2048]{1,0:T(8,128)(2,1)S(1)}, bf16[1024,2048]{1,0:T(8,128)(2,1)}) custom-call(s32[4]{0:T(128)S(1)} %get-tuple-element.279.order_ref, bf16[2048,2048]{1,0:T(8,128)(2,1)} %all-gather.4.cloned.1.call-done.rows_ref, f32[704,2048]{1,0:T(8,128)} %copy-done.8, ...), custom_call_target="tpu_custom_call" | custom-call | flops 1 | bytes 1 | tf_op jit(solution)/shard_map/ffn_rows/pallas_call | solution.py:324
  319.9 20.5 %ffn_rows.3 = (bf16[1408,2048]{1,0:T(8,128)(2,1)}, bf16[704,2048]{1,0:T(8,128)(2,1)S(1)}, bf16[1024,2048]{1,0:T(8,128)(2,1)}) custom-call(s32[4]{0:T(128)S(1)} %get-tuple-element.280.order_ref, bf16[2048,2048]{1,0:T(8,128)(2,1)} %all-gather.4.cloned.1.call-done.rows_ref, f32[704,2048]{1,0:T(8,128)} %copy-done.8, ...), custom_call_target="tpu_custom_call", output_to_operand_aliasing={{0}: (7, {}), {1}: (8, {})} | custom-call | flops 1 | bytes 1 | tf_op jit(solution)/shard_map/ffn_rows/pallas_call | solution.py:324
  410.3 8.3 %collective-permute-start.30 = (bf16[352,2048]{1,0:T(8,128)(2,1)S(1)}, bf16[352,2048]{1,0:T(8,128)(2,1)}, u32[]{:S(2)}, u32[]{:S(2)}) collective-permute-start(bf16[352,2048]{1,0:T(8,128)(2,1)S(1)} %unit_grad.9), channel_id=1, source_target_pairs={{4,0},{8,12},{5,1},{9,13},{6,2},{10,14},{7,3},{11,15},{20,16},{24,... | collective-permute-start | bytes 4325384 | tf_op jit(solution)/shard_map/ppermute | solution.py:590
  418.6 12.4 %collective-permute-done.29.refs_0_ = bf16[352,2048]{1,0:T(8,128)(2,1)S(1)} collective-permute-done((bf16[352,2048]{1,0:T(8,128)(2,1)}, bf16[352,2048]{1,0:T(8,128)(2,1)S(1)}, u32[]{:S(2)}, u32[]{:S(2)}) %collective-permute-start.29) | collective-permute-done | bytes 1441824 | tf_op jit(solution)/shard_map/ppermute | solution.py:587
  439.8 7.6 %collective-permute-start.31 = (bf16[352,2048]{1,0:T(8,128)(2,1)}, bf16[352,2048]{1,0:T(8,128)(2,1)}, u32[]{:S(2)}, u32[]{:S(2)}) collective-permute-start(bf16[352,2048]{1,0:T(8,128)(2,1)} %unit_grad.10), channel_id=1, source_target_pairs={{4,0},{8,12},{5,1},{9,13},{6,2},{10,14},{7,3},{11,15},{20,16},{24,... | collective-permute-start | bytes 4325384 | tf_op jit(solution)/shard_map/ppermute | solution.py:590
  447.5 14.4 %collective-permute-done.28.refs_0_ = bf16[352,2048]{1,0:T(8,128)(2,1)S(1)} collective-permute-done((bf16[352,2048]{1,0:T(8,128)(2,1)}, bf16[352,2048]{1,0:T(8,128)(2,1)S(1)}, u32[]{:S(2)}, u32[]{:S(2)}) %collective-permute-start.28) | collective-permute-done | bytes 1441824 | tf_op jit(solution)/shard_map/ppermute | solution.py:587
  475.7 23.6 %attention_back.1.rows_ref.qkv_ref = bf16[2048,320]{1,0:T(8,128)(2,1)S(1)} custom-call(s32[8]{0:T(128)S(1)} %convert_reduce_fusion.2.first_ref, s32[8]{0:T(128)S(1)} %fusion.20.place_ref, bf16[2048,2048]{1,0:T(8,128)(2,1)} %all-gather.8.cloned.1.call-done.attn_ref, bf16[256,2048]{1,0:T(8,128)(2,1)S(1)} %copy-done.15, bf16[2048,320]{1,0:T(8,128)(2,1)S(1)} %copy-done.32, ...), custom_call_target="tpu_custom_call" | custom-call | flops 1 | bytes 1 | tf_op jit(solution)/shard_map/attention_back/pallas_call | solution.py:245
  503.6 11.2 %collective-permute-start.35 = (bf16[352,2048]{1,0:T(8,128)(2,1)S(1)}, bf16[352,2048]{1,0:T(8,128)(2,1)S(1)}, u32[]{:S(2)}, u32[]{:S(2)}) collective-permute-start(bf16[352,2048]{1,0:T(8,128)(2,1)S(1)} %copy-done.19), channel_id=1, source_target_pairs={{4,0},{8,12},{5,1},{9,13},{6,2},{10,14},{7,3},{11,15},{20,16},{24,... | collective-permute-start | bytes 4325384 | tf_op jit(solution)/shard_map/ppermute | solution.py:590
  521.6 9.1 %head_grads.1 = (f32[288,2048]{1,0:T(8,128)S(1)}, bf16[288,2048]{1,0:T(8,128)(2,1)S(1)}, f32[1,2048]{1,0:T(1,128)S(1)}) custom-call(bf16[2048,320]{1,0:T(8,128)(2,1)S(1)} %attention_back.1.rows_ref.qkv_ref, bf16[1024,2048]{1,0:T(8,128)(2,1)} %collective-permute-done.8.twin_ref, bf16[1024,2048]{1,0:T(8,128)(2,1)} %constant_dynamic-update-slice_fusion.1.own_ref, ...), custom_call_target="tpu_custom_call" | custom-call | flops 1 | bytes 1 | tf_op jit(solution)/shard_map/head_grads/pallas_call | solution.py:467
  542.1 13.1 %collective-permute-done.34 = bf16[256,2048]{1,0:T(8,128)(2,1)S(1)} collective-permute-done((bf16[256,2048]{1,0:T(8,128)(2,1)S(1)}, bf16[256,2048]{1,0:T(8,128)(2,1)S(1)}, u32[]{:S(2)}, u32[]{:S(2)}) %collective-permute-start.34) | collective-permute-done | bytes 1048608 | tf_op jit(solution)/shard_map/ppermute | solution.py:661
  574.6 10.9 %collective-permute-start.38 = (bf16[256,2048]{1,0:T(8,128)(2,1)S(1)}, bf16[256,2048]{1,0:T(8,128)(2,1)}, u32[]{:S(2)}, u32[]{:S(2)}) collective-permute-start(bf16[256,2048]{1,0:T(8,128)(2,1)S(1)} %fusion.8), channel_id=1, source_target_pairs={{0,0},{4,8},{8,4},{12,12},{1,1},{5,9},{9,5},{13,13},{2,2},{6,10},{... | collective-permute-start | bytes 3145736 | tf_op jit(solution)/shard_map/ppermute | solution.py:584
  590.9 10.2 %collective-permute-start.40 = (bf16[288,2048]{1,0:T(8,128)(2,1)}, bf16[288,2048]{1,0:T(8,128)(2,1)}, u32[]{:S(2)}, u32[]{:S(2)}) collective-permute-start(bf16[288,2048]{1,0:T(8,128)(2,1)} %add_convert_fusion), channel_id=1, source_target_pairs={{4,0},{8,12},{5,1},{9,13},{6,2},{10,14},{7,3},{11,15},{20,16},{24,... | collective-permute-start | bytes 3538952 | tf_op jit(solution)/shard_map/ppermute | solution.py:590
  602.2 15.0 %collective-permute-done.38 = bf16[256,2048]{1,0:T(8,128)(2,1)} collective-permute-done((bf16[256,2048]{1,0:T(8,128)(2,1)S(1)}, bf16[256,2048]{1,0:T(8,128)(2,1)}, u32[]{:S(2)}, u32[]{:S(2)}) %collective-permute-start.38) | collective-permute-done | bytes 1048608 | tf_op jit(solution)/shard_map/ppermute | solution.py:584
  626.4 19.1 %collective-permute-done.42 = bf16[256,2048]{1,0:T(8,128)(2,1)} collective-permute-done((bf16[256,2048]{1,0:T(8,128)(2,1)}, bf16[256,2048]{1,0:T(8,128)(2,1)}, u32[]{:S(2)}, u32[]{:S(2)}) %collective-permute-start.42) | collective-permute-done | bytes 1048608 | tf_op jit(solution)/shard_map/ppermute | solution.py:661
  690.9 16.2 %collective-permute-done.52 = bf16[256,2048]{1,0:T(8,128)(2,1)S(1)} collective-permute-done((bf16[256,2048]{1,0:T(8,128)(2,1)S(1)}, bf16[256,2048]{1,0:T(8,128)(2,1)S(1)}, u32[]{:S(2)}, u32[]{:S(2)}) %collective-permute-start.52) | collective-permute-done | bytes 1048608 | tf_op jit(solution)/shard_map/ppermute | solution.py:584
  (372 shorter events, 306.5 us)
Async XLA Ops:
  7.2 272.5 %all-gather.6.cloned.1.call-start = ((), (), s32[]{:S(2)}) async-start(), calls=%async_computation.1 | async-start | bytes 9437184 | tf_op jit(solution)/shard_map/all_gather | solution.py:664
  41.2 55.3 %collective-permute-start.3 = (bf16[304,2048]{1,0:T(8,128)(2,1)}, bf16[304,2048]{1,0:T(8,128)(2,1)S(1)}, u32[]{:S(2)}, u32[]{:S(2)}) collective-permute-start(bf16[304,2048]{1,0:T(8,128)(2,1)} %constant_dynamic-update-slice_fusion), channel_id=1, source_target_pairs={{0,0},{4,8},{8,4},{12,12},{1,1},{5,9},{9,5},{13,13},{2,2},{6,10},{... | collective-permute-start | bytes 3735560 | tf_op jit(solution)/shard_map/ppermute | solution.py:584
  43.1 53.3 %collective-permute-start.4 = (bf16[256,2048]{1,0:T(8,128)(2,1)S(1)}, bf16[256,2048]{1,0:T(8,128)(2,1)S(1)}, u32[]{:S(2)}, u32[]{:S(2)}) collective-permute-start(bf16[256,2048]{1,0:T(8,128)(2,1)S(1)} %copy-done.64), channel_id=1, source_target_pairs={{0,0},{4,8},{8,4},{12,12},{1,1},{5,9},{9,5},{13,13},{2,2},{6,10},{... | collective-permute-start | bytes 3145736 | tf_op jit(solution)/shard_map/ppermute | solution.py:584
  47.7 48.8 %collective-permute-start.2 = (bf16[256,2048]{1,0:T(8,128)(2,1)}, bf16[256,2048]{1,0:T(8,128)(2,1)}, u32[]{:S(2)}, u32[]{:S(2)}) collective-permute-start(bf16[256,2048]{1,0:T(8,128)(2,1)} %fusion.3), channel_id=1, source_target_pairs={{0,2},{2,0},{1,3},{3,1},{4,6},{6,4},{5,7},{7,5},{8,10},{10,8},{9,1... | collective-permute-start | bytes 3145736 | tf_op jit(solution)/shard_map/ppermute | solution.py:661
  48.9 47.5 %collective-permute-start.1 = (bf16[256,2048]{1,0:T(8,128)(2,1)}, bf16[256,2048]{1,0:T(8,128)(2,1)}, u32[]{:S(2)}, u32[]{:S(2)}) collective-permute-start(bf16[256,2048]{1,0:T(8,128)(2,1)} %fusion.3), channel_id=1, source_target_pairs={{0,1},{1,0},{2,3},{3,2},{4,5},{5,4},{6,7},{7,6},{8,9},{9,8},{10,11... | collective-permute-start | bytes 3145736 | tf_op jit(solution)/shard_map/ppermute | solution.py:661
  101.9 197.4 %all-gather.4.cloned.1.call-start = ((), (), s32[]{:S(2)}) async-start(), calls=%async_computation | async-start | bytes 9437184 | tf_op jit(solution)/shard_map/all_gather | solution.py:664
  147.0 38.7 %collective-permute-start.10 = (bf16[1024,2048]{1,0:T(8,128)(2,1)S(1)}, bf16[1024,2048]{1,0:T(8,128)(2,1)S(1)}, u32[]{:S(2)}, u32[]{:S(2)}) collective-permute-start(bf16[1024,2048]{1,0:T(8,128)(2,1)S(1)} %product_rows.7), channel_id=1, source_target_pairs={{0,8},{8,0},{1,9},{9,1},{2,10},{10,2},{3,11},{11,3},{4,12},{12,4},... | collective-permute-start | bytes 12582920 | tf_op jit(solution)/shard_map/ppermute | solution.py:661
  147.0 38.7 %collective-permute-start.11 = (bf16[352,2048]{1,0:T(8,128)(2,1)S(1)}, bf16[352,2048]{1,0:T(8,128)(2,1)S(1)}, u32[]{:S(2)}, u32[]{:S(2)}) collective-permute-start(bf16[352,2048]{1,0:T(8,128)(2,1)S(1)} %copy-done.54), channel_id=1, source_target_pairs={{0,0},{4,8},{8,4},{12,12},{1,1},{5,9},{9,5},{13,13},{2,2},{6,10},{... | collective-permute-start | bytes 4325384 | tf_op jit(solution)/shard_map/ppermute | solution.py:584
  189.3 43.0 %collective-permute-start.17 = (bf16[352,2048]{1,0:T(8,128)(2,1)S(1)}, bf16[352,2048]{1,0:T(8,128)(2,1)}, u32[]{:S(2)}, u32[]{:S(2)}) collective-permute-start(bf16[352,2048]{1,0:T(8,128)(2,1)S(1)} %copy-done.55), channel_id=1, source_target_pairs={{0,0},{4,8},{8,4},{12,12},{1,1},{5,9},{9,5},{13,13},{2,2},{6,10},{... | collective-permute-start | bytes 4325384 | tf_op jit(solution)/shard_map/ppermute | solution.py:584
  236.6 234.5 %all-gather.8.cloned.1.call-start = ((), (), s32[]{:S(2)}) async-start(), calls=%async_computation.2 | async-start | bytes 9437184 | tf_op jit(solution)/shard_map/all_gather | solution.py:664
  236.6 43.0 %collective-permute-start.18 = (bf16[352,2048]{1,0:T(8,128)(2,1)}, bf16[352,2048]{1,0:T(8,128)(2,1)}, u32[]{:S(2)}, u32[]{:S(2)}) collective-permute-start(bf16[352,2048]{1,0:T(8,128)(2,1)} %get-tuple-element.153), channel_id=1, source_target_pairs={{0,0},{4,8},{8,4},{12,12},{1,1},{5,9},{9,5},{13,13},{2,2},{6,10},{... | collective-permute-start | bytes 4325384 | tf_op jit(solution)/shard_map/ppermute | solution.py:584
  241.2 51.6 %collective-permute-start.20 = (bf16[352,2048]{1,0:T(8,128)(2,1)}, bf16[352,2048]{1,0:T(8,128)(2,1)}, u32[]{:S(2)}, u32[]{:S(2)}) collective-permute-start(bf16[352,2048]{1,0:T(8,128)(2,1)} %collective-permute-done.17.refs_0_), channel_id=1, source_target_pairs={{0,16},{16,0},{1,17},{17,1},{2,18},{18,2},{3,19},{19,3},{4,20},{20... | collective-permute-start | bytes 4325384 | tf_op jit(solution)/shard_map/ppermute | solution.py:587
  351.7 38.6 %collective-permute-start.26 = (bf16[352,2048]{1,0:T(8,128)(2,1)S(1)}, bf16[352,2048]{1,0:T(8,128)(2,1)S(1)}, u32[]{:S(2)}, u32[]{:S(2)}) collective-permute-start(bf16[352,2048]{1,0:T(8,128)(2,1)S(1)} %unit_grad.6), channel_id=1, source_target_pairs={{0,16},{16,0},{1,17},{17,1},{2,18},{18,2},{3,19},{19,3},{4,20},{20... | collective-permute-start | bytes 4325384 | tf_op jit(solution)/shard_map/ppermute | solution.py:587
  395.2 71.2 %collective-permute-start.27 = (bf16[1024,2048]{1,0:T(8,128)(2,1)}, bf16[1024,2048]{1,0:T(8,128)(2,1)S(1)}, u32[]{:S(2)}, u32[]{:S(2)}) collective-permute-start(bf16[1024,2048]{1,0:T(8,128)(2,1)} %copy-done.26), channel_id=1, source_target_pairs={{0,8},{8,0},{1,9},{9,1},{2,10},{10,2},{3,11},{11,3},{4,12},{12,4},... | collective-permute-start | bytes 12582920 | tf_op jit(solution)/shard_map/ppermute | solution.py:661
  397.6 64.3 %collective-permute-start.28 = (bf16[352,2048]{1,0:T(8,128)(2,1)}, bf16[352,2048]{1,0:T(8,128)(2,1)S(1)}, u32[]{:S(2)}, u32[]{:S(2)}) collective-permute-start(bf16[352,2048]{1,0:T(8,128)(2,1)} %unit_grad.8), channel_id=1, source_target_pairs={{0,16},{16,0},{1,17},{17,1},{2,18},{18,2},{3,19},{19,3},{4,20},{20... | collective-permute-start | bytes 4325384 | tf_op jit(solution)/shard_map/ppermute | solution.py:587
  410.3 89.0 %collective-permute-start.30 = (bf16[352,2048]{1,0:T(8,128)(2,1)S(1)}, bf16[352,2048]{1,0:T(8,128)(2,1)}, u32[]{:S(2)}, u32[]{:S(2)}) collective-permute-start(bf16[352,2048]{1,0:T(8,128)(2,1)S(1)} %unit_grad.9), channel_id=1, source_target_pairs={{4,0},{8,12},{5,1},{9,13},{6,2},{10,14},{7,3},{11,15},{20,16},{24,... | collective-permute-start | bytes 4325384 | tf_op jit(solution)/shard_map/ppermute | solution.py:590
  439.8 59.5 %collective-permute-start.31 = (bf16[352,2048]{1,0:T(8,128)(2,1)}, bf16[352,2048]{1,0:T(8,128)(2,1)}, u32[]{:S(2)}, u32[]{:S(2)}) collective-permute-start(bf16[352,2048]{1,0:T(8,128)(2,1)} %unit_grad.10), channel_id=1, source_target_pairs={{4,0},{8,12},{5,1},{9,13},{6,2},{10,14},{7,3},{11,15},{20,16},{24,... | collective-permute-start | bytes 4325384 | tf_op jit(solution)/shard_map/ppermute | solution.py:590
  530.7 43.9 %collective-permute-start.39 = (bf16[288,2048]{1,0:T(8,128)(2,1)S(1)}, bf16[288,2048]{1,0:T(8,128)(2,1)S(1)}, u32[]{:S(2)}, u32[]{:S(2)}) collective-permute-start(bf16[288,2048]{1,0:T(8,128)(2,1)S(1)} %get-tuple-element.205), channel_id=1, source_target_pairs={{0,16},{16,0},{1,17},{17,1},{2,18},{18,2},{3,19},{19,3},{4,20},{20... | collective-permute-start | bytes 3538952 | tf_op jit(solution)/shard_map/ppermute | solution.py:587
  532.9 52.7 %collective-permute-start.44 = (bf16[352,2048]{1,0:T(8,128)(2,1)S(1)}, bf16[352,2048]{1,0:T(8,128)(2,1)}, u32[]{:S(2)}, u32[]{:S(2)}) collective-permute-start(bf16[352,2048]{1,0:T(8,128)(2,1)S(1)} %add.358.mine_ref), channel_id=1, source_target_pairs={{0,16},{12,28},{16,0},{28,12},{1,17},{13,29},{17,1},{29,13},{2,18}... | collective-permute-start | bytes 4325384 | tf_op jit(solution)/shard_map/ppermute | solution.py:593
  540.8 49.0 %collective-permute-start.43 = (bf16[352,2048]{1,0:T(8,128)(2,1)S(1)}, bf16[352,2048]{1,0:T(8,128)(2,1)S(1)}, u32[]{:S(2)}, u32[]{:S(2)}) collective-permute-start(bf16[352,2048]{1,0:T(8,128)(2,1)S(1)} %add.358.mine_ref), channel_id=1, source_target_pairs={{0,8},{12,4},{1,9},{13,5},{2,10},{14,6},{3,11},{15,7},{16,24},{28,... | collective-permute-start | bytes 4325384 | tf_op jit(solution)/shard_map/ppermute | solution.py:596
  574.6 42.6 %collective-permute-start.38 = (bf16[256,2048]{1,0:T(8,128)(2,1)S(1)}, bf16[256,2048]{1,0:T(8,128)(2,1)}, u32[]{:S(2)}, u32[]{:S(2)}) collective-permute-start(bf16[256,2048]{1,0:T(8,128)(2,1)S(1)} %fusion.8), channel_id=1, source_target_pairs={{0,0},{4,8},{8,4},{12,12},{1,1},{5,9},{9,5},{13,13},{2,2},{6,10},{... | collective-permute-start | bytes 3145736 | tf_op jit(solution)/shard_map/ppermute | solution.py:584
  585.6 59.9 %collective-permute-start.45 = (bf16[352,2048]{1,0:T(8,128)(2,1)}, bf16[352,2048]{1,0:T(8,128)(2,1)}, u32[]{:S(2)}, u32[]{:S(2)}) collective-permute-start(bf16[352,2048]{1,0:T(8,128)(2,1)} %collective-permute-done.44.theirs_ref), channel_id=1, source_target_pairs={{0,8},{12,4},{1,9},{13,5},{2,10},{14,6},{3,11},{15,7},{16,24},{28,... | collective-permute-start | bytes 4325384 | tf_op jit(solution)/shard_map/ppermute | solution.py:596
  587.0 58.5 %collective-permute-start.48 = (bf16[352,2048]{1,0:T(8,128)(2,1)}, bf16[352,2048]{1,0:T(8,128)(2,1)}, u32[]{:S(2)}, u32[]{:S(2)}) collective-permute-start(bf16[352,2048]{1,0:T(8,128)(2,1)} %collective-permute-done.47.theirs_ref), channel_id=1, source_target_pairs={{0,8},{12,4},{1,9},{13,5},{2,10},{14,6},{3,11},{15,7},{16,24},{28,... | collective-permute-start | bytes 4325384 | tf_op jit(solution)/shard_map/ppermute | solution.py:596
  590.9 54.6 %collective-permute-start.40 = (bf16[288,2048]{1,0:T(8,128)(2,1)}, bf16[288,2048]{1,0:T(8,128)(2,1)}, u32[]{:S(2)}, u32[]{:S(2)}) collective-permute-start(bf16[288,2048]{1,0:T(8,128)(2,1)} %add_convert_fusion), channel_id=1, source_target_pairs={{4,0},{8,12},{5,1},{9,13},{6,2},{10,14},{7,3},{11,15},{20,16},{24,... | collective-permute-start | bytes 3538952 | tf_op jit(solution)/shard_map/ppermute | solution.py:590
  (113 other events, 1593.2 us)
Sparse Core Ops, SparseCore 0:
  102.0 49.9 all-gather.5
  236.7 61.7 all-gather.3
  395.3 70.6 all-gather.7

commit v6 on v5

--- a/solution.py
+++ b/solution.py
@@ -738,7 +738,7 @@
         from_twin = flip(product_rows(for_twin, mixed_heads, wo), "k")
         from_twin, down_mine = sync(from_twin, down_mine)
         down_other = over_y(down_mine)
-        gate_mine = trade(after(gate_half, mixed_heads))
+        gate_mine = trade(after(gate_half, down_mine))
         (first_x, first_l), rest = scatter_first(
             product_rows(for_own, mixed_heads, wo), from_twin
         )

time: 732 us -> 731 us (level)
    ppermute x29, waiting for transfers between devices: 101 us -> 110 us  [flip(): return lax.ppermute(values, name, FLIP)]
    ppermute x8, starting transfers between devices: 45.6 us -> 38.1 us  [trade(): return lax.ppermute(values, ('k', 'h'), [(0, 0), (1, 2), (2, 1), (3, 3)])]
  transfers between devices with their start and end apart: 66 -> 66, of which waited for: 23 -> 24; matrix products, arithmetic and copies ran while one was open for 10% -> 9% of each run, Pallas kernels for 20% -> 19%
where the time goes in v6:
time: 731 us; the launch traced here: 719 us
  waiting for transfers between devices  297 us (41%)
  Pallas kernels  168 us (23%)
  starting transfers between devices  120 us (16%)
  local copies, waits for them, and re-layouts  62.3 us (9%)
  other arithmetic  56.1 us (8%)
  between operations  15.6 us (2%)
    ppermute x8, waiting for transfers between devices, trade(): return lax.ppermute(values, ('k', 'h'), [(0, 0), (1, 2), (2, 1), (3, 3)])  150 us
    ppermute x29, waiting for transfers between devices, flip(): return lax.ppermute(values, name, FLIP)  110 us
    unnamed x157, local copies, waits for them, and re-layouts  50.2 us
    pallas_call x2, Pallas kernels, ffn_rows(): pl.pallas_call(functools.partial(ffn_kernel, pieces), out_shape=[jax.Shap...  41.1 us
    ppermute x8, starting transfers between devices, trade(): return lax.ppermute(values, ('k', 'h'), [(0, 0), (1, 2), (2, 1), (3, 3)])  38.1 us
    ppermute x9, waiting for transfers between devices, over_y(): return lax.ppermute(values, 'y', y_pairs)  34.2 us
    ppermute x4, starting transfers between devices, over_h(): return lax.ppermute(values, ('k', 'h'), [(1, 0), (2, 3)])  33.8 us
    pallas_call x6, Pallas kernels, unit_grad(): pl.pallas_call(functools.partial(unit_kernel, arrived is not None), out_s...  29 us
  transfers between devices with their start and end apart: 66, of which 24 were waited for; matrix products, arithmetic and copies ran while one was open for 9% of the time, Pallas kernels for 19%

profile of v6, /device:TPU:1, one launch (start us, length us, event | category | flops | bytes accessed | tf_op | source)
XLA Modules:
  0.0 719.2 jit_solution(11627604248325976195)
XLA Ops:
  27.4 9.7 %collective-permute-done = bf16[256,2048]{1,0:T(8,128)(2,1)} collective-permute-done((bf16[256,2048]{1,0:T(8,128)(2,1)}, bf16[256,2048]{1,0:T(8,128)(2,1)}, u32[]{:S(2)}, u32[]{:S(2)}) %collective-permute-start) | collective-permute-done | bytes 1048608 | tf_op jit(solution)/shard_map/ppermute | solution.py:584
  50.1 46.3 %collective-permute-done.4 = bf16[256,2048]{1,0:T(8,128)(2,1)S(1)} collective-permute-done((bf16[256,2048]{1,0:T(8,128)(2,1)S(1)}, bf16[256,2048]{1,0:T(8,128)(2,1)S(1)}, u32[]{:S(2)}, u32[]{:S(2)}) %collective-permute-start.4) | collective-permute-done | bytes 1048608 | tf_op jit(solution)/shard_map/ppermute | solution.py:584
  126.3 18.1 %attention_rows.1 = (bf16[2048,320]{1,0:T(8,128)(2,1)S(1)}, bf16[2048,256]{1,0:T(8,128)(2,1)S(1)}, f32[2048,256]{1,0:T(8,128)S(1)}, f32[2048,256]{1,0:T(8,128)S(1)}) custom-call(s32[8]{0:T(128)S(1)} %convert_reduce_fusion.2.first_ref, s32[8]{0:T(128)S(1)} %get-tuple-element.282.twin_at_ref, s32[8]{0:T(128)S(1)} %get-tuple-element.281.own_at_ref, ...), custom_call_target="tpu_custom_call" | custom-call | flops 1 | bytes 1 | tf_op jit(solution)/shard_map/attention_rows/pallas_call | solution.py:131
  153.5 30.3 %collective-permute-done.11.mine_ref = bf16[352,2048]{1,0:T(8,128)(2,1)S(1)} collective-permute-done((bf16[352,2048]{1,0:T(8,128)(2,1)S(1)}, bf16[352,2048]{1,0:T(8,128)(2,1)S(1)}, u32[]{:S(2)}, u32[]{:S(2)}) %collective-permute-start.11) | collective-permute-done | bytes 1441824 | tf_op jit(solution)/shard_map/ppermute | solution.py:584
  193.8 14.0 %collective-permute-done.12 = bf16[256,2048]{1,0:T(8,128)(2,1)S(1)} collective-permute-done((bf16[256,2048]{1,0:T(8,128)(2,1)S(1)}, bf16[256,2048]{1,0:T(8,128)(2,1)S(1)}, u32[]{:S(2)}, u32[]{:S(2)}) %collective-permute-start.12) | collective-permute-done | bytes 1048608 | tf_op jit(solution)/shard_map/ppermute | solution.py:661
  207.8 13.5 %collective-permute-done.13 = bf16[256,2048]{1,0:T(8,128)(2,1)S(1)} collective-permute-done((bf16[256,2048]{1,0:T(8,128)(2,1)S(1)}, bf16[256,2048]{1,0:T(8,128)(2,1)S(1)}, u32[]{:S(2)}, u32[]{:S(2)}) %collective-permute-start.13) | collective-permute-done | bytes 1048608 | tf_op jit(solution)/shard_map/ppermute | solution.py:661
  224.5 7.1 collective-permute-done.15
  241.6 38.4 %collective-permute-done.18.refs_1_ = bf16[352,2048]{1,0:T(8,128)(2,1)} collective-permute-done((bf16[352,2048]{1,0:T(8,128)(2,1)}, bf16[352,2048]{1,0:T(8,128)(2,1)}, u32[]{:S(2)}, u32[]{:S(2)}) %collective-permute-start.18) | collective-permute-done | bytes 1441824 | tf_op jit(solution)/shard_map/ppermute | solution.py:584
  299.8 20.5 %ffn_rows.2 = (bf16[1408,2048]{1,0:T(8,128)(2,1)}, bf16[704,2048]{1,0:T(8,128)(2,1)S(1)}, bf16[1024,2048]{1,0:T(8,128)(2,1)}) custom-call(s32[4]{0:T(128)S(1)} %get-tuple-element.279.order_ref, bf16[2048,2048]{1,0:T(8,128)(2,1)} %all-gather.4.cloned.1.call-done.rows_ref, f32[704,2048]{1,0:T(8,128)} %copy-done.8, ...), custom_call_target="tpu_custom_call" | custom-call | flops 1 | bytes 1 | tf_op jit(solution)/shard_map/ffn_rows/pallas_call | solution.py:324
  320.4 20.6 %ffn_rows.3 = (bf16[1408,2048]{1,0:T(8,128)(2,1)}, bf16[704,2048]{1,0:T(8,128)(2,1)S(1)}, bf16[1024,2048]{1,0:T(8,128)(2,1)}) custom-call(s32[4]{0:T(128)S(1)} %get-tuple-element.280.order_ref, bf16[2048,2048]{1,0:T(8,128)(2,1)} %all-gather.4.cloned.1.call-done.rows_ref, f32[704,2048]{1,0:T(8,128)} %copy-done.8, ...), custom_call_target="tpu_custom_call", output_to_operand_aliasing={{0}: (7, {}), {1}: (8, {})} | custom-call | flops 1 | bytes 1 | tf_op jit(solution)/shard_map/ffn_rows/pallas_call | solution.py:324
  411.2 7.8 %collective-permute-start.30 = (bf16[352,2048]{1,0:T(8,128)(2,1)S(1)}, bf16[352,2048]{1,0:T(8,128)(2,1)}, u32[]{:S(2)}, u32[]{:S(2)}) collective-permute-start(bf16[352,2048]{1,0:T(8,128)(2,1)S(1)} %unit_grad.9), channel_id=1, source_target_pairs={{4,0},{8,12},{5,1},{9,13},{6,2},{10,14},{7,3},{11,15},{20,16},{24,... | collective-permute-start | bytes 4325384 | tf_op jit(solution)/shard_map/ppermute | solution.py:590
  419.0 12.8 %collective-permute-done.29.refs_0_ = bf16[352,2048]{1,0:T(8,128)(2,1)S(1)} collective-permute-done((bf16[352,2048]{1,0:T(8,128)(2,1)}, bf16[352,2048]{1,0:T(8,128)(2,1)S(1)}, u32[]{:S(2)}, u32[]{:S(2)}) %collective-permute-start.29) | collective-permute-done | bytes 1441824 | tf_op jit(solution)/shard_map/ppermute | solution.py:587
  440.5 7.4 %collective-permute-start.31 = (bf16[352,2048]{1,0:T(8,128)(2,1)}, bf16[352,2048]{1,0:T(8,128)(2,1)}, u32[]{:S(2)}, u32[]{:S(2)}) collective-permute-start(bf16[352,2048]{1,0:T(8,128)(2,1)} %unit_grad.10), channel_id=1, source_target_pairs={{4,0},{8,12},{5,1},{9,13},{6,2},{10,14},{7,3},{11,15},{20,16},{24,... | collective-permute-start | bytes 4325384 | tf_op jit(solution)/shard_map/ppermute | solution.py:590
  447.9 14.8 %collective-permute-done.28.refs_0_ = bf16[352,2048]{1,0:T(8,128)(2,1)S(1)} collective-permute-done((bf16[352,2048]{1,0:T(8,128)(2,1)}, bf16[352,2048]{1,0:T(8,128)(2,1)S(1)}, u32[]{:S(2)}, u32[]{:S(2)}) %collective-permute-start.28) | collective-permute-done | bytes 1441824 | tf_op jit(solution)/shard_map/ppermute | solution.py:587
  476.5 23.6 %attention_back.1.rows_ref.qkv_ref = bf16[2048,320]{1,0:T(8,128)(2,1)S(1)} custom-call(s32[8]{0:T(128)S(1)} %convert_reduce_fusion.2.first_ref, s32[8]{0:T(128)S(1)} %fusion.20.place_ref, bf16[2048,2048]{1,0:T(8,128)(2,1)} %all-gather.8.cloned.1.call-done.attn_ref, bf16[256,2048]{1,0:T(8,128)(2,1)S(1)} %copy-done.15, bf16[2048,320]{1,0:T(8,128)(2,1)S(1)} %copy-done.32, ...), custom_call_target="tpu_custom_call" | custom-call | flops 1 | bytes 1 | tf_op jit(solution)/shard_map/attention_back/pallas_call | solution.py:245
  517.4 9.1 %head_grads.1 = (f32[288,2048]{1,0:T(8,128)S(1)}, bf16[288,2048]{1,0:T(8,128)(2,1)S(1)}, f32[1,2048]{1,0:T(1,128)S(1)}) custom-call(bf16[2048,320]{1,0:T(8,128)(2,1)S(1)} %attention_back.1.rows_ref.qkv_ref, bf16[1024,2048]{1,0:T(8,128)(2,1)} %collective-permute-done.8.twin_ref, bf16[1024,2048]{1,0:T(8,128)(2,1)} %constant_dynamic-update-slice_fusion.1.own_ref, ...), custom_call_target="tpu_custom_call" | custom-call | flops 1 | bytes 1 | tf_op jit(solution)/shard_map/head_grads/pallas_call | solution.py:467
  539.0 15.9 %collective-permute-done.34 = bf16[256,2048]{1,0:T(8,128)(2,1)S(1)} collective-permute-done((bf16[256,2048]{1,0:T(8,128)(2,1)S(1)}, bf16[256,2048]{1,0:T(8,128)(2,1)S(1)}, u32[]{:S(2)}, u32[]{:S(2)}) %collective-permute-start.34) | collective-permute-done | bytes 1048608 | tf_op jit(solution)/shard_map/ppermute | solution.py:661
  559.3 9.8 %collective-permute-done.36 = bf16[128,2048]{1,0:T(8,128)(2,1)S(1)} collective-permute-done((bf16[128,2048]{1,0:T(8,128)(2,1)S(1)}, bf16[128,2048]{1,0:T(8,128)(2,1)S(1)}, u32[]{:S(2)}, u32[]{:S(2)}) %collective-permute-start.36) | collective-permute-done | bytes 524320 | tf_op jit(solution)/shard_map/ppermute | solution.py:661
  588.6 12.4 %collective-permute-start.40 = (bf16[288,2048]{1,0:T(8,128)(2,1)}, bf16[288,2048]{1,0:T(8,128)(2,1)}, u32[]{:S(2)}, u32[]{:S(2)}) collective-permute-start(bf16[288,2048]{1,0:T(8,128)(2,1)} %add_convert_fusion), channel_id=1, source_target_pairs={{4,0},{8,12},{5,1},{9,13},{6,2},{10,14},{7,3},{11,15},{20,16},{24,... | collective-permute-start | bytes 3538952 | tf_op jit(solution)/shard_map/ppermute | solution.py:590
  602.1 8.5 %collective-permute-done.38 = bf16[256,2048]{1,0:T(8,128)(2,1)} collective-permute-done((bf16[256,2048]{1,0:T(8,128)(2,1)S(1)}, bf16[256,2048]{1,0:T(8,128)(2,1)}, u32[]{:S(2)}, u32[]{:S(2)}) %collective-permute-start.38) | collective-permute-done | bytes 1048608 | tf_op jit(solution)/shard_map/ppermute | solution.py:584
  612.3 13.0 %collective-permute-done.41 = bf16[256,2048]{1,0:T(8,128)(2,1)S(1)} collective-permute-done((bf16[256,2048]{1,0:T(8,128)(2,1)S(1)}, bf16[256,2048]{1,0:T(8,128)(2,1)S(1)}, u32[]{:S(2)}, u32[]{:S(2)}) %collective-permute-start.41) | collective-permute-done | bytes 1048608 | tf_op jit(solution)/shard_map/ppermute | solution.py:661
  626.8 15.4 %collective-permute-done.42 = bf16[256,2048]{1,0:T(8,128)(2,1)} collective-permute-done((bf16[256,2048]{1,0:T(8,128)(2,1)}, bf16[256,2048]{1,0:T(8,128)(2,1)}, u32[]{:S(2)}, u32[]{:S(2)}) %collective-permute-start.42) | collective-permute-done | bytes 1048608 | tf_op jit(solution)/shard_map/ppermute | solution.py:661
  677.1 7.5 %collective-permute-start.52 = (bf16[256,2048]{1,0:T(8,128)(2,1)S(1)}, bf16[256,2048]{1,0:T(8,128)(2,1)S(1)}, u32[]{:S(2)}, u32[]{:S(2)}) collective-permute-start(bf16[256,2048]{1,0:T(8,128)(2,1)S(1)} %fusion.10), channel_id=1, source_target_pairs={{0,0},{4,8},{8,4},{12,12},{1,1},{5,9},{9,5},{13,13},{2,2},{6,10},{... | collective-permute-start | bytes 3145736 | tf_op jit(solution)/shard_map/ppermute | solution.py:584
  691.5 16.2 %collective-permute-done.52 = bf16[256,2048]{1,0:T(8,128)(2,1)S(1)} collective-permute-done((bf16[256,2048]{1,0:T(8,128)(2,1)S(1)}, bf16[256,2048]{1,0:T(8,128)(2,1)S(1)}, u32[]{:S(2)}, u32[]{:S(2)}) %collective-permute-start.52) | collective-permute-done | bytes 1048608 | tf_op jit(solution)/shard_map/ppermute | solution.py:584
  (372 shorter events, 310.7 us)
Async XLA Ops:
  7.2 272.9 %all-gather.6.cloned.1.call-start = ((), (), s32[]{:S(2)}) async-start(), calls=%async_computation.1 | async-start | bytes 9437184 | tf_op jit(solution)/shard_map/all_gather | solution.py:664
  41.2 55.3 %collective-permute-start.3 = (bf16[304,2048]{1,0:T(8,128)(2,1)}, bf16[304,2048]{1,0:T(8,128)(2,1)S(1)}, u32[]{:S(2)}, u32[]{:S(2)}) collective-permute-start(bf16[304,2048]{1,0:T(8,128)(2,1)} %constant_dynamic-update-slice_fusion), channel_id=1, source_target_pairs={{0,0},{4,8},{8,4},{12,12},{1,1},{5,9},{9,5},{13,13},{2,2},{6,10},{... | collective-permute-start | bytes 3735560 | tf_op jit(solution)/shard_map/ppermute | solution.py:584
  43.1 53.3 %collective-permute-start.4 = (bf16[256,2048]{1,0:T(8,128)(2,1)S(1)}, bf16[256,2048]{1,0:T(8,128)(2,1)S(1)}, u32[]{:S(2)}, u32[]{:S(2)}) collective-permute-start(bf16[256,2048]{1,0:T(8,128)(2,1)S(1)} %copy-done.64), channel_id=1, source_target_pairs={{0,0},{4,8},{8,4},{12,12},{1,1},{5,9},{9,5},{13,13},{2,2},{6,10},{... | collective-permute-start | bytes 3145736 | tf_op jit(solution)/shard_map/ppermute | solution.py:584
  47.7 48.8 %collective-permute-start.2 = (bf16[256,2048]{1,0:T(8,128)(2,1)}, bf16[256,2048]{1,0:T(8,128)(2,1)}, u32[]{:S(2)}, u32[]{:S(2)}) collective-permute-start(bf16[256,2048]{1,0:T(8,128)(2,1)} %fusion.3), channel_id=1, source_target_pairs={{0,2},{2,0},{1,3},{3,1},{4,6},{6,4},{5,7},{7,5},{8,10},{10,8},{9,1... | collective-permute-start | bytes 3145736 | tf_op jit(solution)/shard_map/ppermute | solution.py:661
  48.9 47.5 %collective-permute-start.1 = (bf16[256,2048]{1,0:T(8,128)(2,1)}, bf16[256,2048]{1,0:T(8,128)(2,1)}, u32[]{:S(2)}, u32[]{:S(2)}) collective-permute-start(bf16[256,2048]{1,0:T(8,128)(2,1)} %fusion.3), channel_id=1, source_target_pairs={{0,1},{1,0},{2,3},{3,2},{4,5},{5,4},{6,7},{7,6},{8,9},{9,8},{10,11... | collective-permute-start | bytes 3145736 | tf_op jit(solution)/shard_map/ppermute | solution.py:661
  101.9 197.9 %all-gather.4.cloned.1.call-start = ((), (), s32[]{:S(2)}) async-start(), calls=%async_computation | async-start | bytes 9437184 | tf_op jit(solution)/shard_map/all_gather | solution.py:664
  183.8 37.5 %collective-permute-start.14 = (bf16[352,2048]{1,0:T(8,128)(2,1)S(1)}, bf16[352,2048]{1,0:T(8,128)(2,1)S(1)}, u32[]{:S(2)}, u32[]{:S(2)}) collective-permute-start(bf16[352,2048]{1,0:T(8,128)(2,1)S(1)} %collective-permute-done.11.mine_ref), channel_id=1, source_target_pairs={{0,16},{16,0},{1,17},{17,1},{2,18},{18,2},{3,19},{19,3},{4,20},{20... | collective-permute-start | bytes 4325384 | tf_op jit(solution)/shard_map/ppermute | solution.py:587
  189.3 43.0 %collective-permute-start.17 = (bf16[352,2048]{1,0:T(8,128)(2,1)S(1)}, bf16[352,2048]{1,0:T(8,128)(2,1)}, u32[]{:S(2)}, u32[]{:S(2)}) collective-permute-start(bf16[352,2048]{1,0:T(8,128)(2,1)S(1)} %copy-done.55), channel_id=1, source_target_pairs={{0,0},{4,8},{8,4},{12,12},{1,1},{5,9},{9,5},{13,13},{2,2},{6,10},{... | collective-permute-start | bytes 4325384 | tf_op jit(solution)/shard_map/ppermute | solution.py:584
  236.6 235.3 %all-gather.8.cloned.1.call-start = ((), (), s32[]{:S(2)}) async-start(), calls=%async_computation.2 | async-start | bytes 9437184 | tf_op jit(solution)/shard_map/all_gather | solution.py:664
  236.6 43.4 %collective-permute-start.18 = (bf16[352,2048]{1,0:T(8,128)(2,1)}, bf16[352,2048]{1,0:T(8,128)(2,1)}, u32[]{:S(2)}, u32[]{:S(2)}) collective-permute-start(bf16[352,2048]{1,0:T(8,128)(2,1)} %get-tuple-element.153), channel_id=1, source_target_pairs={{0,0},{4,8},{8,4},{12,12},{1,1},{5,9},{9,5},{13,13},{2,2},{6,10},{... | collective-permute-start | bytes 4325384 | tf_op jit(solution)/shard_map/ppermute | solution.py:584
  241.5 51.7 %collective-permute-start.20 = (bf16[352,2048]{1,0:T(8,128)(2,1)}, bf16[352,2048]{1,0:T(8,128)(2,1)}, u32[]{:S(2)}, u32[]{:S(2)}) collective-permute-start(bf16[352,2048]{1,0:T(8,128)(2,1)} %collective-permute-done.17.refs_0_), channel_id=1, source_target_pairs={{0,16},{16,0},{1,17},{17,1},{2,18},{18,2},{3,19},{19,3},{4,20},{20... | collective-permute-start | bytes 4325384 | tf_op jit(solution)/shard_map/ppermute | solution.py:587
  352.5 38.6 %collective-permute-start.26 = (bf16[352,2048]{1,0:T(8,128)(2,1)S(1)}, bf16[352,2048]{1,0:T(8,128)(2,1)S(1)}, u32[]{:S(2)}, u32[]{:S(2)}) collective-permute-start(bf16[352,2048]{1,0:T(8,128)(2,1)S(1)} %unit_grad.6), channel_id=1, source_target_pairs={{0,16},{16,0},{1,17},{17,1},{2,18},{18,2},{3,19},{19,3},{4,20},{20... | collective-permute-start | bytes 4325384 | tf_op jit(solution)/shard_map/ppermute | solution.py:587
  396.0 71.2 %collective-permute-start.27 = (bf16[1024,2048]{1,0:T(8,128)(2,1)}, bf16[1024,2048]{1,0:T(8,128)(2,1)S(1)}, u32[]{:S(2)}, u32[]{:S(2)}) collective-permute-start(bf16[1024,2048]{1,0:T(8,128)(2,1)} %copy-done.26), channel_id=1, source_target_pairs={{0,8},{8,0},{1,9},{9,1},{2,10},{10,2},{3,11},{11,3},{4,12},{12,4},... | collective-permute-start | bytes 12582920 | tf_op jit(solution)/shard_map/ppermute | solution.py:661
  398.3 64.4 %collective-permute-start.28 = (bf16[352,2048]{1,0:T(8,128)(2,1)}, bf16[352,2048]{1,0:T(8,128)(2,1)S(1)}, u32[]{:S(2)}, u32[]{:S(2)}) collective-permute-start(bf16[352,2048]{1,0:T(8,128)(2,1)} %unit_grad.8), channel_id=1, source_target_pairs={{0,16},{16,0},{1,17},{17,1},{2,18},{18,2},{3,19},{19,3},{4,20},{20... | collective-permute-start | bytes 4325384 | tf_op jit(solution)/shard_map/ppermute | solution.py:587
  411.2 89.0 %collective-permute-start.30 = (bf16[352,2048]{1,0:T(8,128)(2,1)S(1)}, bf16[352,2048]{1,0:T(8,128)(2,1)}, u32[]{:S(2)}, u32[]{:S(2)}) collective-permute-start(bf16[352,2048]{1,0:T(8,128)(2,1)S(1)} %unit_grad.9), channel_id=1, source_target_pairs={{4,0},{8,12},{5,1},{9,13},{6,2},{10,14},{7,3},{11,15},{20,16},{24,... | collective-permute-start | bytes 4325384 | tf_op jit(solution)/shard_map/ppermute | solution.py:590
  440.5 59.6 %collective-permute-start.31 = (bf16[352,2048]{1,0:T(8,128)(2,1)}, bf16[352,2048]{1,0:T(8,128)(2,1)}, u32[]{:S(2)}, u32[]{:S(2)}) collective-permute-start(bf16[352,2048]{1,0:T(8,128)(2,1)} %unit_grad.10), channel_id=1, source_target_pairs={{4,0},{8,12},{5,1},{9,13},{6,2},{10,14},{7,3},{11,15},{20,16},{24,... | collective-permute-start | bytes 4325384 | tf_op jit(solution)/shard_map/ppermute | solution.py:590
  516.4 38.5 %collective-permute-start.34 = (bf16[256,2048]{1,0:T(8,128)(2,1)S(1)}, bf16[256,2048]{1,0:T(8,128)(2,1)S(1)}, u32[]{:S(2)}, u32[]{:S(2)}) collective-permute-start(bf16[256,2048]{1,0:T(8,128)(2,1)S(1)} %pad_maximum_fusion.11), channel_id=1, source_target_pairs={{0,2},{2,0},{1,3},{3,1},{4,6},{6,4},{5,7},{7,5},{8,10},{10,8},{9,1... | collective-permute-start | bytes 3145736 | tf_op jit(solution)/shard_map/ppermute | solution.py:661
  516.5 38.4 %collective-permute-start.33 = (bf16[256,2048]{1,0:T(8,128)(2,1)S(1)}, bf16[256,2048]{1,0:T(8,128)(2,1)}, u32[]{:S(2)}, u32[]{:S(2)}) collective-permute-start(bf16[256,2048]{1,0:T(8,128)(2,1)S(1)} %pad_maximum_fusion.10), channel_id=1, source_target_pairs={{0,1},{1,0},{2,3},{3,2},{4,5},{5,4},{6,7},{7,6},{8,9},{9,8},{10,11... | collective-permute-start | bytes 3145736 | tf_op jit(solution)/shard_map/ppermute | solution.py:661
  526.5 51.9 %collective-permute-start.39 = (bf16[288,2048]{1,0:T(8,128)(2,1)S(1)}, bf16[288,2048]{1,0:T(8,128)(2,1)S(1)}, u32[]{:S(2)}, u32[]{:S(2)}) collective-permute-start(bf16[288,2048]{1,0:T(8,128)(2,1)S(1)} %get-tuple-element.205), channel_id=1, source_target_pairs={{0,16},{16,0},{1,17},{17,1},{2,18},{18,2},{3,19},{19,3},{4,20},{20... | collective-permute-start | bytes 3538952 | tf_op jit(solution)/shard_map/ppermute | solution.py:587
  532.2 51.1 %collective-permute-start.44 = (bf16[352,2048]{1,0:T(8,128)(2,1)S(1)}, bf16[352,2048]{1,0:T(8,128)(2,1)}, u32[]{:S(2)}, u32[]{:S(2)}) collective-permute-start(bf16[352,2048]{1,0:T(8,128)(2,1)S(1)} %add.358.mine_ref), channel_id=1, source_target_pairs={{0,16},{12,28},{16,0},{28,12},{1,17},{13,29},{17,1},{29,13},{2,18}... | collective-permute-start | bytes 4325384 | tf_op jit(solution)/shard_map/ppermute | solution.py:593
  537.7 49.8 %collective-permute-start.43 = (bf16[352,2048]{1,0:T(8,128)(2,1)S(1)}, bf16[352,2048]{1,0:T(8,128)(2,1)S(1)}, u32[]{:S(2)}, u32[]{:S(2)}) collective-permute-start(bf16[352,2048]{1,0:T(8,128)(2,1)S(1)} %add.358.mine_ref), channel_id=1, source_target_pairs={{0,8},{12,4},{1,9},{13,5},{2,10},{14,6},{3,11},{15,7},{16,24},{28,... | collective-permute-start | bytes 4325384 | tf_op jit(solution)/shard_map/ppermute | solution.py:596
  583.3 58.9 %collective-permute-start.45 = (bf16[352,2048]{1,0:T(8,128)(2,1)}, bf16[352,2048]{1,0:T(8,128)(2,1)}, u32[]{:S(2)}, u32[]{:S(2)}) collective-permute-start(bf16[352,2048]{1,0:T(8,128)(2,1)} %collective-permute-done.44.theirs_ref), channel_id=1, source_target_pairs={{0,8},{12,4},{1,9},{13,5},{2,10},{14,6},{3,11},{15,7},{16,24},{28,... | collective-permute-start | bytes 4325384 | tf_op jit(solution)/shard_map/ppermute | solution.py:596
  584.7 57.5 %collective-permute-start.48 = (bf16[352,2048]{1,0:T(8,128)(2,1)}, bf16[352,2048]{1,0:T(8,128)(2,1)}, u32[]{:S(2)}, u32[]{:S(2)}) collective-permute-start(bf16[352,2048]{1,0:T(8,128)(2,1)} %collective-permute-done.47.theirs_ref), channel_id=1, source_target_pairs={{0,8},{12,4},{1,9},{13,5},{2,10},{14,6},{3,11},{15,7},{16,24},{28,... | collective-permute-start | bytes 4325384 | tf_op jit(solution)/shard_map/ppermute | solution.py:596
  588.6 53.6 %collective-permute-start.40 = (bf16[288,2048]{1,0:T(8,128)(2,1)}, bf16[288,2048]{1,0:T(8,128)(2,1)}, u32[]{:S(2)}, u32[]{:S(2)}) collective-permute-start(bf16[288,2048]{1,0:T(8,128)(2,1)} %add_convert_fusion), channel_id=1, source_target_pairs={{4,0},{8,12},{5,1},{9,13},{6,2},{10,14},{7,3},{11,15},{20,16},{24,... | collective-permute-start | bytes 3538952 | tf_op jit(solution)/shard_map/ppermute | solution.py:590
  (113 other events, 1622.2 us)
Sparse Core Ops, SparseCore 0:
  102.0 50.0 all-gather.5
  236.7 61.9 all-gather.3
  396.1 70.2 all-gather.7
